TPU v7x, 32 devices: a whole 2x2x4 slice. The times are simulated.
32 devices in a mesh: batch: 2 (over y), row: 4 (over x, core), col: 4 (over z).
Axes of the slice: x: 2, y: 2, z: 4, core: 2. Of those that a mesh axis runs over, the one named last changes fastest.
Arguments:
- patches: bfloat16 [2, 4096, 1280], P('batch', 'col', 'row'), may hold values from -6 to 6
- qkv_weight: bfloat16 [1280, 3, 1280], P('row', None, 'col'), may hold values from -0.15625 to 0.15625
- qv_bias: float32 [2, 1280], P(None, 'col'), may hold values from -0.6 to 0.6
- proj_weight: bfloat16 [1280, 1280], P('col', 'row'), may hold values from -2.5 to 2.5
- proj_bias: float32 [1280], P('row'), may hold values from -1.2 to 1.2
- norm1_gain: float32 [1280], P('row'), may hold values from 0.5 to 1.5
- norm1_shift: float32 [1280], P('row'), may hold values from -1.2 to 1.2
- norm2_gain: float32 [1280], P('row'), may hold values from 0.5 to 1.5
- norm2_shift: float32 [1280], P('row'), may hold values from -1.2 to 1.2
- fc1_weight: bfloat16 [1280, 5120], P('row', 'col'), may hold values from -0.15625 to 0.15625
- fc1_bias: float32 [5120], P('col'), may hold values from -1.2 to 1.2
- fc2_weight: bfloat16 [5120, 1280], P('col', 'row'), may hold values from -0.078125 to 0.078125
- fc2_bias: float32 [1280], P('row'), may hold values from -1.2 to 1.2
- height_table: bfloat16 [127, 80], replicated, may hold values from -0.625 to 0.625
- width_table: bfloat16 [127, 80], replicated, may hold values from -0.625 to 0.625
- out_grad: bfloat16 [2, 4096, 1280], P('batch', 'col', 'row'), may hold values from -6 to 6
Outputs:
- block_out: bfloat16 [2, 4096, 1280], P('batch', 'col', 'row')
- patches_grad: float32 [2, 4096, 1280], P('batch', 'col', 'row')
- qkv_weight_grad: float32 [1280, 3, 1280], P('row', None, 'col')
- qv_bias_grad: float32 [2, 1280], P(None, 'col')
- proj_weight_grad: float32 [1280, 1280], P('col', 'row')
- proj_bias_grad: float32 [1280], P('row')
- norm1_gain_grad: float32 [1280], P('row')
- norm1_shift_grad: float32 [1280], P('row')
- norm2_gain_grad: float32 [1280], P('row')
- norm2_shift_grad: float32 [1280], P('row')
- fc1_weight_grad: float32 [1280, 5120], P('row', 'col')
- fc1_bias_grad: float32 [5120], P('col')
- fc2_weight_grad: float32 [5120, 1280], P('col', 'row')
- fc2_bias_grad: float32 [1280], P('row')
- height_table_grad: float32 [127, 80], replicated
- width_table_grad: float32 [127, 80], replicated
All inputs are finite; a program needn't handle non-finite values.
Results may differ from a plain program's by a relative error of at most 0.012.
Values may be sent and summed in bfloat16 or wider, within the bound.
A program may use at most 256 MiB of HBM per device.

v0:
```python
from functools import partial

import jax
import jax.numpy as jnp
from jax import lax
from jax.sharding import PartitionSpec as P

D = 1280
HEAD_DIM = 80
GRID = 64


EPSILON = 1e-06
HIGHEST = lax.Precision.HIGHEST


def feature_sums(first, second):
    return lax.psum((first, second), "row")


def rows_over_col(values):
    return lax.all_gather(values, "col", axis=0, tiled=True)


def rows_over_row(values):
    return lax.all_gather(values, "row", axis=0, tiled=True)


def sum_over_row(values):
    return lax.psum_scatter(values, "row", scatter_dimension=0, tiled=True)


def sum_over_col(values):
    return lax.psum_scatter(values, "col", scatter_dimension=0, tiled=True)


def gather_key_value(key_local, value_local):
    couple = jnp.stack([key_local, value_local], 1).astype(jnp.bfloat16)
    couple_full = lax.all_gather(couple, "row", axis=0, tiled=True)
    return (couple_full[:, 0], couple_full[:, 1])


def normalize(values, norm_gain, norm_shift, model_width):
    first, second = feature_sums(jnp.sum(values, -1), jnp.sum(values * values, -1))
    center = first / model_width
    inv_scale = lax.rsqrt(second / model_width - center * center + EPSILON)
    scaled = (values - center[:, None]) * inv_scale[:, None]
    return (scaled, inv_scale, (scaled * norm_gain + norm_shift).astype(jnp.bfloat16))


def normalize_back(grad_in, scaled, inv_scale, norm_gain, model_width):
    scaled_grad = grad_in * norm_gain
    first, second = feature_sums(jnp.sum(scaled_grad, -1), jnp.sum(scaled_grad * scaled, -1))
    return inv_scale[:, None] * (
        scaled_grad - first[:, None] / model_width - scaled * (second[:, None] / model_width)
    )


def select_table(row_count, col_count, offset, grid_side):
    shape = (row_count, col_count, 2 * grid_side - 1)
    first = lax.broadcasted_iota(jnp.int32, shape, 0) + offset
    second = lax.broadcasted_iota(jnp.int32, shape, 1)
    third = lax.broadcasted_iota(jnp.int32, shape, 2)
    return (first - second + grid_side - 1 == third).astype(jnp.bfloat16)


def head_scores(query_one, key_one, row_select, col_select, score_scale, grid_side):
    query_lines = query_one.shape[0] // grid_side
    query_grid = query_one.reshape(query_lines, grid_side, query_one.shape[1])
    rel_rows = jnp.einsum(
        "hwc,hkc->hwk", query_grid, row_select, preferred_element_type=jnp.float32
    )
    rel_cols = jnp.einsum(
        "hwc,wkc->hwk", query_grid, col_select, preferred_element_type=jnp.float32
    )
    position = (rel_rows[:, :, :, None] + rel_cols[:, :, None, :]).reshape(
        query_one.shape[0], grid_side * grid_side
    )
    raw = jnp.einsum("qc,kc->qk", query_one, key_one, preferred_element_type=jnp.float32)
    return raw * score_scale + position


def shards(
    patches,
    qkv_weight,
    qv_bias,
    proj_weight,
    proj_bias,
    norm1_gain,
    norm1_shift,
    norm2_gain,
    norm2_shift,
    fc1_weight,
    fc1_bias,
    fc2_weight,
    fc2_bias,
    height_table,
    width_table,
    out_grad,
):
    grid_side = GRID
    model_width = D
    head_size = HEAD_DIM
    score_scale = head_size ** (-0.5)
    local_cols = qkv_weight.shape[2]
    head_count = local_cols // head_size
    image_tokens = grid_side * grid_side
    query_rows = image_tokens // lax.axis_size("row")
    query_lines = query_rows // grid_side
    residual = patches[0].astype(jnp.float32)
    scaled1, inv_scale1, normed1 = normalize(residual, norm1_gain, norm1_shift, model_width)
    gathered1 = rows_over_col(normed1)
    partial_qkv = jnp.einsum(
        "lf,fkh->lkh", gathered1, qkv_weight, preferred_element_type=jnp.float32
    )
    local_qkv = sum_over_row(partial_qkv)
    queries = local_qkv[:, 0] + qv_bias[0]
    key_full, value_full = gather_key_value(local_qkv[:, 1], local_qkv[:, 2] + qv_bias[1])
    queries = queries.astype(jnp.bfloat16)
    row_onehot = select_table(
        query_lines, grid_side, lax.axis_index("row") * query_lines, grid_side
    )
    col_onehot = select_table(grid_side, grid_side, 0, grid_side)
    row_select = jnp.einsum(
        "ijd,dc->ijc", row_onehot, height_table, preferred_element_type=jnp.float32
    ).astype(jnp.bfloat16)
    col_select = jnp.einsum(
        "ijd,dc->ijc", col_onehot, width_table, preferred_element_type=jnp.float32
    ).astype(jnp.bfloat16)

    def split_heads(values):
        return values.reshape(values.shape[0], head_count, head_size).transpose(1, 0, 2)

    def join_heads(values):
        return values.transpose(1, 0, 2).reshape(values.shape[1], head_count * head_size)

    query_heads = split_heads(queries)
    key_heads = split_heads(key_full)
    value_heads = split_heads(value_full)

    def attend(operands):
        query_one, key_one, value_one = operands
        scores = head_scores(query_one, key_one, row_select, col_select, score_scale, grid_side)
        row_max = jnp.max(scores, -1, keepdims=True)
        raw_weights = jnp.exp(scores - row_max)
        row_total = jnp.sum(raw_weights, -1, keepdims=True)
        weights = (raw_weights / row_total).astype(jnp.bfloat16)
        result = jnp.dot(weights, value_one, preferred_element_type=jnp.float32).astype(
            jnp.bfloat16
        )
        return (result, (row_max + jnp.log(row_total))[:, 0])

    attended, log_total = lax.map(attend, (query_heads, key_heads, value_heads))
    merged = join_heads(attended)
    gathered_attn = rows_over_row(merged)
    projected = sum_over_col(
        jnp.dot(gathered_attn, proj_weight, preferred_element_type=jnp.float32)
    )
    middle = residual + (projected + proj_bias)
    scaled2, inv_scale2, normed2 = normalize(middle, norm2_gain, norm2_shift, model_width)
    gathered2 = rows_over_col(normed2)
    preact = (
        sum_over_row(jnp.dot(gathered2, fc1_weight, preferred_element_type=jnp.float32)) + fc1_bias
    )
    activated = jax.nn.gelu(preact, approximate=False).astype(jnp.bfloat16)
    gathered_act = rows_over_row(activated)
    lowered = sum_over_col(jnp.dot(gathered_act, fc2_weight, preferred_element_type=jnp.float32))
    final = middle + (lowered + fc2_bias)
    cotangent = out_grad[0]
    cot_all = rows_over_col(cotangent)
    fc2_grad, fc2_bias_grad = (
        jnp.einsum("lh,lf->hf", gathered_act, cot_all, preferred_element_type=jnp.float32),
        jnp.sum(cot_all, 0, dtype=jnp.float32),
    )
    act_grad = sum_over_row(
        jnp.einsum("lf,hf->lh", cot_all, fc2_weight, preferred_element_type=jnp.float32)
    )
    gelu_fn = partial(jax.nn.gelu, approximate=False)
    unused, gelu_back = jax.vjp(gelu_fn, preact)
    preact_grad = gelu_back(act_grad)[0].astype(jnp.bfloat16)
    preact_all = rows_over_row(preact_grad)
    fc1_grad, fc1_bias_grad = (
        jnp.einsum("lf,lh->fh", gathered2, preact_all, preferred_element_type=jnp.float32),
        jnp.sum(preact_all, 0, dtype=jnp.float32),
    )
    normed2_grad = sum_over_col(
        jnp.einsum("lh,fh->lf", preact_all, fc1_weight, preferred_element_type=jnp.float32)
    )
    gain2_part = jnp.sum(normed2_grad * scaled2, 0)
    shift2_part = jnp.sum(normed2_grad, 0)
    middle_grad = cotangent.astype(jnp.float32) + normalize_back(
        normed2_grad, scaled2, inv_scale2, norm2_gain, model_width
    )
    branch_grad = middle_grad.astype(jnp.bfloat16)
    branch_all = rows_over_col(branch_grad)
    proj_grad, proj_bias_grad = (
        jnp.einsum("lh,lf->hf", gathered_attn, branch_all, preferred_element_type=jnp.float32),
        jnp.sum(branch_all, 0, dtype=jnp.float32),
    )
    merged_grad = sum_over_row(
        jnp.einsum("lf,hf->lh", branch_all, proj_weight, preferred_element_type=jnp.float32)
    ).astype(jnp.bfloat16)
    merged_grad_heads = split_heads(merged_grad)

    def attend_back(operands):
        query_one, key_one, value_one, grad_one, total_one = operands
        scores = head_scores(query_one, key_one, row_select, col_select, score_scale, grid_side)
        weights = jnp.exp(scores - total_one[:, None])
        weight_grad = jnp.einsum(
            "qc,kc->qk", grad_one, value_one, preferred_element_type=jnp.float32
        )
        row_inner = jnp.sum(weights * weight_grad, -1, keepdims=True)
        score_grad = (weights * (weight_grad - row_inner)).astype(jnp.bfloat16)
        value_part = jnp.einsum(
            "qk,qc->kc", weights.astype(jnp.bfloat16), grad_one, preferred_element_type=jnp.float32
        )
        key_part = (
            jnp.einsum("qk,qc->kc", score_grad, query_one, preferred_element_type=jnp.float32)
            * score_scale
        )
        query_part = jnp.dot(score_grad, key_one, preferred_element_type=jnp.float32) * score_scale
        grid_form = score_grad.astype(jnp.float32).reshape(
            query_lines, grid_side, grid_side, grid_side
        )
        row_grad = jnp.sum(grid_form, 3)
        col_grad = jnp.sum(grid_form, 2)
        query_grid = query_one.astype(jnp.float32).reshape(query_lines, grid_side, head_size)
        from_rows = jnp.einsum(
            "hwk,hkc->hwc", row_grad, row_select.astype(jnp.float32), precision=HIGHEST
        )
        from_cols = jnp.einsum(
            "hwk,wkc->hwc", col_grad, col_select.astype(jnp.float32), precision=HIGHEST
        )
        query_part = query_part + (from_rows + from_cols).reshape(query_rows, head_size)
        row_select_grad = jnp.einsum("hwk,hwc->hkc", row_grad, query_grid, precision=HIGHEST)
        col_select_grad = jnp.einsum("hwk,hwc->wkc", col_grad, query_grid, precision=HIGHEST)
        return (query_part, key_part, value_part, row_select_grad, col_select_grad)

    query_parts, key_parts, value_parts, row_sel_grads, col_sel_grads = lax.map(
        attend_back, (query_heads, key_heads, value_heads, merged_grad_heads, log_total)
    )
    kv_grad = sum_over_row(jnp.stack([join_heads(key_parts), join_heads(value_parts)], 1)).astype(
        jnp.bfloat16
    )
    query_grad = join_heads(query_parts).astype(jnp.bfloat16)
    qkv_grad_local = jnp.concatenate([query_grad[:, None], kv_grad], 1)
    qkv_all = rows_over_row(qkv_grad_local)
    qkv_grad, qv_bias_grad = (
        jnp.einsum("lf,lkh->fkh", gathered1, qkv_all, preferred_element_type=jnp.float32),
        jnp.stack(
            [
                jnp.sum(qkv_all[:, 0], 0, dtype=jnp.float32),
                jnp.sum(qkv_all[:, 2], 0, dtype=jnp.float32),
            ],
            0,
        ),
    )
    normed1_grad = sum_over_col(
        jnp.einsum("lkh,fkh->lf", qkv_all, qkv_weight, preferred_element_type=jnp.float32)
    )
    gain1_part = jnp.sum(normed1_grad * scaled1, 0)
    shift1_part = jnp.sum(normed1_grad, 0)
    input_grad = middle_grad + normalize_back(
        normed1_grad, scaled1, inv_scale1, norm1_gain, model_width
    )
    height_part = jnp.einsum(
        "ijd,ijc->dc", row_onehot.astype(jnp.float32), jnp.sum(row_sel_grads, 0), precision=HIGHEST
    )
    width_part = jnp.einsum(
        "ijd,ijc->dc", col_onehot.astype(jnp.float32), jnp.sum(col_sel_grads, 0), precision=HIGHEST
    )
    gain1_grad, shift1_grad, gain2_grad, shift2_grad = lax.psum(
        (gain1_part, shift1_part, gain2_part, shift2_part), ("batch", "col")
    )
    height_grad, width_grad = lax.psum((height_part, width_part), ("batch", "row", "col"))
    (
        qkv_grad,
        qv_bias_grad,
        proj_grad,
        proj_bias_grad,
        fc1_grad,
        fc1_bias_grad,
        fc2_grad,
        fc2_bias_grad,
    ) = (
        lax.psum(qkv_grad.astype(jnp.bfloat16), "batch").astype(jnp.float32),
        lax.psum(qv_bias_grad.astype(jnp.bfloat16), "batch").astype(jnp.float32),
        lax.psum(proj_grad.astype(jnp.bfloat16), "batch").astype(jnp.float32),
        lax.psum(proj_bias_grad.astype(jnp.bfloat16), "batch").astype(jnp.float32),
        lax.psum(fc1_grad.astype(jnp.bfloat16), "batch").astype(jnp.float32),
        lax.psum(fc1_bias_grad.astype(jnp.bfloat16), "batch").astype(jnp.float32),
        lax.psum(fc2_grad.astype(jnp.bfloat16), "batch").astype(jnp.float32),
        lax.psum(fc2_bias_grad.astype(jnp.bfloat16), "batch").astype(jnp.float32),
    )
    return (
        final[None].astype(jnp.bfloat16),
        input_grad[None],
        qkv_grad,
        qv_bias_grad,
        proj_grad,
        proj_bias_grad,
        gain1_grad,
        shift1_grad,
        gain2_grad,
        shift2_grad,
        fc1_grad,
        fc1_bias_grad,
        fc2_grad,
        fc2_bias_grad,
        height_grad,
        width_grad,
    )


def solution(mesh):
    in_specs = (
        P("batch", "col", "row"),
        P("row", None, "col"),
        P(None, "col"),
        P("col", "row"),
        P("row"),
        P("row"),
        P("row"),
        P("row"),
        P("row"),
        P("row", "col"),
        P("col"),
        P("col", "row"),
        P("row"),
        P(),
        P(),
        P("batch", "col", "row"),
    )
    out_specs = (
        P("batch", "col", "row"),
        P("batch", "col", "row"),
        P("row", None, "col"),
        P(None, "col"),
        P("col", "row"),
        P("row"),
        P("row"),
        P("row"),
        P("row"),
        P("row"),
        P("row", "col"),
        P("col"),
        P("col", "row"),
        P("row"),
        P(),
        P(),
    )
    return jax.shard_map(shards, mesh=mesh, in_specs=in_specs, out_specs=out_specs, check_vma=False)
```

profile of v0, /device:TPU:8, one launch (start us, length us, event | category | flops | bytes accessed | tf_op | source)
XLA Modules:
  0.0 2642.5 jit_solution(13296211281150519857)
XLA Ops:
  19.7 53.3 %all-gather.11.cloned.1.call-done = bf16[4096,320]{0,1:T(8,128)(2,1)} async-done(((bf16[1024,320]{0,1:T(8,128)(2,1)}), bf16[4096,320]{0,1:T(8,128)(2,1)}) %all-gather.11.cloned.1.call-update) | async-done | bytes 2621456 | tf_op jit(solution)/shard_map/all_gather | solution.py:22
  85.4 119.9 %reduce-scatter.10.cloned.1.call-done = f32[1024,3,320]{0,2,1:T(8,128)} async-done(((f32[4096,3,320]{0,2,1:T(8,128)}), f32[1024,3,320]{0,2,1:T(8,128)}) %reduce-scatter.10.cloned.1.call-update) | async-done | bytes 3932176 | tf_op jit(solution)/shard_map/reduce_scatter | solution.py:30
  217.9 33.7 %all-gather.13.cloned.1.call-done = bf16[4096,2,320]{0,2,1:T(8,128)(2,1)} async-done(((bf16[1024,2,320]{0,2,1:T(8,128)(2,1)}), bf16[4096,2,320]{0,2,1:T(8,128)(2,1)}) %all-gather.13.cloned.1.call-update) | async-done | bytes 5242896 | tf_op jit(solution)/shard_map/all_gather | solution.py:39
  268.2 293.5 %while.30 = (s32[]{:T(128)}, bf16[4,1024,80]{1,2,0:T(8,128)(2,1)S(1)}, f32[4,1024]{1,0:T(4,128)}, bf16[4,1024,80]{2,1,0:T(8,128)(2,1)}, bf16[4,4096,80]{2,1,0:T(...) while((s32[]{:T(128)}, ...), condition=%wide.region_8.9_spmd, body=%wide.region_5.8_spmd.sunk | while | flops 1400978432 | bytes 123054200 | solution.py:153
  281.7 27.9 %add.329 = f32[1024,4096]{1,0:T(8,128)} reshape(f32[16,64,64,64]{3,2,1,0:T(8,128)} %broadcast_add_fusion.4) | data formatting | bytes 33554432 | tf_op jit(solution)/shard_map/while/body/eval_jaxpr/add | solution.py:76
  355.1 27.9 %add.329 = f32[1024,4096]{1,0:T(8,128)} reshape(f32[16,64,64,64]{3,2,1,0:T(8,128)} %broadcast_add_fusion.4) | data formatting | bytes 33554432 | tf_op jit(solution)/shard_map/while/body/eval_jaxpr/add | solution.py:76
  428.4 27.9 %add.329 = f32[1024,4096]{1,0:T(8,128)} reshape(f32[16,64,64,64]{3,2,1,0:T(8,128)} %broadcast_add_fusion.4) | data formatting | bytes 33554432 | tf_op jit(solution)/shard_map/while/body/eval_jaxpr/add | solution.py:76
  501.8 27.9 %add.329 = f32[1024,4096]{1,0:T(8,128)} reshape(f32[16,64,64,64]{3,2,1,0:T(8,128)} %broadcast_add_fusion.4) | data formatting | bytes 33554432 | tf_op jit(solution)/shard_map/while/body/eval_jaxpr/add | solution.py:76
  563.0 25.3 all-gather.15.cloned.1.call-done
  594.5 93.3 %reduce-scatter.12.cloned.1.call-done = f32[1024,320]{0,1:T(8,128)} async-done(((f32[4096,320]{0,1:T(8,128)}), f32[1024,320]{0,1:T(8,128)}) %reduce-scatter.12.cloned.1.call-update) | async-done | bytes 1310736 | tf_op jit(solution)/shard_map/reduce_scatter | solution.py:34
  700.1 42.7 %all-gather.27.cloned.1.call-done = bf16[1,4096,320]{1,2,0:T(8,128)(2,1)} async-done(((bf16[1,1024,320]{1,2,0:T(8,128)(2,1)}), bf16[1,4096,320]{1,2,0:T(8,128)(2,1)}) %all-gather.27.cloned.1.call-update) | async-done | bytes 2621456 | tf_op jit(solution)/shard_map/all_gather | solution.py:22
  754.6 43.9 %all-gather.17.cloned.1.call-done = bf16[4096,320]{0,1:T(8,128)(2,1)} async-done(((bf16[1024,320]{0,1:T(8,128)(2,1)}), bf16[4096,320]{0,1:T(8,128)(2,1)}) %all-gather.17.cloned.1.call-update) | async-done | bytes 2621456 | tf_op jit(solution)/shard_map/all_gather | solution.py:22
  812.8 142.1 %reduce-scatter.18.cloned.1.call-done = f32[1024,1280]{1,0:T(8,128)} async-done(((f32[4096,1280]{1,0:T(8,128)}), f32[1024,1280]{1,0:T(8,128)}) %reduce-scatter.18.cloned.1.call-update) | async-done | bytes 5242896 | tf_op jit(solution)/shard_map/reduce_scatter | solution.py:30
  954.9 155.9 %reduce-scatter.14.cloned.1.call-done = f32[1024,1280]{1,0:T(8,128)} async-done(((f32[4096,1280]{1,0:T(8,128)}), f32[1024,1280]{1,0:T(8,128)}) %reduce-scatter.14.cloned.1.call-update) | async-done | bytes 5242896 | tf_op jit(solution)/shard_map/reduce_scatter | solution.py:30
  1126.2 70.3 %all-gather.21.cloned.1.call-done = bf16[4096,1280]{1,0:T(8,128)(2,1)} async-done(((bf16[1024,1280]{1,0:T(8,128)(2,1)}), bf16[4096,1280]{1,0:T(8,128)(2,1)}) %all-gather.21.cloned.1.call-update) | async-done | bytes 10485776 | tf_op jit(solution)/shard_map/all_gather | solution.py:26
  1209.2 93.9 %reduce-scatter.20.cloned.1.call-done = f32[1024,320]{0,1:T(8,128)} async-done(((f32[4096,320]{0,1:T(8,128)}), f32[1024,320]{0,1:T(8,128)}) %reduce-scatter.20.cloned.1.call-update) | async-done | bytes 1310736 | tf_op jit(solution)/shard_map/reduce_scatter | solution.py:34
  1316.0 52.7 %all-gather.23.cloned.1.call-done = bf16[4096,320]{0,1:T(8,128)(2,1)} async-done(((bf16[1024,320]{0,1:T(8,128)(2,1)}), bf16[4096,320]{0,1:T(8,128)(2,1)}) %all-gather.23.cloned.1.call-update) | async-done | bytes 2621456 | tf_op jit(solution)/shard_map/all_gather | solution.py:22
  1374.4 52.1 %reduce-scatter.22.cloned.1.call-done = f32[1024,320]{0,1:T(8,128)} async-done(((f32[4096,320]{0,1:T(8,128)}), f32[1024,320]{0,1:T(8,128)}) %reduce-scatter.22.cloned.1.call-update) | async-done | bytes 1310736 | tf_op jit(solution)/shard_map/reduce_scatter | solution.py:30
  1429.1 574.6 %while.31 = (s32[]{:T(128)}, bf16[4,1024,80]{1,2,0:T(8,128)(2,1)}, f32[4,4096,80]{1,2,0:T(8,128)}, f32[4,4096,80]{1,2,0:T(8,128)}, f32[4,16,64,80]{3,2,1,0:T(8,1...) while((s32[]{:T(128)}, bf16[4,1024,80]{1,2,0:T(8,128)(2,1)}, ...), condition=%wide.region_27.28_spmd, body=%wide.region_23.27_spmd.sunk | while | flops 3678845952 | bytes 353068224 | solution.py:239
  1452.8 27.9 %add.336 = f32[1024,4096]{1,0:T(8,128)} reshape(f32[16,64,64,64]{3,2,1,0:T(8,128)} %broadcast_add_fusion.5) | data formatting | bytes 33554432 | tf_op jit(solution)/shard_map/while/body/eval_jaxpr/add | solution.py:76
  1520.0 24.0 reshape.157
  1596.4 27.9 %add.336 = f32[1024,4096]{1,0:T(8,128)} reshape(f32[16,64,64,64]{3,2,1,0:T(8,128)} %broadcast_add_fusion.5) | data formatting | bytes 33554432 | tf_op jit(solution)/shard_map/while/body/eval_jaxpr/add | solution.py:76
  1663.6 24.0 reshape.157
  1739.9 27.9 %add.336 = f32[1024,4096]{1,0:T(8,128)} reshape(f32[16,64,64,64]{3,2,1,0:T(8,128)} %broadcast_add_fusion.5) | data formatting | bytes 33554432 | tf_op jit(solution)/shard_map/while/body/eval_jaxpr/add | solution.py:76
  1883.3 27.9 %add.336 = f32[1024,4096]{1,0:T(8,128)} reshape(f32[16,64,64,64]{3,2,1,0:T(8,128)} %broadcast_add_fusion.5) | data formatting | bytes 33554432 | tf_op jit(solution)/shard_map/while/body/eval_jaxpr/add | solution.py:76
  2019.9 78.4 %reduce-scatter.24.cloned.1.call-done = f32[1024,2,320]{0,2,1:T(8,128)} async-done(((f32[4096,2,320]{0,2,1:T(8,128)}), f32[1024,2,320]{0,2,1:T(8,128)}) %reduce-scatter.24.cloned.1.call-update) | async-done | bytes 2621456 | tf_op jit(solution)/shard_map/reduce_scatter | solution.py:30
  2111.5 58.5 %all-gather.19.cloned.1.call-done = bf16[4096,1280]{1,0:T(8,128)(2,1)} async-done(((bf16[1024,1280]{1,0:T(8,128)(2,1)}), bf16[4096,1280]{1,0:T(8,128)(2,1)}) %all-gather.19.cloned.1.call-update) | async-done | bytes 10485776 | tf_op jit(solution)/shard_map/all_gather | solution.py:26
  2179.6 47.3 %all-gather.25.cloned.1.call-done = bf16[4096,3,320]{0,2,1:T(8,128)(2,1)} async-done(((bf16[1024,3,320]{0,2,1:T(8,128)(2,1)}), bf16[4096,3,320]{0,2,1:T(8,128)(2,1)}) %all-gather.25.cloned.1.call-update) | async-done | bytes 7864336 | tf_op jit(solution)/shard_map/all_gather | solution.py:26
  2285.6 25.0 all-reduce.13.cloned.1.call-done
  2318.5 88.2 %reduce-scatter.26.cloned.1.call-done = f32[1024,320]{0,1:T(8,128)} async-done(((f32[4096,320]{0,1:T(8,128)}), f32[1024,320]{0,1:T(8,128)}) %reduce-scatter.26.cloned.1.call-update) | async-done | bytes 1310736 | tf_op jit(solution)/shard_map/reduce_scatter | solution.py:34
  2415.5 87.7 %reduce-scatter.16.cloned.1.call-done = f32[1024,320]{0,1:T(8,128)} async-done(((f32[4096,320]{0,1:T(8,128)}), f32[1024,320]{0,1:T(8,128)}) %reduce-scatter.16.cloned.1.call-update) | async-done | bytes 1310736 | tf_op jit(solution)/shard_map/reduce_scatter | solution.py:34
  2526.7 106.0 %all-reduce.11.cloned.1.call-done = (f32[127,80]{0,1:T(8,128)}, f32[127,80]{0,1:T(8,128)}) async-done(((f32[127,80]{0,1:T(8,128)}, f32[127,80]{0,1:T(8,128)}), (f32[127,80]{0,1:T(8,128)}, f32[127,80]{0,1:T(8,128)})) %all-reduce.11.cloned.1.call-update) | async-done | bytes 81296 | tf_op jit(solution)/shard_map/psum | solution.py:275
  (338 shorter events, 885.2 us)
Async XLA Ops:
  7.2 791.3 %copy-start = (bf16[320,1280]{1,0:T(8,128)(2,1)S(1)}, bf16[320,1280]{1,0:T(8,128)(2,1)}, u32[]{:S(2)}) copy-start(bf16[320,1280]{1,0:T(8,128)(2,1)} %param.29) | copy-start | bytes 2457604
  7.2 65.8 %all-gather.11.cloned.1.call-start = ((), (), s32[]{:S(2)}) async-start(), calls=%async_computation.9 | async-start | bytes 3276800 | tf_op jit(solution)/shard_map/all_gather | solution.py:22
  19.7 185.7 %reduce-scatter.10.cloned.1.call-start = ((), (), s32[]{:S(2)}) async-start(), calls=%async_computation.10 | async-start | bytes 19660800 | tf_op jit(solution)/shard_map/reduce_scatter | solution.py:30
  84.7 166.8 %all-gather.13.cloned.1.call-start = ((), (), s32[]{:S(2)}) async-start(), calls=%async_computation.11 | async-start | bytes 6553600 | tf_op jit(solution)/shard_map/all_gather | solution.py:39
  211.0 377.3 %all-gather.15.cloned.1.call-start = ((), (), s32[]{:S(2)}) async-start(), calls=%async_computation.12 | async-start | bytes 3276800 | tf_op jit(solution)/shard_map/all_gather | solution.py:26
  268.2 320.1 %copy-start.13 = (bf16[320,320]{1,0:T(8,128)(2,1)S(1)}, bf16[320,320]{1,0:T(8,128)(2,1)}, u32[]{:S(2)}) copy-start(bf16[320,320]{1,0:T(8,128)(2,1)} %param.23) | copy-start | bytes 614404
  562.5 125.3 %reduce-scatter.12.cloned.1.call-start = ((), (), s32[]{:S(2)}) async-start(), calls=%async_computation.13 | async-start | bytes 6553600 | tf_op jit(solution)/shard_map/reduce_scatter | solution.py:34
  593.9 148.9 %all-gather.27.cloned.1.call-start = ((), (), s32[]{:S(2)}) async-start(), calls=%async_computation.26 | async-start | bytes 3276800 | tf_op jit(solution)/shard_map/all_gather | solution.py:22
  594.5 204.0 %all-gather.17.cloned.1.call-start = ((), (), s32[]{:S(2)}) async-start(), calls=%async_computation.14 | async-start | bytes 3276800 | tf_op jit(solution)/shard_map/all_gather | solution.py:22
  697.5 615.4 %copy-start.19 = (f32[1024]{0:T(1024)}, f32[1024]{0:T(1024)S(1)}, u32[]{:S(2)}) copy-start(f32[1024]{0:T(1024)S(1)} %get-tuple-element.230) | copy-start | bytes 12292
  697.5 615.4 %copy-start.21 = (f32[1024]{0:T(1024)}, f32[1024]{0:T(1024)S(1)}, u32[]{:S(2)}) copy-start(f32[1024]{0:T(1024)S(1)} %get-tuple-element.231) | copy-start | bytes 12292
  700.0 254.9 %reduce-scatter.18.cloned.1.call-start = ((), (), s32[]{:S(2)}) async-start(), calls=%async_computation.18 | async-start | bytes 26214400 | tf_op jit(solution)/shard_map/reduce_scatter | solution.py:30
  754.5 356.3 %reduce-scatter.14.cloned.1.call-start = ((), (), s32[]{:S(2)}) async-start(), calls=%async_computation.15 | async-start | bytes 26214400 | tf_op jit(solution)/shard_map/reduce_scatter | solution.py:30
  812.7 298.1 %copy-start.33 = (f32[1280]{0:T(1024)S(1)}, f32[1280]{0:T(1024)}, u32[]{:S(2)}) copy-start(f32[1280]{0:T(1024)} %param.30) | copy-start | bytes 15364
  812.7 383.8 %all-gather.21.cloned.1.call-start = ((), (), s32[]{:S(2)}) async-start(), calls=%async_computation.19 | async-start | bytes 13107200 | tf_op jit(solution)/shard_map/all_gather | solution.py:26
  1126.1 176.9 %reduce-scatter.20.cloned.1.call-start = ((), (), s32[]{:S(2)}) async-start(), calls=%async_computation.20 | async-start | bytes 6553600 | tf_op jit(solution)/shard_map/reduce_scatter | solution.py:34
  1209.1 159.5 %all-gather.23.cloned.1.call-start = ((), (), s32[]{:S(2)}) async-start(), calls=%async_computation.21 | async-start | bytes 3276800 | tf_op jit(solution)/shard_map/all_gather | solution.py:22
  1315.9 110.5 %reduce-scatter.22.cloned.1.call-start = ((), (), s32[]{:S(2)}) async-start(), calls=%async_computation.22 | async-start | bytes 6553600 | tf_op jit(solution)/shard_map/reduce_scatter | solution.py:30
  1374.3 724.1 %reduce-scatter.24.cloned.1.call-start = ((), (), s32[]{:S(2)}) async-start(), calls=%async_computation.23 | async-start | bytes 13107200 | tf_op jit(solution)/shard_map/reduce_scatter | solution.py:30
  2012.9 157.2 %all-gather.19.cloned.1.call-start = ((), (), s32[]{:S(2)}) async-start(), calls=%async_computation.16 | async-start | bytes 13107200 | tf_op jit(solution)/shard_map/all_gather | solution.py:26
  2019.9 207.0 %all-gather.25.cloned.1.call-start = ((), (), s32[]{:S(2)}) async-start(), calls=%async_computation.24 | async-start | bytes 9830400 | tf_op jit(solution)/shard_map/all_gather | solution.py:26
  2101.8 208.8 %all-reduce.13.cloned.1.call-start = ((), (), s32[]{:S(2)}) async-start(), calls=%async_computation.28 | async-start | bytes 5242880 | tf_op jit(solution)/shard_map/psum | solution.py:286
  2235.4 171.2 %reduce-scatter.26.cloned.1.call-start = ((), (), s32[]{:S(2)}) async-start(), calls=%async_computation.25 | async-start | bytes 6553600 | tf_op jit(solution)/shard_map/reduce_scatter | solution.py:34
  2243.4 259.8 %reduce-scatter.16.cloned.1.call-start = ((), (), s32[]{:S(2)}) async-start(), calls=%async_computation.17 | async-start | bytes 6553600 | tf_op jit(solution)/shard_map/reduce_scatter | solution.py:34
  2257.3 375.4 %all-reduce.11.cloned.1.call-start = ((), (), s32[]{:S(2)}) async-start(), calls=%async_computation.27 | async-start | bytes 163840 | tf_op jit(solution)/shard_map/psum | solution.py:275
  2277.9 225.3 %copy-start.4 = (f32[1024,320]{0,1:T(8,128)S(1)}, f32[1024,320]{0,1:T(8,128)}, u32[]{:S(2)}) copy-start(f32[1024,320]{0,1:T(8,128)} %get-tuple-element.219) | copy-start | bytes 3932164
  2277.9 225.3 %copy-start.11 = (bf16[1,1024,320]{1,2,0:T(8,128)(2,1)S(1)}, bf16[1,1024,320]{1,2,0:T(8,128)(2,1)}, u32[]{:S(2)}) copy-start(bf16[1,1024,320]{1,2,0:T(8,128)(2,1)} %param.35) | copy-start | bytes 1966084
  2277.9 225.3 %copy-start.20 = (f32[1024]{0:T(1024)S(1)}, f32[1024]{0:T(1024)}, u32[]{:S(2)}) copy-start(f32[1024]{0:T(1024)} %copy-done.19) | copy-start | bytes 12292
  2277.9 225.3 %copy-start.22 = (f32[1024]{0:T(1024)S(1)}, f32[1024]{0:T(1024)}, u32[]{:S(2)}) copy-start(f32[1024]{0:T(1024)} %copy-done.21) | copy-start | bytes 12292
  2277.9 225.3 %copy-start.28 = (f32[1024]{0:T(1024)S(1)}, f32[1024]{0:T(1024)}, u32[]{:S(2)}) copy-start(f32[1024]{0:T(1024)} %copy-done.27) | copy-start | bytes 12292
  2277.9 225.3 %copy-start.30 = (f32[1024]{0:T(1024)S(1)}, f32[1024]{0:T(1024)}, u32[]{:S(2)}) copy-start(f32[1024]{0:T(1024)} %copy-done.29) | copy-start | bytes 12292
  2317.2 318.3 %copy-start.1 = (bf16[320,1280]{1,0:T(8,128)(2,1)S(1)}, bf16[320,1280]{1,0:T(8,128)(2,1)}, u32[]{:S(2)}) copy-start(bf16[320,1280]{1,0:T(8,128)(2,1)} %param.29) | copy-start | bytes 2457604
  (40 other events, 2584.5 us)
Sparse Core Ops, SparseCore 0:
  19.8 53.1 all-gather.10
  84.8 120.4 reduce-scatter.9
  211.1 40.4 all-gather.12
  562.7 25.5 all-gather.14
  594.0 93.7 reduce-scatter.11
  689.2 53.4 all-gather.26
  744.9 53.5 all-gather.16
  801.1 153.7 reduce-scatter.17
  957.7 153.1 reduce-scatter.13
  1126.3 70.1 all-gather.20
  1209.2 93.7 reduce-scatter.19
  1316.0 52.5 all-gather.22
  1374.4 51.9 reduce-scatter.21
  2013.0 85.3 reduce-scatter.23
  2099.8 70.1 all-gather.18
  2171.6 55.3 all-gather.24
  2235.5 75.0 all-reduce.12
  2312.8 93.8 reduce-scatter.25
  2408.9 94.2 reduce-scatter.15
  2509.3 123.3 all-reduce.10
where the time goes:
time: 2660 us; the launch traced here: 2640 us
  waiting for transfers between devices  1470 us (55%)
  matrix products  398 us (15%)
  local copies, waits for them, and re-layouts  380 us (14%)
  other arithmetic  324 us (12%)
  blocking collectives  52.3 us (2%)
    reduce_scatter x5, waiting for transfers between devices, sum_over_row(): return lax.psum_scatter(values, 'row', scatter_dimension=0, tiled=True)  548 us
    reduce_scatter x4, waiting for transfers between devices, sum_over_col(): return lax.psum_scatter(values, 'col', scatter_dimension=0, tiled=True)  363 us
    add x8, local copies, waits for them, and re-layouts, head_scores(): rel_rows[:, :, :, None] + rel_cols[:, :, None, :]  223 us
    all_gather x4, waiting for transfers between devices, rows_over_row(): return lax.all_gather(values, 'row', axis=0, tiled=True)  201 us
    all_gather x4, waiting for transfers between devices, rows_over_col(): return lax.all_gather(values, 'col', axis=0, tiled=True)  193 us
    dot_general x8, matrix products, head_scores(): jnp.einsum('qc,kc->qk', query_one, key_one, preferred_element_type=jnp.fl...  124 us
    psum x1, waiting for transfers between devices, shards(): lax.psum((height_part, width_part), ('batch', 'row', 'col'))  106 us
    reshape x4, local copies, waits for them, and re-layouts, attend_back(): score_grad.astype(jnp.float32)  96.1 us
  transfers between devices with their start and end apart: 20, of which 20 were waited for; matrix products, arithmetic and copies ran while one was open for 5% of the time, Pallas kernels for 0%

commit v1 on v0

v1 whole, which is shorter than its diff:
```python
import math
from functools import partial

import jax
import jax.numpy as jnp
from jax import lax
from jax.experimental import pallas as pl
from jax.experimental.pallas import tpu as pltpu
from jax.sharding import PartitionSpec as P

D = 1280
HEAD_DIM = 80
GRID = 64
EPSILON = 1e-06

LINES = 4
QUERIES = LINES * GRID
KEYS = 512
LOG2E = math.log2(math.e)
SCALE = HEAD_DIM**-0.5
BF16 = jnp.bfloat16
F32 = jnp.float32


def mm(left, right):
    return jnp.dot(left, right, preferred_element_type=F32)


def mm_nt(left, right):
    return lax.dot_general(left, right, (((1,), (1,)), ((), ())), preferred_element_type=F32)


def split(values, parts):
    terms = []
    for _ in range(parts):
        term = values.astype(BF16)
        terms.append(term)
        values = values - term.astype(F32)
    return terms


def skew(values, shift):
    n = values.shape[1]
    for bit, rows in ((32, 96), (16, 80), (8, 72)):
        take = jnp.broadcast_to(shift, (rows, n)) & bit
        values = jnp.where(take != 0, values[bit : bit + rows], values[:rows])
    for bit in (4, 2, 1):
        take = jnp.broadcast_to(shift, values.shape) & bit
        values = jnp.where(take != 0, pltpu.roll(values, values.shape[0] - bit, 0), values)
    return values[:GRID]


def unskew(values, shift):
    n = values.shape[1]
    values = jnp.concatenate([values, jnp.zeros((8, n), F32)], 0)
    for bit in (1, 2, 4):
        take = jnp.broadcast_to(shift, values.shape) & bit
        values = jnp.where(take != 0, pltpu.roll(values, bit, 0), values)
    for bit in (8, 16, 32):
        zeros = jnp.zeros((bit, n), F32)
        take = jnp.broadcast_to(shift, (values.shape[0] + bit, n)) & bit
        values = jnp.where(
            take != 0,
            jnp.concatenate([zeros, values], 0),
            jnp.concatenate([values, zeros], 0),
        )
    return values


def token_shifts(step):
    lane = lax.broadcasted_iota(jnp.int32, (1, QUERIES), 1)
    return (GRID - 1) - (step * LINES + lane // GRID), (GRID - 1) - lane % GRID


def fill_keys(k_ref, kaug):
    count, _, width = k_ref.shape
    token = lax.broadcasted_iota(jnp.int32, (width, 2 * GRID), 0)
    lane = lax.broadcasted_iota(jnp.int32, (width, 2 * GRID), 1)
    pad_row = lax.broadcasted_iota(jnp.int32, (128 - HEAD_DIM, width), 0)
    pad = jnp.where(pad_row < 3, 1.0, 0.0)
    for part in range(count):
        at = token + part * width
        place = jnp.where(lane < GRID, at // GRID, at % GRID + GRID)
        hot = jnp.where(place == lane, 1.0, 0.0)
        kaug[part * width : (part + 1) * width, 0:128] = hot.astype(BF16)
        key = jnp.concatenate([k_ref[part].astype(F32), pad], 0)
        kaug[part * width : (part + 1) * width, 128:256] = key.T.astype(BF16)


def query_columns(q, tab, step, tail):
    shift_rows, shift_cols = token_shifts(step)
    both = mm(tab, q)
    rel_rows = skew(both[: 2 * GRID], shift_rows)
    rel_cols = skew(both[2 * GRID :], shift_cols)
    rel = jnp.concatenate([rel_rows, rel_cols], 0) * (1.0 / SCALE)
    return jnp.concatenate([rel.astype(BF16), q, tail], 0)


def attend_kernel(q_ref, k_ref, v_ref, tab_ref, merged_ref, exact_ref, stat_ref, kaug):
    step = pl.program_id(0)

    @pl.when(step == 0)
    def _():
        fill_keys(k_ref, kaug)

    width = k_ref.shape[2]
    q = q_ref[0]
    columns = query_columns(q, tab_ref[...], step, jnp.zeros((128 - HEAD_DIM, QUERIES), BF16))
    top = total = acc = None
    for chunk in range(kaug.shape[0] // KEYS):
        start = chunk * KEYS
        scores = mm(kaug[start : start + KEYS, :], columns)
        chunk_top = jnp.max(scores, 0, keepdims=True)
        new_top = chunk_top if top is None else jnp.maximum(top, chunk_top)
        weights = jnp.exp2((scores - new_top) * (SCALE * LOG2E))
        chunk_total = jnp.sum(weights, 0, keepdims=True)
        v = v_ref[start // width, :, start % width : start % width + KEYS]
        result = mm(v, weights.astype(BF16))
        if top is None:
            total, acc = chunk_total, result
        else:
            keep = jnp.exp2((top - new_top) * (SCALE * LOG2E))
            total, acc = total * keep + chunk_total, acc * keep + result
        top = new_top
    exact = acc * (1.0 / total)
    exact_ref[0] = exact
    merged_ref[0] = exact.astype(BF16)
    stat_ref[0] = jnp.broadcast_to(top + jnp.log2(total) * (1.0 / (SCALE * LOG2E)), (8, QUERIES))


def attend_back_kernel(
    q_ref, k_ref, v_ref, tab_ref, tab_t_ref, grad_ref, exact_ref, stat_ref,
    out_ref, tab_grad_ref, kaug, kaug_t, vaug, key_sum, value_sum,
):
    step = pl.program_id(0)
    count, _, width = k_ref.shape
    tail_row = lax.broadcasted_iota(jnp.int32, (128 - HEAD_DIM, width), 0)

    @pl.when(step == 0)
    def _():
        fill_keys(k_ref, kaug)
        pad = jnp.where(tail_row < 3, 1.0, 0.0)
        for part in range(count):
            rows = slice(part * width, (part + 1) * width)
            value = jnp.concatenate([v_ref[part].astype(F32), pad], 0)
            vaug[rows, :] = value.T.astype(BF16)
            kaug_t[0:128, rows] = kaug[rows, 0:128].astype(F32).T.astype(BF16)
            kaug_t[128:208, rows] = k_ref[part]
            kaug_t[208:256, rows] = jnp.zeros((48, width), BF16)
        key_sum[...] = jnp.zeros_like(key_sum)
        value_sum[...] = jnp.zeros_like(value_sum)
        tab_grad_ref[...] = jnp.zeros_like(tab_grad_ref)

    q = q_ref[0]
    grad = grad_ref[0]
    tail_row = lax.broadcasted_iota(jnp.int32, (128 - HEAD_DIM, QUERIES), 0)

    def tail(row):
        out = jnp.zeros((128 - HEAD_DIM, QUERIES), F32)
        for place, term in enumerate(split(row, 3)):
            out = jnp.where(tail_row == place, term.astype(F32), out)
        return out.astype(BF16)

    inner = jnp.sum(grad.astype(F32) * exact_ref[0], 0, keepdims=True)
    columns = query_columns(q, tab_ref[...], step, tail(-stat_ref[0, 0:1]))
    grad_columns = jnp.concatenate([grad, tail(-inner)], 0)
    zero_tail = jnp.zeros((128 - HEAD_DIM, QUERIES), F32)
    grad_rows = jnp.concatenate([grad.astype(F32), zero_tail], 0).T.astype(BF16)
    q_rows = jnp.concatenate([q.astype(F32), zero_tail], 0).T.astype(BF16)
    spread = None
    for chunk in range(kaug.shape[0] // KEYS):
        keys = slice(chunk * KEYS, (chunk + 1) * KEYS)
        weights = jnp.exp2(mm(kaug[keys, :], columns) * (SCALE * LOG2E))
        score_grad = (weights * mm(vaug[keys, :], grad_columns)).astype(BF16)
        value_sum[keys, :] += mm(weights.astype(BF16), grad_rows)
        key_sum[keys, :] += mm(score_grad, q_rows)
        result = mm(kaug_t[:, keys], score_grad)
        spread = result if spread is None else spread + result

    shift_rows, shift_cols = token_shifts(step)
    lifted = jnp.concatenate(
        [unskew(spread[:GRID], shift_rows), unskew(spread[GRID : 2 * GRID], shift_cols)], 0
    )
    high, low = split(lifted, 2)
    query_grad = spread[128 : 128 + HEAD_DIM] * SCALE
    query_grad = query_grad + (mm(tab_t_ref[...], high) + mm(tab_t_ref[...], low))
    tab_grad_ref[...] += mm_nt(high, q) + mm_nt(low, q)
    per_part = width // QUERIES
    lanes = pl.ds(pl.multiple_of((step % per_part) * QUERIES, QUERIES), QUERIES)
    out_ref[step // per_part, 0:HEAD_DIM, lanes] = query_grad.astype(BF16)

    @pl.when(step == pl.num_programs(0) - 1)
    def _():
        for part in range(count):
            rows = slice(part * width, (part + 1) * width)
            key_grad = (key_sum[rows, :] * SCALE).T[:HEAD_DIM]
            out_ref[part, HEAD_DIM : 2 * HEAD_DIM, :] = key_grad.astype(BF16)
            value_grad = value_sum[rows, :].T[:HEAD_DIM]
            out_ref[part, 2 * HEAD_DIM : 3 * HEAD_DIM, :] = value_grad.astype(BF16)


def part_spec(rows, width, row_block):
    per_part = width // QUERIES
    return pl.BlockSpec((1, rows, QUERIES), lambda i: (i // per_part, row_block, i % per_part))


def whole_spec(shape, at=None):
    place = at or (0,) * len(shape)
    return pl.BlockSpec(shape, lambda i: place, pipeline_mode=pl.Buffered(1))


def attention(qkv, table):
    count, _, width = qkv.shape
    tokens = count * width
    heads = (count, HEAD_DIM, width)
    return pl.pallas_call(
        attend_kernel,
        grid=(tokens // QUERIES,),
        in_specs=[
            part_spec(HEAD_DIM, width, 0),
            whole_spec(heads, (0, 1, 0)),
            whole_spec(heads, (0, 2, 0)),
            whole_spec(table.shape),
        ],
        out_specs=[part_spec(HEAD_DIM, width, 0), part_spec(HEAD_DIM, width, 0), part_spec(8, width, 0)],
        out_shape=[
            jax.ShapeDtypeStruct(heads, BF16),
            jax.ShapeDtypeStruct(heads, F32),
            jax.ShapeDtypeStruct((count, 8, width), F32),
        ],
        scratch_shapes=[pltpu.VMEM((tokens, 256), BF16)],
        compiler_params=pltpu.CompilerParams(vmem_limit_bytes=48 << 20),
        cost_estimate=pl.CostEstimate(
            flops=2 * tokens * tokens * 512,
            bytes_accessed=6 * tokens * HEAD_DIM * 2,
            transcendentals=tokens * tokens,
        ),
        name="attend",
    )(qkv, qkv, qkv, table)


def attention_back(qkv, table, grad, exact, stat):
    count, _, width = qkv.shape
    tokens = count * width
    heads = (count, HEAD_DIM, width)
    return pl.pallas_call(
        attend_back_kernel,
        grid=(tokens // QUERIES,),
        in_specs=[
            part_spec(HEAD_DIM, width, 0),
            whole_spec(heads, (0, 1, 0)),
            whole_spec(heads, (0, 2, 0)),
            whole_spec(table.shape),
            whole_spec(table.shape[::-1]),
            part_spec(HEAD_DIM, width, 0),
            part_spec(HEAD_DIM, width, 0),
            part_spec(8, width, 0),
        ],
        out_specs=[whole_spec((count, 3 * HEAD_DIM, width)), whole_spec(table.shape)],
        out_shape=[
            jax.ShapeDtypeStruct((count, 3 * HEAD_DIM, width), BF16),
            jax.ShapeDtypeStruct(table.shape, F32),
        ],
        scratch_shapes=[
            pltpu.VMEM((tokens, 256), BF16),
            pltpu.VMEM((256, tokens), BF16),
            pltpu.VMEM((tokens, 128), BF16),
            pltpu.VMEM((tokens, 128), F32),
            pltpu.VMEM((tokens, 128), F32),
        ],
        compiler_params=pltpu.CompilerParams(vmem_limit_bytes=48 << 20),
        cost_estimate=pl.CostEstimate(
            flops=2 * tokens * tokens * 1280,
            bytes_accessed=12 * tokens * HEAD_DIM * 2,
            transcendentals=tokens * tokens,
        ),
        name="attend_back",
    )(qkv, qkv, qkv, table, table.T, grad, exact, stat)


def moments(values):
    center = jnp.mean(values, -1, keepdims=True)
    spread = jnp.mean(values * values, -1, keepdims=True)
    return center, lax.rsqrt(spread - center * center + EPSILON)


def shards(
    patches,
    qkv_weight,
    qv_bias,
    proj_weight,
    proj_bias,
    norm1_gain,
    norm1_shift,
    norm2_gain,
    norm2_shift,
    fc1_weight,
    fc1_bias,
    fc2_weight,
    fc2_bias,
    height_table,
    width_table,
    out_grad,
):
    rows, cols = lax.axis_size("row"), lax.axis_size("col")
    row, col = lax.axis_index("row"), lax.axis_index("col")
    width = patches.shape[1]
    part = patches.shape[2]
    model = part * rows
    own = width // rows
    hidden = fc1_bias.shape[0] // rows
    head = HEAD_DIM

    def over_row(values):
        return lax.all_gather(values, "row", axis=1, tiled=True)

    def spread_rows(values):
        moved = lax.all_to_all(values, "row", 0, 0, tiled=True)
        return moved.transpose(1, 0, 2).reshape(values.shape[1], model)

    def whole_weight(values):
        return lax.all_gather(spread_rows(values), "col", axis=0, tiled=False)

    residual = over_row(patches[0])
    cotangent = over_row(out_grad[0])
    vectors = lax.all_gather(
        jnp.stack([norm1_gain, norm1_shift, norm2_gain, norm2_shift, proj_bias, fc2_bias]),
        "row", axis=1, tiled=True,
    )
    gain1, shift1, gain2, shift2, bias_proj, bias_fc2 = [vectors[i] for i in range(6)]
    by_col = lax.all_gather(
        jnp.concatenate([qv_bias.reshape(-1), fc1_bias]), "col", axis=0, tiled=False
    )
    bias_qv = by_col[:, : 2 * rows * head].reshape(cols, 2, rows, head)
    bias_qv = lax.dynamic_index_in_dim(bias_qv, row, 2, keepdims=False)
    bias_fc1 = by_col[:, 2 * rows * head :].reshape(cols, rows, hidden)
    bias_fc1 = lax.dynamic_index_in_dim(bias_fc1, row, 1, keepdims=False)
    bias_fc1 = bias_fc1.reshape(cols * hidden)

    local_qkv = qkv_weight.reshape(part, 3, rows, head).transpose(2, 1, 3, 0)
    weight_qkv = whole_weight(local_qkv.reshape(rows, 3 * head, part))
    weight_proj = whole_weight(proj_weight.reshape(rows, head, part)).reshape(cols * head, model)
    weight_fc1 = whole_weight(fc1_weight.T.reshape(rows, hidden, part)).reshape(cols * hidden, model)
    weight_fc2 = whole_weight(fc2_weight.reshape(rows, hidden, part)).reshape(cols * hidden, model)

    zero_row = jnp.zeros((1, head), BF16)
    table = jnp.concatenate([height_table[::-1], zero_row, width_table[::-1], zero_row], 0)

    first = residual.astype(F32)
    center1, inv1 = moments(first)
    scaled1 = (first - center1) * inv1
    normed1 = (scaled1 * gain1 + shift1).astype(BF16)
    bias = jnp.stack([bias_qv[:, 0], jnp.zeros_like(bias_qv[:, 0]), bias_qv[:, 1]], 1)
    qkv = mm_nt(weight_qkv.reshape(cols * 3 * head, model), normed1)
    qkv = (qkv.reshape(cols, 3 * head, width) + bias.reshape(cols, 3 * head, 1)).astype(BF16)
    qkv = lax.all_to_all(qkv, "col", 0, 0, tiled=True)
    merged, exact, stat = attention(qkv, table)
    merged = lax.all_to_all(merged, "col", 0, 0, tiled=True).reshape(cols * head, width)

    def contract_rows(left, right):
        return lax.dot_general(left, right, (((0,), (0,)), ((), ())), preferred_element_type=F32)

    def tokens_of_row(values):
        return lax.dynamic_slice_in_dim(values, row * own, own, 0)

    def sum_tokens(values):
        return lax.psum_scatter(values.astype(BF16), "row", scatter_dimension=0, tiled=True)

    projected = sum_tokens(contract_rows(merged, weight_proj)).astype(F32)
    middle = tokens_of_row(residual).astype(F32) + (projected + bias_proj)
    center2, inv2 = moments(middle)
    scaled2 = (middle - center2) * inv2
    normed2 = (scaled2 * gain2 + shift2).astype(BF16)
    normed2 = lax.all_gather(normed2, "row", axis=0, tiled=True)
    preact = mm_nt(normed2, weight_fc1) + bias_fc1
    activated, gelu_back = jax.vjp(partial(jax.nn.gelu, approximate=False), preact)
    activated = activated.astype(BF16)
    lowered = sum_tokens(mm(activated, weight_fc2)).astype(F32)
    final = (middle + (lowered + bias_fc2)).astype(BF16)
    final = final.reshape(own, rows, part).transpose(1, 0, 2)
    final = lax.all_to_all(final, "row", 0, 0, tiled=True).reshape(width, part)

    act_grad = mm_nt(cotangent, weight_fc2)
    preact_grad = gelu_back(act_grad)[0].astype(BF16)
    normed2_grad = sum_tokens(mm(preact_grad, weight_fc1)).astype(F32)
    scaled_grad = normed2_grad * gain2
    middle_grad = tokens_of_row(cotangent).astype(F32) + inv2 * (
        scaled_grad
        - jnp.mean(scaled_grad, -1, keepdims=True)
        - scaled2 * jnp.mean(scaled_grad * scaled2, -1, keepdims=True)
    )
    branch_grad = lax.all_gather(middle_grad.astype(BF16), "row", axis=0, tiled=True)
    middle_own = middle_grad.reshape(own, rows, part).transpose(1, 0, 2)
    middle_own = lax.all_to_all(middle_own, "row", 0, 0, tiled=True).reshape(width, part)

    merged_grad = mm_nt(weight_proj, branch_grad).astype(BF16).reshape(cols, head, width)
    merged_grad = lax.all_to_all(merged_grad, "col", 0, 0, tiled=True)
    qkv_grad, table_grad = attention_back(qkv, table, merged_grad, exact, stat)
    bias_grad = jnp.sum(qkv_grad, (0, 2), dtype=F32).reshape(3, head)
    qkv_grad = lax.all_to_all(qkv_grad, "col", 0, 0, tiled=True).reshape(cols * 3 * head, width)

    normed1_grad = contract_rows(qkv_grad, weight_qkv.reshape(cols * 3 * head, model))
    gain1_part = jnp.sum(normed1_grad * scaled1, 0)
    shift1_part = jnp.sum(normed1_grad, 0)
    scaled_grad = normed1_grad * gain1
    means = lax.psum(
        jnp.stack([jnp.sum(scaled_grad, -1), jnp.sum(scaled_grad * scaled1, -1)]), "row"
    ) / model
    by_row = normed1_grad.astype(BF16).reshape(width, rows, part).transpose(1, 0, 2)
    normed1_own = lax.psum_scatter(by_row, "row", scatter_dimension=0, tiled=False).astype(F32)
    scaled1_own = (patches[0].astype(F32) - center1) * inv1
    input_grad = middle_own + inv1 * (
        normed1_own * norm1_gain - means[0][:, None] - scaled1_own * means[1][:, None]
    )

    def weight_back(values):
        values = lax.psum_scatter(values.astype(BF16), "col", scatter_dimension=0, tiled=False)
        values = lax.psum(values, "batch")
        values = values.reshape(-1, rows, part).transpose(1, 0, 2)
        return lax.all_to_all(values, "row", 0, 0, tiled=True).astype(F32)

    fc2_grad = contract_rows(activated, cotangent).reshape(cols, hidden, model)
    fc2_grad = weight_back(fc2_grad).reshape(rows * hidden, part)
    fc1_grad = contract_rows(preact_grad, normed2).reshape(cols, hidden, model)
    fc1_grad = weight_back(fc1_grad).reshape(rows * hidden, part).T
    proj_grad = mm(merged, branch_grad).reshape(cols, head, model)
    proj_grad = weight_back(proj_grad).reshape(rows * head, part)
    qkv_weight_grad = mm(qkv_grad, normed1).reshape(cols, 3 * head, model)
    qkv_weight_grad = weight_back(qkv_weight_grad).reshape(rows, 3, head, part)
    qkv_weight_grad = qkv_weight_grad.transpose(3, 1, 0, 2).reshape(part, 3, rows * head)

    everywhere = ("batch", "row", "col")
    fc1_bias_part = jnp.sum(preact_grad, 0, dtype=F32).reshape(cols, 1, hidden)
    fc1_bias_part = lax.dynamic_update_slice(
        jnp.zeros((cols, rows, hidden), F32), fc1_bias_part, (0, row, 0)
    )
    fc2_bias_part = jnp.sum(out_grad[0], 0, dtype=F32)
    fc2_bias_grad = lax.psum(fc2_bias_part, ("batch", "col"))
    gain2_grad, shift2_grad, proj_bias_grad, fc1_bias_grad = lax.psum(
        (
            jnp.sum(normed2_grad * scaled2, 0),
            jnp.sum(normed2_grad, 0),
            jnp.sum(tokens_of_row(branch_grad), 0, dtype=F32),
            fc1_bias_part,
        ),
        everywhere,
    )
    bias_part = lax.dynamic_update_slice(
        jnp.zeros((cols, 2, rows, head), F32),
        jnp.stack([bias_grad[0], bias_grad[2]])[None, :, None],
        (col, 0, row, 0),
    )
    table_grad, bias_total = lax.psum((table_grad, bias_part), everywhere)
    gain1_grad, shift1_grad = lax.psum((gain1_part, shift1_part), everywhere)

    def features_of_row(values):
        return lax.dynamic_slice_in_dim(values, row * part, part, 0)

    side = 2 * GRID - 1
    return (
        final[None],
        input_grad[None],
        qkv_weight_grad,
        lax.dynamic_index_in_dim(bias_total, col, 0, keepdims=False).reshape(2, rows * head),
        proj_grad,
        features_of_row(proj_bias_grad),
        features_of_row(gain1_grad),
        features_of_row(shift1_grad),
        features_of_row(gain2_grad),
        features_of_row(shift2_grad),
        fc1_grad,
        lax.dynamic_index_in_dim(fc1_bias_grad, col, 0, keepdims=False).reshape(rows * hidden),
        fc2_grad,
        fc2_bias_grad,
        table_grad[:side][::-1],
        table_grad[2 * GRID : 2 * GRID + side][::-1],
    )


def solution(mesh):
    in_specs = (
        P("batch", "col", "row"),
        P("row", None, "col"),
        P(None, "col"),
        P("col", "row"),
        P("row"),
        P("row"),
        P("row"),
        P("row"),
        P("row"),
        P("row", "col"),
        P("col"),
        P("col", "row"),
        P("row"),
        P(),
        P(),
        P("batch", "col", "row"),
    )
    out_specs = (
        P("batch", "col", "row"),
        P("batch", "col", "row"),
        P("row", None, "col"),
        P(None, "col"),
        P("col", "row"),
        P("row"),
        P("row"),
        P("row"),
        P("row"),
        P("row"),
        P("row", "col"),
        P("col"),
        P("col", "row"),
        P("row"),
        P(),
        P(),
    )
    return jax.shard_map(shards, mesh=mesh, in_specs=in_specs, out_specs=out_specs, check_vma=False)
```

time: 2660 us -> 1190 us (0.45)
  waiting for transfers between devices: 1470 us -> 626 us
  local copies, waits for them, and re-layouts: 380 us -> 63.8 us
  matrix products: 398 us -> 89.6 us
  other arithmetic: 324 us -> 24.1 us
  blocking collectives: 52.3 us -> 179 us
  Pallas kernels: 0 us -> 126 us
  starting transfers between devices: 1.41 us -> 56.1 us
    reduce_scatter x9 -> x8, waiting for transfers between devices: 911 us -> 136 us  [the longest x3 76.8 us: sum_tokens(): lax.psum_scatter(values.astype(BF16), 'row', scatter_dimension=0, tiled=T...]
    dot_general x76 -> x12, matrix products: 398 us -> 89.6 us  [the longest x4 38.2 us: mm_nt(): lax.dot_general(left, right, (((1,), (1,)), ((), ())), preferred_element_...]
    all_gather x9 -> x7, waiting for transfers between devices: 428 us -> 202 us  [the longest x3 147 us: whole_weight(): return lax.all_gather(spread_rows(values), 'col', axis=0, tiled=False)]
    add x9 -> x3, local copies, waits for them, and re-layouts: 223 us -> 2.95 us  [the longest x1 2.78 us: shards(): tokens_of_row(cotangent).astype(F32)]
    all_to_all x0 -> x11, waiting for transfers between devices: none -> 143 us  [the longest x1 63.3 us: shards(): lax.all_to_all(qkv_grad, 'col', 0, 0, tiled=True)]
    pallas_call x0 -> x2, Pallas kernels: none -> 126 us  [the longest x1 63.7 us: attention_back(): pl.pallas_call(attend_back_kernel, grid=(tokens // QUERIES,), in_specs=[p...]
    reduce_sum x18 -> x7, other arithmetic: 119 us -> 8.03 us  [the longest x2 2.1 us: moments(): center = jnp.mean(values, -1, keepdims=True)]
    add x13 -> x1, other arithmetic: 91 us -> 2.6 us  [shards(): middle_own + inv1 * (normed1_own * norm1_gain - means[0][:, None] - scale...]
  transfers between devices with their start and end apart: 20 -> 28, of which waited for: 20 -> 18; matrix products, arithmetic and copies ran while one was open for 5% -> 12% of each run, Pallas kernels for 0% -> 11%
where the time goes in v1:
time: 1190 us; the launch traced here: 1180 us
  waiting for transfers between devices  626 us (53%)
  blocking collectives  179 us (15%)
  Pallas kernels  126 us (11%)
  matrix products  89.6 us (8%)
  local copies, waits for them, and re-layouts  63.8 us (5%)
  starting transfers between devices  56.1 us (5%)
  other arithmetic  24.1 us (2%)
  between operations  14.9 us (1%)
    all_gather x3, waiting for transfers between devices, whole_weight(): return lax.all_gather(spread_rows(values), 'col', axis=0, tiled=False)  147 us
    psum x1, waiting for transfers between devices, shards(): table_grad, bias_total = lax.psum((table_grad, bias_part), everywhere)  125 us
    reduce_scatter x3, waiting for transfers between devices, sum_tokens(): lax.psum_scatter(values.astype(BF16), 'row', scatter_dimension=0, tiled=T...  76.8 us
    pallas_call x1, Pallas kernels, attention_back(): pl.pallas_call(attend_back_kernel, grid=(tokens // QUERIES,), in_specs=[p...  63.7 us
    all_to_all x1, waiting for transfers between devices, shards(): lax.all_to_all(qkv_grad, 'col', 0, 0, tiled=True)  63.3 us
    pallas_call x1, Pallas kernels, attention(): pl.pallas_call(attend_kernel, grid=(tokens // QUERIES,), in_specs=[part_s...  62.2 us
    reduce_scatter x4, waiting for transfers between devices, weight_back(): lax.psum_scatter(values.astype(BF16), 'col', scatter_dimension=0, tiled=F...  59.4 us
    psum x1, blocking collectives, shards(): table_grad, bias_total = lax.psum((table_grad, bias_part), everywhere)  57.4 us
  transfers between devices with their start and end apart: 28, of which 18 were waited for; matrix products, arithmetic and copies ran while one was open for 12% of the time, Pallas kernels for 11%

profile of v1, /device:TPU:8, one launch (start us, length us, event | category | flops | bytes accessed | tf_op | source)
XLA Modules:
  0.0 1179.6 jit_solution(5910710321426009404)
XLA Ops:
  9.9 15.1 %all_to_all.70 = bf16[4,240,320]{1,2,0:T(8,128)(2,1)S(1)} all-to-all(bf16[4,240,320]{1,2,0:T(8,128)(2,1)S(1)} %copy.129), channel_id=1, replica_groups=mesh['batch'=2,'row'=4,'col'=4] {'row'}, dimensions={0} | all-to-all | bytes 1228800 | tf_op jit(solution)/shard_map/all_to_all | solution.py:318
  31.9 13.5 %all-gather.4 = f32[4,1,1920]{2,1,0:T(1,128)S(1)} all-gather(f32[1,1,1920]{2,1,0:T(1,128)S(1)} %reshape.300), channel_id=3, replica_groups=mesh['batch'=2,'row'=4,'col'=4] {'col'}, dimensions={0}, use_global_device_ids=true | all-gather | bytes 38400 | tf_op jit(solution)/shard_map/all_gather | solution.py:331
  50.7 40.7 %all-gather.13.cloned.1.call-done = bf16[4,240,1280]{2,1,0:T(8,128)(2,1)} async-done(((bf16[1,240,1280]{2,1,0:T(8,128)(2,1)}), bf16[4,240,1280]{2,1,0:T(8,128)(2,1)}) %all-gather.13.cloned.1.call-update) | async-done | bytes 2457616 | tf_op jit(solution)/shard_map/all_gather | solution.py:322
  104.0 41.9 %all-to-all-done.1.q_ref.k_ref.v_ref = bf16[4,240,1024]{2,1,0:T(8,128)(2,1)S(1)} async-done(((bf16[4,240,1024]{2,1,0:T(8,128)(2,1)}), bf16[4,240,1024]{2,1,0:T(8,128)(2,1)S(1)}, u32[]{:S(2)}, u32[]{:S(2)}) %all-to-all-start.1) | async-done | bytes 1966112 | tf_op jit(solution)/shard_map/all_to_all | solution.py:356
  150.0 62.2 %attend.1 = (bf16[4,80,1024]{2,1,0:T(8,128)(2,1)}, f32[4,80,1024]{2,1,0:T(8,128)S(1)}, f32[4,8,1024]{2,1,0:T(8,128)S(1)}) custom-call(bf16[4,240,1024]{2,1,0:T(8,128)(2,1)S(1)} %all-to-all-done.1.q_ref.k_ref.v_ref, bf16[4,240,1024]{2,1,0:T(8,128)(2,1)S(1)} %all-to-all-done.1.q_ref.k_ref.v_ref, bf16[4,240,1024]{2,1,0:T(8,128)(2,1)S(1)} %all-to-all-done.1.q_ref.k_ref.v_ref, ...), custom_call_target="tpu_custom_call" | custom-call | flops 17179869184 | bytes 3932160 | tf_op jit(solution)/shard_map/attend/pallas_call | solution.py:216
  220.8 29.7 %all_gather.38 = bf16[4,80,1280]{2,1,0:T(8,128)(2,1)} all-gather(bf16[1,80,1280]{2,1,0:T(8,128)(2,1)S(1)} %all_gather_reshape.13), channel_id=1, replica_groups=mesh['batch'=2,'row'=4,'col'=4] {'col'}, dimensions={0}, use_global_device_ids=true | all-gather | bytes 1024000 | tf_op jit(solution)/shard_map/all_gather | solution.py:322
  255.7 17.2 %all_to_all.71 = bf16[4,320,320]{2,1,0:T(8,128)(2,1)S(1)} all-to-all(bf16[4,320,320]{2,1,0:T(8,128)(2,1)S(1)} %bitcast.188), channel_id=1, replica_groups=mesh['batch'=2,'row'=4,'col'=4] {'row'}, dimensions={0} | all-to-all | bytes 1638400 | tf_op jit(solution)/shard_map/all_to_all | solution.py:318
  275.4 16.4 %reduce-scatter.9.cloned.1.call-done = bf16[256,1280]{1,0:T(8,128)(2,1)} async-done(((bf16[1024,1280]{1,0:T(8,128)(2,1)}), bf16[256,1280]{1,0:T(8,128)(2,1)}) %reduce-scatter.9.cloned.1.call-update) | async-done | bytes 655376 | tf_op jit(solution)/shard_map/reduce_scatter | solution.py:367
  297.3 16.2 %all_to_all.72 = bf16[4,320,320]{2,1,0:T(8,128)(2,1)S(1)} all-to-all(bf16[4,320,320]{2,1,0:T(8,128)(2,1)S(1)} %bitcast.189), channel_id=1, replica_groups=mesh['batch'=2,'row'=4,'col'=4] {'row'}, dimensions={0} | all-to-all | bytes 1638400 | tf_op jit(solution)/shard_map/all_to_all | solution.py:318
  316.4 40.7 %all-gather.17.cloned.1.call-done = bf16[4,320,1280]{2,1,0:T(8,128)(2,1)} async-done(((bf16[1,320,1280]{2,1,0:T(8,128)(2,1)}), bf16[4,320,1280]{2,1,0:T(8,128)(2,1)}) %all-gather.17.cloned.1.call-update) | async-done | bytes 3276816 | tf_op jit(solution)/shard_map/all_gather | solution.py:322
  357.2 28.7 %all-gather.15.cloned.1.call-done = bf16[1024,1280]{1,0:T(8,128)(2,1)} async-done(((bf16[256,1280]{1,0:T(8,128)(2,1)}), bf16[1024,1280]{1,0:T(8,128)(2,1)}) %all-gather.15.cloned.1.call-update) | async-done | bytes 2621456 | tf_op jit(solution)/shard_map/all_gather | solution.py:374
  385.9 18.1 %multiply_convert_fusion = (bf16[1024,1280]{1,0:T(8,128)(2,1)}, f32[1024,1280]{1,0:T(8,128)}, f32[1024,1280]{1,0:T(8,128)}) fusion(f32[1280]{0:T(1024)S(1)} %add.185, bf16[1024,1280]{1,0:T(8,128)(2,1)} %all-gather.15.cloned.1.call-done, bf16[1280,1280]{1,0:T(8,128)(2,1)} %bitcast.215), kind=kOutput, calls=%fused_computation.23 | convolution fusion | flops 3441950720 | bytes 19010560 | tf_op jit(solution)/shard_map/dot_general | solution.py:30
  403.9 9.0 all-gather.25.cloned.1.call-done
  413.0 65.5 %all-gather.19.cloned.1.call-done = bf16[4,320,1280]{2,1,0:T(8,128)(2,1)} async-done(((bf16[1,320,1280]{2,1,0:T(8,128)(2,1)}), bf16[4,320,1280]{2,1,0:T(8,128)(2,1)}) %all-gather.19.cloned.1.call-update) | async-done | bytes 3276816 | tf_op jit(solution)/shard_map/all_gather | solution.py:322
  478.4 11.9 %convert_reduce_fusion.1 = (f32[1280]{0:T(1024)}, bf16[1024,1280]{1,0:T(8,128)(2,1)S(1)}) fusion(f32[1024,1280]{1,0:T(8,128)} %get-tuple-element.136, bf16[1280,1280]{1,0:T(8,128)(2,1)} %bitcast.217, bf16[1,1024,1280]{1,2,0:T(8,128)(2,1)} %all-gather.25.cloned.1.call-done, f32[1024,1280]{1,0:T(8,128)} %get-tuple-element.152, f32[1280]{0:T(1024)S(1)} %add.185), kind=kOutput, calls=%fused_computation.21 | convolution fusion | flops 3377724160 | bytes 19015680 | tf_op jit(solution)/shard_map/dot_general | solution.py:30
  497.0 7.8 convolution_convert_fusion.3
  507.3 25.2 %reduce-scatter.13.cloned.1.call-done = bf16[256,1280]{1,0:T(8,128)(2,1)} async-done(((bf16[1024,1280]{1,0:T(8,128)(2,1)}), bf16[256,1280]{1,0:T(8,128)(2,1)}) %reduce-scatter.13.cloned.1.call-update) | async-done | bytes 655376 | tf_op jit(solution)/shard_map/reduce_scatter | solution.py:367
  534.7 35.2 %reduce-scatter.11.cloned.1.call-done = bf16[256,1280]{1,0:T(8,128)(2,1)} async-done(((bf16[1024,1280]{1,0:T(8,128)(2,1)}), bf16[256,1280]{1,0:T(8,128)(2,1)}) %reduce-scatter.11.cloned.1.call-update) | async-done | bytes 655376 | tf_op jit(solution)/shard_map/reduce_scatter | solution.py:367
  573.7 7.8 convolution_convert_fusion.1
  581.6 17.8 %all-gather.21.cloned.1.call-done = bf16[1024,1280]{1,0:T(8,128)(2,1)} async-done(((bf16[256,1280]{1,0:T(8,128)(2,1)}), bf16[1024,1280]{1,0:T(8,128)(2,1)}) %all-gather.21.cloned.1.call-update) | async-done | bytes 2621456 | tf_op jit(solution)/shard_map/all_gather | solution.py:392
  608.6 7.9 convolution_convert_fusion
  616.6 24.1 %all-to-all-done.8.grad_ref = bf16[4,80,1024]{2,1,0:T(8,128)(2,1)S(1)} async-done(((bf16[4,80,1024]{2,1,0:T(8,128)(2,1)}), bf16[4,80,1024]{2,1,0:T(8,128)(2,1)S(1)}, u32[]{:S(2)}, u32[]{:S(2)}) %all-to-all-start.8) | async-done | bytes 655392 | tf_op jit(solution)/shard_map/all_to_all | solution.py:397
  640.7 63.7 %attend_back.1 = (bf16[4,240,1024]{2,1,0:T(8,128)(2,1)}, f32[256,80]{1,0:T(8,128)}) custom-call(bf16[4,240,1024]{2,1,0:T(8,128)(2,1)} %copy-done, bf16[4,240,1024]{2,1,0:T(8,128)(2,1)} %copy-done, bf16[4,240,1024]{2,1,0:T(8,128)(2,1)} %copy-done, bf16[256,80]{1,0:T(8,128)(2,1)S(1)} %copy.131.tab_ref, bf16[80,256]{1,0:T(8,128)(2,1)S(1)} %get-tuple-element.140.tab_t_ref, ...), custom_call_target="tpu_custom_call" | custom-call | flops 42949672960 | bytes 7864320 | tf_op jit(solution)/shard_map/attend_back/pallas_call | solution.py:246
  704.4 7.7 all-to-all-start.9
  716.5 63.3 %all-to-all-done.9 = bf16[4,240,1024]{2,1,0:T(8,128)(2,1)} async-done(((bf16[4,240,1024]{2,1,0:T(8,128)(2,1)}), bf16[4,240,1024]{2,1,0:T(8,128)(2,1)}, u32[]{:S(2)}, u32[]{:S(2)}) %all-to-all-start.9) | async-done | bytes 1966112 | tf_op jit(solution)/shard_map/all_to_all | solution.py:400
  790.2 9.3 reduce-scatter.19.cloned.1.call-done
  801.5 50.1 %reduce-scatter.17.cloned.1.call-done = bf16[1,240,1280]{2,1,0:T(8,128)(2,1)} async-done(((bf16[4,240,1280]{2,1,0:T(8,128)(2,1)}), bf16[1,240,1280]{2,1,0:T(8,128)(2,1)}) %reduce-scatter.17.cloned.1.call-update) | async-done | bytes 614416 | tf_op jit(solution)/shard_map/reduce_scatter | solution.py:417
  854.4 8.7 bitcast_convert_fusion
  887.8 19.0 %psum.110 = f32[320]{0:T(512)} all-reduce(f32[320]{0:T(512)S(1)} %convert_reduce_fusion.4), channel_id=1, replica_groups=mesh['batch'=2,'row'=4,'col'=4] {'batch','col'}, use_global_device_ids=true, to_apply=%region_36.37 | all-reduce | flops 320 | bytes 2560 | tf_op jit(solution)/shard_map/psum | solution.py:438
  919.1 16.9 %all-reduce.7.cloned.1.call-done = (bf16[4,320,320]{1,2,0:T(8,128)(2,1)}, bf16[4,320,320]{1,2,0:T(8,128)(2,1)}, bf16[4,240,320]{1,2,0:T(8,128)(2,1)}, bf16[4,80,320]{2,1,0:T(8,128)(2,1)}) async-done(((bf16[4,320,320]{1,2,0:T(8,128)(2,1)}, bf16[4,320,320]{1,2,0:T(8,128)(2,1)}, bf16[4,240,320]{1,2,0:T(8,128)(2,1)}, bf16[4,80,320]{2,1,0:T(8,128)(2,1)}), (bf16[4,320,320]{1,2,0:T(8,128)(2,1)}, ...) | async-done | bytes 2457616 | tf_op jit(solution)/shard_map/psum | solution.py:418
  939.4 125.3 %all-reduce.5.cloned.1.call-done = f32[256,80]{1,0:T(8,128)} async-done(((f32[256,80]{1,0:T(8,128)}), f32[256,80]{1,0:T(8,128)}) %all-reduce.5.cloned.1.call-update) | async-done | bytes 81936 | tf_op jit(solution)/shard_map/psum | solution.py:453
  1085.4 57.4 %all-reduce = (f32[4,2,4,80]{3,1,2,0:T(2,128)S(1)}, f32[1280]{0:T(1024)S(1)}, f32[1280]{0:T(1024)S(1)}, f32[1280]{0:T(1024)S(1)}, f32[1280]{0:T(1024)S(1)}, /*index=5*/f32[1280]{0:T(1024)S(1)}, f32[4,4,320]{2,1,0:T(4,128)S(1)}) all-reduce(f32[4,2,4,80]{3,1,2,0:T(2,128)S(1)} %constant_dynamic-up, ...), channel_id=1, replica_groups=mesh['batch'=2,'row'=4,'col'=4] {'batch','row','col'}, use_global_device_ids=true, to_apply=%region_16.17 | all-reduce | flops 14080 | bytes 112640 | tf_op jit(solution)/shard_map/psum | solution.py:453
  (238 shorter events, 190.4 us)
Async XLA Ops:
  7.2 39.4 %all-gather.23.cloned.1.call-start = ((), (), s32[]{:S(2)}) async-start(), calls=%async_computation.36 | async-start | bytes 3276800 | tf_op jit(solution)/shard_map/all_gather | solution.py:315
  7.9 83.5 %all-gather.13.cloned.1.call-start = ((), (), s32[]{:S(2)}) async-start(), calls=%async_computation.22 | async-start | bytes 3072000 | tf_op jit(solution)/shard_map/all_gather | solution.py:322
  97.7 48.3 %all-to-all-start.1 = ((bf16[4,240,1024]{2,1,0:T(8,128)(2,1)}), bf16[4,240,1024]{2,1,0:T(8,128)(2,1)S(1)}, u32[]{:S(2)}, u32[]{:S(2)}) async-start(bf16[4,240,1024]{2,1,0:T(8,128)(2,1)} %add_convert_fusion.1), calls=%async_computation.1 | async-start | bytes 3932160 | tf_op jit(solution)/shard_map/all_to_all | solution.py:356
  145.9 66.2 %all-to-all-start.3 = ((bf16[4,80,320]{2,1,0:T(8,128)(2,1)}), bf16[4,80,320]{2,1,0:T(8,128)(2,1)}, u32[]{:S(2)}, u32[]{:S(2)}) async-start(bf16[4,80,320]{2,1,0:T(8,128)(2,1)} %bitcast.14), calls=%async_computation.3 | async-start | bytes 491520 | tf_op jit(solution)/shard_map/all_to_all | solution.py:318
  212.2 38.3 %all-to-all-start.2 = ((bf16[4,80,1024]{2,1,0:T(8,128)(2,1)}), bf16[4,80,1024]{2,1,0:T(8,128)(2,1)}, u32[]{:S(2)}, u32[]{:S(2)}) async-start(bf16[4,80,1024]{2,1,0:T(8,128)(2,1)} %get-tuple-element.21), calls=%async_computation.2 | async-start | bytes 1310720 | tf_op jit(solution)/shard_map/all_to_all | solution.py:358
  219.6 72.2 %reduce-scatter.9.cloned.1.call-start = ((), (), s32[]{:S(2)}) async-start(), calls=%async_computation.23 | async-start | bytes 3276800 | tf_op jit(solution)/shard_map/reduce_scatter | solution.py:367
  255.0 102.1 %all-gather.17.cloned.1.call-start = ((), (), s32[]{:S(2)}) async-start(), calls=%async_computation.25 | async-start | bytes 4096000 | tf_op jit(solution)/shard_map/all_gather | solution.py:322
  275.3 110.5 %all-gather.15.cloned.1.call-start = ((), (), s32[]{:S(2)}) async-start(), calls=%async_computation.24 | async-start | bytes 3276800 | tf_op jit(solution)/shard_map/all_gather | solution.py:374
  296.1 116.9 %all-gather.25.cloned.1.call-start = ((), (), s32[]{:S(2)}) async-start(), calls=%async_computation.37 | async-start | bytes 3276800 | tf_op jit(solution)/shard_map/all_gather | solution.py:315
  296.6 181.8 %all-gather.19.cloned.1.call-start = ((), (), s32[]{:S(2)}) async-start(), calls=%async_computation.26 | async-start | bytes 4096000 | tf_op jit(solution)/shard_map/all_gather | solution.py:322
  316.0 216.6 %reduce-scatter.13.cloned.1.call-start = ((), (), s32[]{:S(2)}) async-start(), calls=%async_computation.28 | async-start | bytes 3276800 | tf_op jit(solution)/shard_map/reduce_scatter | solution.py:367
  496.7 73.2 %reduce-scatter.11.cloned.1.call-start = ((), (), s32[]{:S(2)}) async-start(), calls=%async_computation.27 | async-start | bytes 3276800 | tf_op jit(solution)/shard_map/reduce_scatter | solution.py:367
  504.8 94.6 %all-gather.21.cloned.1.call-start = ((), (), s32[]{:S(2)}) async-start(), calls=%async_computation.29 | async-start | bytes 3276800 | tf_op jit(solution)/shard_map/all_gather | solution.py:392
  573.7 212.1 %reduce-scatter.21.cloned.1.call-start = ((), (), s32[]{:S(2)}) async-start(), calls=%async_computation.33 | async-start | bytes 4096000 | tf_op jit(solution)/shard_map/reduce_scatter | solution.py:417
  603.0 37.6 %all-to-all-start.8 = ((bf16[4,80,1024]{2,1,0:T(8,128)(2,1)}), bf16[4,80,1024]{2,1,0:T(8,128)(2,1)S(1)}, u32[]{:S(2)}, u32[]{:S(2)}) async-start(bf16[4,80,1024]{2,1,0:T(8,128)(2,1)} %bitcast.205), calls=%async_computation.11 | async-start | bytes 1310720 | tf_op jit(solution)/shard_map/all_to_all | solution.py:397
  608.2 179.9 %reduce-scatter.23.cloned.1.call-start = ((), (), s32[]{:S(2)}) async-start(), calls=%async_computation.34 | async-start | bytes 4096000 | tf_op jit(solution)/shard_map/reduce_scatter | solution.py:417
  704.4 75.4 %all-to-all-start.9 = ((bf16[4,240,1024]{2,1,0:T(8,128)(2,1)}), bf16[4,240,1024]{2,1,0:T(8,128)(2,1)}, u32[]{:S(2)}, u32[]{:S(2)}) async-start(bf16[4,240,1024]{2,1,0:T(8,128)(2,1)} %get-tuple-element.24), calls=%async_computation.12 | async-start | bytes 3932160 | tf_op jit(solution)/shard_map/all_to_all | solution.py:400
  712.2 67.6 %copy-start.18 = (f32[1280]{0:T(1024)S(1)}, f32[1280]{0:T(1024)}, u32[]{:S(2)}) copy-start(f32[1280]{0:T(1024)} %copy-done.17) | copy-start | bytes 15364
  712.2 87.4 %reduce-scatter.19.cloned.1.call-start = ((), (), s32[]{:S(2)}) async-start(), calls=%async_computation.32 | async-start | bytes 1024000 | tf_op jit(solution)/shard_map/reduce_scatter | solution.py:417
  716.2 135.3 %reduce-scatter.17.cloned.1.call-start = ((), (), s32[]{:S(2)}) async-start(), calls=%async_computation.31 | async-start | bytes 3072000 | tf_op jit(solution)/shard_map/reduce_scatter | solution.py:417
  785.8 150.2 %all-reduce.7.cloned.1.call-start = ((), (), s32[]{:S(2)}) async-start(), calls=%async_computation.38 | async-start | bytes 5734400 | tf_op jit(solution)/shard_map/psum | solution.py:418
  853.8 210.9 %all-reduce.5.cloned.1.call-start = ((), (), s32[]{:S(2)}) async-start(), calls=%async_computation.35 | async-start | bytes 262144 | tf_op jit(solution)/shard_map/psum | solution.py:453
  854.3 303.4 %reduce-scatter.15.cloned.1.call-start = ((), (), s32[]{:S(2)}) async-start(), calls=%async_computation.30 | async-start | bytes 3276800 | tf_op jit(solution)/shard_map/reduce_scatter | solution.py:410
  868.6 14.6 %all-to-all-start.6 = ((bf16[4,256,320]{1,2,0:T(8,128)(2,1)}), bf16[4,256,320]{1,2,0:T(8,128)(2,1)}, u32[]{:S(2)}, u32[]{:S(2)}) async-start(bf16[4,256,320]{1,2,0:T(8,128)(2,1)} %bitcast.198), calls=%async_computation.8 | async-start | bytes 1310720 | tf_op jit(solution)/shard_map/all_to_all | solution.py:381
  883.2 26.6 %all-to-all-start.7 = ((f32[4,256,320]{1,2,0:T(8,128)}), f32[4,256,320]{1,2,0:T(8,128)}, u32[]{:S(2)}, u32[]{:S(2)}) async-start(f32[4,256,320]{1,2,0:T(8,128)} %bitcast.186), calls=%async_computation.10 | async-start | bytes 2621440 | tf_op jit(solution)/shard_map/all_to_all | solution.py:394
  936.0 131.1 %all-to-all-start.11 = ((bf16[4,80,320]{2,1,0:T(8,128)(2,1)}), bf16[4,80,320]{2,1,0:T(8,128)(2,1)S(1)}, u32[]{:S(2)}, u32[]{:S(2)}) async-start(bf16[4,80,320]{2,1,0:T(8,128)(2,1)} %get-tuple-element.132), calls=%async_computation.17 | async-start | bytes 491520 | tf_op jit(solution)/shard_map/all_to_all | solution.py:420
  1067.1 14.7 %all-to-all-start.10 = ((bf16[4,240,320]{1,2,0:T(8,128)(2,1)}), bf16[4,240,320]{1,2,0:T(8,128)(2,1)}, u32[]{:S(2)}, u32[]{:S(2)}) async-start(bf16[4,240,320]{1,2,0:T(8,128)(2,1)} %get-tuple-element.131), calls=%async_computation.15 | async-start | bytes 1310720 | tf_op jit(solution)/shard_map/all_to_all | solution.py:420
  1075.9 81.8 %copy-start.4 = (f32[1,1024,320]{1,2,0:T(8,128)S(1)}, f32[1,1024,320]{1,2,0:T(8,128)}, u32[]{:S(2)}) copy-start(f32[1,1024,320]{1,2,0:T(8,128)} %reshape.256) | copy-start | bytes 3932164
  1075.9 81.8 %copy-start.6 = (bf16[1,1024,320]{1,2,0:T(8,128)(2,1)S(1)}, bf16[1,1024,320]{1,2,0:T(8,128)(2,1)}, u32[]{:S(2)}) copy-start(bf16[1,1024,320]{1,2,0:T(8,128)(2,1)} %param.16) | copy-start | bytes 1966084
  1075.9 81.8 %copy-start.22 = (f32[320]{0:T(512)S(1)}, f32[320]{0:T(512)}, u32[]{:S(2)}) copy-start(f32[320]{0:T(512)} %param.21) | copy-start | bytes 3844
  1081.8 67.1 %all-to-all-start.12 = ((bf16[4,320,320]{1,2,0:T(8,128)(2,1)}), bf16[4,320,320]{1,2,0:T(8,128)(2,1)S(1)}, u32[]{:S(2)}, u32[]{:S(2)}) async-start(bf16[4,320,320]{1,2,0:T(8,128)(2,1)} %get-tuple-element.130), calls=%async_computation.19 | async-start | bytes 1966080 | tf_op jit(solution)/shard_map/all_to_all | solution.py:420
  1148.8 19.7 %all-to-all-start.13 = ((bf16[4,320,320]{1,2,0:T(8,128)(2,1)}), bf16[4,320,320]{1,2,0:T(8,128)(2,1)}, u32[]{:S(2)}, u32[]{:S(2)}) async-start(bf16[4,320,320]{1,2,0:T(8,128)(2,1)} %get-tuple-element.129), calls=%async_computation.21 | async-start | bytes 1966080 | tf_op jit(solution)/shard_map/all_to_all | solution.py:420
  (31 other events, 892.4 us)
Sparse Core Ops, SparseCore 0:
  9.6 28.9 all-gather.22
  40.7 50.6 all-gather.12
  255.1 36.6 reduce-scatter.8
  293.9 63.2 all-gather.16
  359.2 26.6 all-gather.14
  387.4 25.5 all-gather.24
  415.2 63.2 all-gather.18
  496.8 35.7 reduce-scatter.12
  535.1 34.6 reduce-scatter.10
  573.8 25.5 all-gather.20
  601.8 75.9 reduce-scatter.20
  680.1 93.9 reduce-scatter.22
  777.1 22.3 reduce-scatter.18
  801.8 49.7 reduce-scatter.16
  855.2 80.7 all-reduce.6
  942.3 122.3 all-reduce.4
  1067.2 44.6 reduce-scatter.14

commit v2 on v1

--- a/solution.py
+++ b/solution.py
@@ -20,6 +20,7 @@
 SCALE = HEAD_DIM**-0.5
 BF16 = jnp.bfloat16
 F32 = jnp.float32
+MESH = pl.DeviceIdType.MESH
 
 
 def mm(left, right):
@@ -207,6 +208,175 @@
 def whole_spec(shape, at=None):
     place = at or (0,) * len(shape)
     return pl.BlockSpec(shape, lambda i: place, pipeline_mode=pl.Buffered(1))
+
+
+MIX_SUBS = 2
+TO_NEAR, PASS_ON, TO_FAR, OUT_NEAR, OUT_FAR, OUT_ON = range(6)
+
+
+def normal(values):
+    center, inv = moments(values)
+    return (values - center) * inv, inv
+
+
+def normal_back(grad, scaled, inv, gain):
+    grad = grad * gain
+    return inv * (
+        grad
+        - jnp.mean(grad, -1, keepdims=True)
+        - scaled * jnp.mean(grad * scaled, -1, keepdims=True)
+    )
+
+
+def add_sums(sums_ref, piece, terms):
+    for place, term in enumerate(terms):
+        total = jnp.sum(term, 0, keepdims=True)
+        if piece:
+            total = total + sums_ref[place : place + 1]
+        sums_ref[place : place + 1] = total
+
+
+def forward_finish(total, piece, rows, vec_ref, first_ref, out_refs):
+    middle = first_ref[rows].astype(F32) + (total + vec_ref[2:3])
+    out_refs[0][rows] = middle
+    scaled, _ = normal(middle)
+    return (scaled * vec_ref[0:1] + vec_ref[1:2]).astype(BF16)
+
+
+def backward_finish(total, piece, rows, vec_ref, first_ref, add_ref, out_refs):
+    scaled, inv = normal(first_ref[rows].astype(F32))
+    result = add_ref[rows].astype(F32) + normal_back(total, scaled, inv, vec_ref[0:1])
+    branch = result.astype(BF16)
+    out_refs[0][rows] = result
+    add_sums(out_refs[1], piece, (total * scaled, total, branch.astype(F32)))
+    return branch
+
+
+def last_finish(total, piece, rows, vec_ref, first_ref, add_ref, out_refs):
+    scaled, inv = normal(first_ref[rows].astype(F32))
+    add_sums(out_refs[1], piece, (total * scaled, total))
+    return add_ref[rows] + normal_back(total, scaled, inv, vec_ref[0:1])
+
+
+def row_mix_kernel(finish, extra, outs, left_t, to_features, left_ref, weight_ref, *refs):
+    extra_refs, refs = refs[:extra], refs[extra:]
+    out_refs, refs = refs[:outs], refs[outs:]
+    gathered, out_refs = out_refs[0], out_refs[1:]
+    far_keep, own_keep, out_box, in_box, send_sems, recv_sems = refs[:6]
+    own = far_keep.shape[0]
+    sub = own // MIX_SUBS
+    me = lax.axis_index("row")
+    near = me + 1 - 2 * lax.rem(me, 2)
+    far = lax.rem(me + 2, 4)
+    diag = lax.rem(near + 2, 4)
+    peers = (near, far, diag) if to_features else (near, far)
+    barrier = pltpu.get_barrier_semaphore()
+    for peer in peers:
+        pl.semaphore_signal(barrier, device_id={"row": peer}, device_id_type=MESH)
+    pl.semaphore_wait(barrier, len(peers))
+
+    started = []
+
+    def send(source, target, kind, piece, peer):
+        copy = pltpu.make_async_remote_copy(
+            src_ref=source,
+            dst_ref=target,
+            send_sem=send_sems.at[kind, piece],
+            recv_sem=recv_sems.at[kind, piece],
+            device_id={"row": peer},
+            device_id_type=MESH,
+        )
+        copy.start()
+        started.append(copy)
+        return copy
+
+    def product(owner, piece):
+        at = pl.ds(pl.multiple_of(owner * own + piece * sub, sub), sub)
+        if left_t:
+            left = left_ref[:, at].astype(F32).T.astype(BF16)
+        else:
+            left = left_ref[at, :]
+        return mm(left, weight_ref[...])
+
+    pieces = [slice(piece * sub, (piece + 1) * sub) for piece in range(MIX_SUBS)]
+    passed, direct, summed = [], [], []
+    for piece, rows in enumerate(pieces):
+        out_box[0, rows] = product(diag, piece).astype(BF16)
+        passed.append(send(out_box.at[0, rows], in_box.at[0, rows], PASS_ON, piece, near))
+        far_keep[rows] = product(far, piece)
+    for piece, rows in enumerate(pieces):
+        out_box[1, rows] = product(near, piece).astype(BF16)
+        direct.append(send(out_box.at[1, rows], in_box.at[1, rows], TO_NEAR, piece, near))
+        passed[piece].wait_recv()
+        out_box[2, rows] = (far_keep[rows] + in_box[0, rows].astype(F32)).astype(BF16)
+        summed.append(send(out_box.at[2, rows], in_box.at[2, rows], TO_FAR, piece, far))
+    for piece, rows in enumerate(pieces):
+        own_keep[rows] = product(me, piece)
+    near_out, far_out, on_out = [], [], []
+    for piece, rows in enumerate(pieces):
+        direct[piece].wait_recv()
+        summed[piece].wait_recv()
+        total = own_keep[rows] + in_box[1, rows].astype(F32) + in_box[2, rows].astype(F32)
+        result = finish(total, piece, rows, *extra_refs, out_refs)
+        if to_features:
+            boxes, arrived = refs[6:]
+            part = gathered.shape[1]
+            for place in range(4):
+                boxes[place, rows] = result[:, place * part : (place + 1) * part].astype(BF16)
+            arrived[me, rows] = boxes[me, rows]
+            for kind, peer, copies in ((OUT_NEAR, near, near_out), (OUT_FAR, far, far_out), (OUT_ON, diag, on_out)):
+                copies.append(send(boxes.at[peer, rows], arrived.at[me, rows], kind, piece, peer))
+        else:
+            gathered[me, rows] = result
+            near_out.append(send(gathered.at[me, rows], gathered.at[me, rows], OUT_NEAR, piece, near))
+            far_out.append(send(gathered.at[me, rows], gathered.at[me, rows], OUT_FAR, piece, far))
+    for piece, rows in enumerate(pieces):
+        far_out[piece].wait_recv()
+        if not to_features:
+            on_out.append(send(gathered.at[far, rows], gathered.at[far, rows], OUT_ON, piece, near))
+    for copy in near_out + on_out:
+        copy.wait_recv()
+    if to_features:
+        boxes, arrived = refs[6:]
+        for source in range(4):
+            gathered[source * own : (source + 1) * own, :] = arrived[source].astype(F32)
+    for copy in started:
+        copy.wait_send()
+
+
+def row_mix(finish, name, number, left, weight, extra, out_shapes, left_t, to_features=False):
+    tokens = left.shape[1] if left_t else left.shape[0]
+    model = weight.shape[1]
+    own = tokens // 4
+    if to_features:
+        first = jax.ShapeDtypeStruct((tokens, model // 4), F32)
+        more = [pltpu.VMEM((4, own, model // 4), BF16), pltpu.VMEM((4, own, model // 4), BF16)]
+    else:
+        first = jax.ShapeDtypeStruct((4, own, model), BF16)
+        more = []
+    vmem = pl.BlockSpec(memory_space=pltpu.VMEM)
+    return pl.pallas_call(
+        partial(row_mix_kernel, finish, len(extra), 1 + len(out_shapes), left_t, to_features),
+        out_shape=[first, *out_shapes],
+        in_specs=[vmem] * (2 + len(extra)),
+        out_specs=[vmem] * (1 + len(out_shapes)),
+        scratch_shapes=[
+            pltpu.VMEM((own, model), F32),
+            pltpu.VMEM((own, model), F32),
+            pltpu.VMEM((3, own, model), BF16),
+            pltpu.VMEM((3, own, model), BF16),
+            pltpu.SemaphoreType.DMA((6, MIX_SUBS)),
+            pltpu.SemaphoreType.DMA((6, MIX_SUBS)),
+            *more,
+        ],
+        compiler_params=pltpu.CompilerParams(
+            collective_id=number, has_side_effects=True, vmem_limit_bytes=48 << 20
+        ),
+        cost_estimate=pl.CostEstimate(
+            flops=2 * tokens * weight.size, bytes_accessed=16 * own * model, transcendentals=0
+        ),
+        name=name,
+    )(left, weight, *extra)
 
 
 def attention(qkv, table):
@@ -278,6 +448,57 @@
     )(qkv, qkv, qkv, table, table.T, grad, exact, stat)
 
 
+def sum_kernel(axes, value_ref, out_ref, *scratch):
+    slots, sends, recvs = scratch[: len(axes)], scratch[len(axes) : -1], scratch[-1]
+    me = {name: lax.axis_index(name) for name, _ in axes}
+    barrier = pltpu.get_barrier_semaphore()
+    for name, size in axes:
+        for step in range(1, size):
+            pl.semaphore_signal(
+                barrier, device_id={name: lax.rem(me[name] + step, size)}, device_id_type=MESH
+            )
+    pl.semaphore_wait(barrier, sum(size - 1 for _, size in axes))
+    out_ref[...] = value_ref[...]
+    for order, (name, size) in enumerate(axes):
+        slot, send = slots[order], sends[order]
+        slot[me[name]] = out_ref[...]
+        copies = []
+        for step in range(1, size):
+            copy = pltpu.make_async_remote_copy(
+                src_ref=out_ref,
+                dst_ref=slot.at[me[name]],
+                send_sem=send.at[step],
+                recv_sem=recvs.at[order, step],
+                device_id={name: lax.rem(me[name] + step, size)},
+                device_id_type=MESH,
+            )
+            copy.start()
+            copies.append(copy)
+        for copy in copies:
+            copy.wait()
+        total = slot[0]
+        for source in range(1, size):
+            total = total + slot[source]
+        out_ref[...] = total
+
+
+def sum_everywhere(values):
+    axes = tuple((name, lax.axis_size(name)) for name in ("row", "batch", "col"))
+    return pl.pallas_call(
+        partial(sum_kernel, axes),
+        out_shape=jax.ShapeDtypeStruct(values.shape, F32),
+        in_specs=[pl.BlockSpec(memory_space=pltpu.VMEM)],
+        out_specs=pl.BlockSpec(memory_space=pltpu.VMEM),
+        scratch_shapes=[
+            *[pltpu.VMEM((size, *values.shape), F32) for _, size in axes],
+            *[pltpu.SemaphoreType.DMA((size,)) for _, size in axes],
+            pltpu.SemaphoreType.DMA((len(axes), max(size for _, size in axes))),
+        ],
+        compiler_params=pltpu.CompilerParams(collective_id=0, has_side_effects=True, vmem_limit_bytes=32 << 20),
+        name="sum_everywhere",
+    )(values)
+
+
 def moments(values):
     center = jnp.mean(values, -1, keepdims=True)
     spread = jnp.mean(values * values, -1, keepdims=True)
@@ -318,9 +539,6 @@
         moved = lax.all_to_all(values, "row", 0, 0, tiled=True)
         return moved.transpose(1, 0, 2).reshape(values.shape[1], model)
 
-    def whole_weight(values):
-        return lax.all_gather(spread_rows(values), "col", axis=0, tiled=False)
-
     residual = over_row(patches[0])
     cotangent = over_row(out_grad[0])
     vectors = lax.all_gather(
@@ -338,10 +556,18 @@
     bias_fc1 = bias_fc1.reshape(cols * hidden)
 
     local_qkv = qkv_weight.reshape(part, 3, rows, head).transpose(2, 1, 3, 0)
-    weight_qkv = whole_weight(local_qkv.reshape(rows, 3 * head, part))
-    weight_proj = whole_weight(proj_weight.reshape(rows, head, part)).reshape(cols * head, model)
-    weight_fc1 = whole_weight(fc1_weight.T.reshape(rows, hidden, part)).reshape(cols * hidden, model)
-    weight_fc2 = whole_weight(fc2_weight.reshape(rows, hidden, part)).reshape(cols * hidden, model)
+    local_rest = jnp.concatenate(
+        [
+            proj_weight.reshape(rows, head, part),
+            fc1_weight.T.reshape(rows, hidden, part),
+            fc2_weight.reshape(rows, hidden, part),
+        ],
+        1,
+    )
+    spread_qkv = spread_rows(local_qkv.reshape(rows, 3 * head, part))
+    local_rest, spread_qkv = lax.optimization_barrier((local_rest, spread_qkv))
+    spread_rest = spread_rows(local_rest)
+    weight_qkv = lax.all_gather(spread_qkv, "col", axis=0, tiled=True)
 
     zero_row = jnp.zeros((1, head), BF16)
     table = jnp.concatenate([height_table[::-1], zero_row, width_table[::-1], zero_row], 0)
@@ -350,11 +576,17 @@
     center1, inv1 = moments(first)
     scaled1 = (first - center1) * inv1
     normed1 = (scaled1 * gain1 + shift1).astype(BF16)
+    normed1, spread_rest = lax.optimization_barrier((normed1, spread_rest))
+    weight_proj = lax.all_gather(spread_rest[:head], "col", axis=0, tiled=True)
+    weight_fc1 = lax.all_gather(spread_rest[head : head + hidden], "col", axis=0, tiled=True)
+    weight_fc2 = lax.all_gather(spread_rest[head + hidden :], "col", axis=0, tiled=True)
     bias = jnp.stack([bias_qv[:, 0], jnp.zeros_like(bias_qv[:, 0]), bias_qv[:, 1]], 1)
-    qkv = mm_nt(weight_qkv.reshape(cols * 3 * head, model), normed1)
+    qkv = mm_nt(weight_qkv, normed1)
     qkv = (qkv.reshape(cols, 3 * head, width) + bias.reshape(cols, 3 * head, 1)).astype(BF16)
     qkv = lax.all_to_all(qkv, "col", 0, 0, tiled=True)
+    qkv, weight_fc1 = lax.optimization_barrier((qkv, weight_fc1))
     merged, exact, stat = attention(qkv, table)
+    merged, weight_proj, weight_fc2 = lax.optimization_barrier((merged, weight_proj, weight_fc2))
     merged = lax.all_to_all(merged, "col", 0, 0, tiled=True).reshape(cols * head, width)
 
     def contract_rows(left, right):
@@ -366,12 +598,13 @@
     def sum_tokens(values):
         return lax.psum_scatter(values.astype(BF16), "row", scatter_dimension=0, tiled=True)
 
-    projected = sum_tokens(contract_rows(merged, weight_proj)).astype(F32)
-    middle = tokens_of_row(residual).astype(F32) + (projected + bias_proj)
-    center2, inv2 = moments(middle)
-    scaled2 = (middle - center2) * inv2
-    normed2 = (scaled2 * gain2 + shift2).astype(BF16)
-    normed2 = lax.all_gather(normed2, "row", axis=0, tiled=True)
+    own_shape = (own, model)
+    vec2 = jnp.stack([gain2, shift2, bias_proj])
+    normed2, middle = row_mix(
+        forward_finish, "middle_and_norm2", 1, merged, weight_proj,
+        (vec2, tokens_of_row(residual)), [jax.ShapeDtypeStruct(own_shape, F32)], True,
+    )
+    normed2 = normed2.reshape(width, model)
     preact = mm_nt(normed2, weight_fc1) + bias_fc1
     activated, gelu_back = jax.vjp(partial(jax.nn.gelu, approximate=False), preact)
     activated = activated.astype(BF16)
@@ -382,16 +615,12 @@
 
     act_grad = mm_nt(cotangent, weight_fc2)
     preact_grad = gelu_back(act_grad)[0].astype(BF16)
-    normed2_grad = sum_tokens(mm(preact_grad, weight_fc1)).astype(F32)
-    scaled_grad = normed2_grad * gain2
-    middle_grad = tokens_of_row(cotangent).astype(F32) + inv2 * (
-        scaled_grad
-        - jnp.mean(scaled_grad, -1, keepdims=True)
-        - scaled2 * jnp.mean(scaled_grad * scaled2, -1, keepdims=True)
-    )
-    branch_grad = lax.all_gather(middle_grad.astype(BF16), "row", axis=0, tiled=True)
-    middle_own = middle_grad.reshape(own, rows, part).transpose(1, 0, 2)
-    middle_own = lax.all_to_all(middle_own, "row", 0, 0, tiled=True).reshape(width, part)
+    own_and_sums = [jax.ShapeDtypeStruct(own_shape, F32), jax.ShapeDtypeStruct((3, model), F32)]
+    branch_grad, middle_grad, sums2 = row_mix(
+        backward_finish, "middle_grad", 2, preact_grad, weight_fc1,
+        (vec2, middle, tokens_of_row(cotangent)), own_and_sums, False,
+    )
+    branch_grad = branch_grad.reshape(width, model)
 
     merged_grad = mm_nt(weight_proj, branch_grad).astype(BF16).reshape(cols, head, width)
     merged_grad = lax.all_to_all(merged_grad, "col", 0, 0, tiled=True)
@@ -399,25 +628,19 @@
     bias_grad = jnp.sum(qkv_grad, (0, 2), dtype=F32).reshape(3, head)
     qkv_grad = lax.all_to_all(qkv_grad, "col", 0, 0, tiled=True).reshape(cols * 3 * head, width)
 
-    normed1_grad = contract_rows(qkv_grad, weight_qkv.reshape(cols * 3 * head, model))
-    gain1_part = jnp.sum(normed1_grad * scaled1, 0)
-    shift1_part = jnp.sum(normed1_grad, 0)
-    scaled_grad = normed1_grad * gain1
-    means = lax.psum(
-        jnp.stack([jnp.sum(scaled_grad, -1), jnp.sum(scaled_grad * scaled1, -1)]), "row"
-    ) / model
-    by_row = normed1_grad.astype(BF16).reshape(width, rows, part).transpose(1, 0, 2)
-    normed1_own = lax.psum_scatter(by_row, "row", scatter_dimension=0, tiled=False).astype(F32)
-    scaled1_own = (patches[0].astype(F32) - center1) * inv1
-    input_grad = middle_own + inv1 * (
-        normed1_own * norm1_gain - means[0][:, None] - scaled1_own * means[1][:, None]
+    input_grad, _, sums1 = row_mix(
+        last_finish, "patches_grad", 3, qkv_grad, weight_qkv,
+        (gain1[None], tokens_of_row(residual), middle_grad), own_and_sums, True, True,
     )
 
     def weight_back(values):
         values = lax.psum_scatter(values.astype(BF16), "col", scatter_dimension=0, tiled=False)
-        values = lax.psum(values, "batch")
         values = values.reshape(-1, rows, part).transpose(1, 0, 2)
-        return lax.all_to_all(values, "row", 0, 0, tiled=True).astype(F32)
+        values = lax.all_to_all(values, "row", 0, 0, tiled=True)
+        if lax.axis_size("batch") != 2:
+            return lax.psum(values, "batch").astype(F32)
+        other = lax.ppermute(values, "batch", [(0, 1), (1, 0)])
+        return values.astype(F32) + other.astype(F32)
 
     fc2_grad = contract_rows(activated, cotangent).reshape(cols, hidden, model)
     fc2_grad = weight_back(fc2_grad).reshape(rows * hidden, part)
@@ -429,29 +652,36 @@
     qkv_weight_grad = weight_back(qkv_weight_grad).reshape(rows, 3, head, part)
     qkv_weight_grad = qkv_weight_grad.transpose(3, 1, 0, 2).reshape(part, 3, rows * head)
 
-    everywhere = ("batch", "row", "col")
     fc1_bias_part = jnp.sum(preact_grad, 0, dtype=F32).reshape(cols, 1, hidden)
     fc1_bias_part = lax.dynamic_update_slice(
         jnp.zeros((cols, rows, hidden), F32), fc1_bias_part, (0, row, 0)
     )
-    fc2_bias_part = jnp.sum(out_grad[0], 0, dtype=F32)
-    fc2_bias_grad = lax.psum(fc2_bias_part, ("batch", "col"))
-    gain2_grad, shift2_grad, proj_bias_grad, fc1_bias_grad = lax.psum(
-        (
-            jnp.sum(normed2_grad * scaled2, 0),
-            jnp.sum(normed2_grad, 0),
-            jnp.sum(tokens_of_row(branch_grad), 0, dtype=F32),
-            fc1_bias_part,
-        ),
-        everywhere,
+    fc2_bias_part = lax.dynamic_update_slice(
+        jnp.zeros((rows, part), F32), jnp.sum(out_grad[0], 0, dtype=F32)[None], (row, 0)
     )
     bias_part = lax.dynamic_update_slice(
         jnp.zeros((cols, 2, rows, head), F32),
         jnp.stack([bias_grad[0], bias_grad[2]])[None, :, None],
         (col, 0, row, 0),
     )
-    table_grad, bias_total = lax.psum((table_grad, bias_part), everywhere)
-    gain1_grad, shift1_grad = lax.psum((gain1_part, shift1_part), everywhere)
+    pieces = [
+        table_grad,
+        bias_part,
+        fc1_bias_part,
+        fc2_bias_part,
+        sums2,
+        sums1[:2],
+    ]
+    flat = jnp.concatenate([piece.reshape(-1) for piece in pieces]).reshape(-1, 128)
+    flat = sum_everywhere(flat).reshape(-1)
+    sums = []
+    for piece in pieces:
+        sums.append(flat[: piece.size].reshape(piece.shape))
+        flat = flat[piece.size :]
+    (
+        table_grad, bias_total, fc1_bias_grad, fc2_bias_grad,
+        (gain2_grad, shift2_grad, proj_bias_grad), (gain1_grad, shift1_grad),
+    ) = sums
 
     def features_of_row(values):
         return lax.dynamic_slice_in_dim(values, row * part, part, 0)
@@ -471,7 +701,7 @@
         fc1_grad,
         lax.dynamic_index_in_dim(fc1_bias_grad, col, 0, keepdims=False).reshape(rows * hidden),
         fc2_grad,
-        fc2_bias_grad,
+        lax.dynamic_index_in_dim(fc2_bias_grad, row, 0, keepdims=False),
         table_grad[:side][::-1],
         table_grad[2 * GRID : 2 * GRID + side][::-1],
     )

time: 1190 us -> 809 us (0.68)
  waiting for transfers between devices: 626 us -> 115 us
  Pallas kernels: 126 us -> 257 us
  matrix products: 89.6 us -> 60.9 us
  other arithmetic: 24.1 us -> 39.7 us
    all_gather x5 -> x3, waiting for transfers between devices: 193 us -> 7.61 us  [the longest x1 7.59 us: shards(): weight_qkv = lax.all_gather(spread_qkv, 'col', axis=0, tiled=True)]
    psum x2 -> x0, waiting for transfers between devices: 142 us -> none  [the longest x1 125 us: shards(): table_grad, bias_total = lax.psum((table_grad, bias_part), everywhere)]
    pallas_call x0 -> x4, Pallas kernels: none -> 133 us  [the longest x3 105 us: row_mix(): pl.pallas_call(partial(row_mix_kernel, finish, len(extra), 1 + len(out_sh...]
    psum x3 -> x0, blocking collectives: 82.4 us -> none  [the longest x1 57.4 us: shards(): table_grad, bias_total = lax.psum((table_grad, bias_part), everywhere)]
    all_gather x1, blocking collectives: 29.7 us -> 108 us  [shards(): weight_proj = lax.all_gather(spread_rest[:head], 'col', axis=0, tiled=True)]
    reduce_scatter x3 -> x1, waiting for transfers between devices: 76.8 us -> 0.01 us  [sum_tokens(): lax.psum_scatter(values.astype(BF16), 'row', scatter_dimension=0, tiled=T...]
    reduce_scatter x4, waiting for transfers between devices: 59.4 us -> 0.04 us  [weight_back(): lax.psum_scatter(values.astype(BF16), 'col', scatter_dimension=0, tiled=F...]
    all_to_all x6 -> x4, waiting for transfers between devices: 69.1 us -> 25.3 us  [weight_back(): values = lax.all_to_all(values, 'row', 0, 0, tiled=True)]
  transfers between devices with their start and end apart: 28 -> 24, of which waited for: 18 -> 11; matrix products, arithmetic and copies ran while one was open for 12% -> 16% of each run, Pallas kernels for 11% -> 23%
where the time goes in v2:
time: 809 us; the launch traced here: 799 us
  Pallas kernels  257 us (32%)
  blocking collectives  190 us (23%)
  waiting for transfers between devices  115 us (14%)
  local copies, waits for them, and re-layouts  69.7 us (9%)
  matrix products  60.9 us (8%)
  starting transfers between devices  49.9 us (6%)
  other arithmetic  39.7 us (5%)
  between operations  15.6 us (2%)
    all_gather x1, blocking collectives, shards(): weight_proj = lax.all_gather(spread_rest[:head], 'col', axis=0, tiled=True)  108 us
    pallas_call x3, Pallas kernels, row_mix(): pl.pallas_call(partial(row_mix_kernel, finish, len(extra), 1 + len(out_sh...  105 us
    all_to_all x1, blocking collectives, shards(): lax.all_to_all(qkv_grad, 'col', 0, 0, tiled=True)  63 us
    pallas_call x1, Pallas kernels, attention_back(): pl.pallas_call(attend_back_kernel, grid=(tokens // QUERIES,), in_specs=[p...  62.7 us
    pallas_call x1, Pallas kernels, attention(): pl.pallas_call(attend_kernel, grid=(tokens // QUERIES,), in_specs=[part_s...  62.2 us
    dot_general x4, matrix products, mm_nt(): lax.dot_general(left, right, (((1,), (1,)), ((), ())), preferred_element_...  34.1 us
    pallas_call x1, Pallas kernels, sum_everywhere(): pl.pallas_call(partial(sum_kernel, axes), out_shape=jax.ShapeDtypeStruct(...  27.8 us
    all_to_all x2, waiting for transfers between devices, spread_rows(): moved = lax.all_to_all(values, 'row', 0, 0, tiled=True)  26.9 us
  transfers between devices with their start and end apart: 24, of which 11 were waited for; matrix products, arithmetic and copies ran while one was open for 16% of the time, Pallas kernels for 23%

profile of v2, /device:TPU:8, one launch (start us, length us, event | category | flops | bytes accessed | tf_op | source)
XLA Modules:
  0.0 798.8 jit_solution(9155167276790943438)
XLA Ops:
  20.0 9.8 %all-to-all-done = bf16[4,240,320]{1,2,0:T(8,128)(2,1)} async-done(((bf16[4,240,320]{1,2,0:T(8,128)(2,1)}), bf16[4,240,320]{1,2,0:T(8,128)(2,1)}, u32[]{:S(2)}, u32[]{:S(2)}) %all-to-all-start) | async-done | bytes 614432 | tf_op jit(solution)/shard_map/all_to_all | solution.py:539
  32.1 5.4 all-gather.3
  49.0 17.1 %all-to-all-done.1 = bf16[4,720,320]{1,2,0:T(8,128)(2,1)S(1)} async-done(((bf16[4,720,320]{1,2,0:T(8,128)(2,1)}), bf16[4,720,320]{1,2,0:T(8,128)(2,1)S(1)}, u32[]{:S(2)}, u32[]{:S(2)}) %all-to-all-start.1) | async-done | bytes 1843232 | tf_op jit(solution)/shard_map/all_to_all | solution.py:539
  72.4 13.7 %all-gather.4 = f32[4,1,1920]{2,1,0:T(1,128)S(1)} all-gather(f32[1,1,1920]{2,1,0:T(1,128)S(1)} %reshape.251), channel_id=3, replica_groups=mesh['batch'=2,'row'=4,'col'=4] {'col'}, dimensions={0}, use_global_device_ids=true | all-gather | bytes 38400 | tf_op jit(solution)/shard_map/all_gather | solution.py:549
  86.5 7.6 all-gather.11.cloned.1.call-done.weight_ref
  94.0 5.2 fusion.53
  100.8 5.9 all-to-all-start.2
  107.7 108.4 %all_gather.33.weight_ref = bf16[320,1280]{1,0:T(8,128)(2,1)} all-gather(bf16[80,1280]{1,0:T(8,128)(2,1)S(1)} %slice-done), channel_id=1, replica_groups=mesh['batch'=2,'row'=4,'col'=4] {'col'}, dimensions={0}, use_global_device_ids=true | all-gather | bytes 1024000 | tf_op jit(solution)/shard_map/all_gather | solution.py:580
  216.1 62.2 %attend.1 = (bf16[4,80,1024]{2,1,0:T(8,128)(2,1)}, f32[4,80,1024]{2,1,0:T(8,128)S(1)}, f32[4,8,1024]{2,1,0:T(8,128)S(1)}) custom-call(bf16[4,240,1024]{2,1,0:T(8,128)(2,1)S(1)} %all-to-all-done.2.q_ref.k_ref.v_ref, bf16[4,240,1024]{2,1,0:T(8,128)(2,1)S(1)} %all-to-all-done.2.q_ref.k_ref.v_ref, bf16[4,240,1024]{2,1,0:T(8,128)(2,1)S(1)} %all-to-all-done.2.q_ref.k_ref.v_ref, ...), custom_call_target="tpu_custom_call" | custom-call | flops 17179869184 | bytes 3932160 | tf_op jit(solution)/shard_map/attend/pallas_call | solution.py:386
  280.1 5.8 all-to-all-start.3
  287.5 19.9 %all-gather.19.cloned.1.call-done = bf16[1,1024,1280]{1,2,0:T(8,128)(2,1)} async-done(((bf16[1,1024,320]{1,2,0:T(8,128)(2,1)}), bf16[1,1024,1280]{1,2,0:T(8,128)(2,1)}) %all-gather.19.cloned.1.call-update) | async-done | bytes 2621456 | tf_op jit(solution)/shard_map/all_gather | solution.py:536
  311.6 34.6 %middle_and_norm2.1 = (bf16[4,256,1280]{2,1,0:T(8,128)(2,1)S(1)}, f32[256,1280]{1,0:T(8,128)S(1)}) custom-call(bf16[320,1024]{1,0:T(8,128)(2,1)S(1)} %bitcast.217, bf16[320,1280]{1,0:T(8,128)(2,1)S(1)} %copy-done.1, f32[3,1280]{1,0:T(4,128)S(1)} %slice.132.refs_0_, bf16[256,1280]{1,0:T(8,128)(2,1)S(1)} %bitcast.215), custom_call_target="tpu_custom_call" | custom-call | flops 838860800 | bytes 5242880 | tf_op jit(solution)/shard_map/middle_and_norm2/pallas_call | solution.py:358
  347.7 5.7 fusion.54
  353.4 19.7 %convert_reduce_fusion.1 = (f32[1280]{0:T(1024)}, bf16[1024,1280]{1,0:T(8,128)(2,1)}, f32[1024,1280]{1,0:T(8,128)}, f32[1280,1024]{0,1:T(8,128)}) fusion(f32[1024,1280]{1,0:T(8,128)S(1)} %fusion.54, f32[1280]{0:T(1024)S(1)} %add.118, bf16[1280,1280]{1,0:T(8,128)(2,1)S(1)} %copy-done.42, bf16[1,1024,1280]{1,2,0:T(8,128)(2,1)S(1)} %copy-done.26), kind=kOutput, calls=%fused_computation.48 | convolution fusion | flops 3453745920 | bytes 24258560 | tf_op jit(solution)/shard_map/dot_general | solution.py:31
  373.1 38.2 %middle_grad.1 = (bf16[4,256,1280]{2,1,0:T(8,128)(2,1)S(1)}, f32[256,1280]{1,0:T(8,128)S(1)}, f32[3,1280]{1,0:T(4,128)S(1)}) custom-call(bf16[1024,1280]{1,0:T(8,128)(2,1)} %get-tuple-element.142.left_ref, bf16[1280,1280]{1,0:T(8,128)(2,1)} %all-gather.13.cloned.1.call-done.weight_ref, f32[3,1280]{1,0:T(4,128)S(1)} %slice.132.refs_0_, ...), custom_call_target="tpu_custom_call" | custom-call | flops 3355443200 | bytes 5242880 | tf_op jit(solution)/shard_map/middle_grad/pallas_call | solution.py:358
  415.9 15.2 %fusion.12 = bf16[1280,1024]{0,1:T(8,128)(2,1)} fusion(f32[1280,1024]{0,1:T(8,128)} %get-tuple-element.161, f32[1024,1280]{1,0:T(8,128)} %copy-done.19, f32[1280]{0:T(1024)S(1)} %add.118), kind=kLoop, calls=%fused_computation.17 | loop fusion | flops 95682560 | bytes 13112320 | tf_op jit(solution)/shard_map/convert_element_type | solution.py:617
  431.1 4.5 copy.171
  435.6 7.8 convolution_convert_fusion.1
  443.5 4.9 multiply_convert_fusion
  448.4 5.1 convolution_convert_fusion
  457.2 5.2 all-to-all-start.5
  462.3 7.9 convolution_convert_fusion.2
  470.3 23.0 %all-to-all-done.5.grad_ref = bf16[4,80,1024]{2,1,0:T(8,128)(2,1)S(1)} async-done(((bf16[4,80,1024]{2,1,0:T(8,128)(2,1)}), bf16[4,80,1024]{2,1,0:T(8,128)(2,1)S(1)}, u32[]{:S(2)}, u32[]{:S(2)}) %all-to-all-start.5) | async-done | bytes 655392 | tf_op jit(solution)/shard_map/all_to_all | solution.py:626
  497.4 62.7 %attend_back.1 = (bf16[4,240,1024]{2,1,0:T(8,128)(2,1)S(1)}, f32[256,80]{1,0:T(8,128)S(1)}) custom-call(bf16[4,240,1024]{2,1,0:T(8,128)(2,1)} %copy-done, bf16[4,240,1024]{2,1,0:T(8,128)(2,1)} %copy-done, bf16[4,240,1024]{2,1,0:T(8,128)(2,1)} %copy-done, bf16[256,80]{1,0:T(8,128)(2,1)S(1)} %copy.154.tab_ref, ...), custom_call_target="tpu_custom_call" | custom-call | flops 42949672960 | bytes 7864320 | tf_op jit(solution)/shard_map/attend_back/pallas_call | solution.py:416
  560.1 63.0 %all_to_all.55 = bf16[4,240,1024]{2,1,0:T(8,128)(2,1)S(1)} all-to-all(bf16[4,240,1024]{2,1,0:T(8,128)(2,1)S(1)} %get-tuple-element.52), channel_id=1, replica_groups=mesh['batch'=2,'row'=4,'col'=4] {'col'}, dimensions={0} | all-to-all | bytes 3932160 | tf_op jit(solution)/shard_map/all_to_all | solution.py:629
  643.1 4.3 all-to-all-start.9
  649.6 11.5 %all-to-all-done.9 = bf16[4,320,320]{2,1,0:T(8,128)(2,1)} async-done(((bf16[4,320,320]{2,1,0:T(8,128)(2,1)}), bf16[4,320,320]{2,1,0:T(8,128)(2,1)}, u32[]{:S(2)}, u32[]{:S(2)}) %all-to-all-start.9) | async-done | bytes 819232 | tf_op jit(solution)/shard_map/all_to_all | solution.py:639
  661.2 4.2 all-to-all-start.10
  669.3 9.9 %all-to-all-done.10 = bf16[4,320,320]{1,2,0:T(8,128)(2,1)} async-done(((bf16[4,320,320]{1,2,0:T(8,128)(2,1)}), bf16[4,320,320]{1,2,0:T(8,128)(2,1)}, u32[]{:S(2)}, u32[]{:S(2)}) %all-to-all-start.10) | async-done | bytes 819232 | tf_op jit(solution)/shard_map/all_to_all | solution.py:639
  687.7 31.8 %patches_grad.1 = (f32[1024,320]{1,0:T(8,128)S(1)}, f32[256,1280]{1,0:T(8,128)}, f32[3,1280]{1,0:T(4,128)S(1)}) custom-call(bf16[960,1024]{1,0:T(8,128)(2,1)} %bitcast.234, bf16[960,1280]{1,0:T(8,128)(2,1)} %all-gather.11.cloned.1.call-done.weight_ref, f32[1,1280]{1,0:T(1,128)S(1)} %get-tuple-element.154.refs_0_, bf16[256,1280]{1,0:T(8,128)(2,1)S(1)} %bitcast.216, ...), custom_call_target="tpu_custom_call" | custom-call | flops 2516582400 | bytes 5242880 | tf_op jit(solution)/shard_map/patches_grad/pallas_call | solution.py:358
  719.6 27.8 %sum_everywhere.1 = f32[280,128]{1,0:T(8,128)S(1)} custom-call(f32[280,128]{1,0:T(8,128)S(1)} %bitcast.219), custom_call_target="tpu_custom_call" | custom-call | tf_op jit(solution)/shard_map/sum_everywhere/pallas_call | solution.py:487
  780.0 8.0 collective-permute-done
  (259 shorter events, 127.3 us)
Async XLA Ops:
  7.2 34.7 %all-gather.17.cloned.1.call-start = ((), (), s32[]{:S(2)}) async-start(), calls=%async_computation.24 | async-start | bytes 3276800 | tf_op jit(solution)/shard_map/all_gather | solution.py:536
  10.7 19.1 %all-to-all-start = ((bf16[4,240,320]{1,2,0:T(8,128)(2,1)}), bf16[4,240,320]{1,2,0:T(8,128)(2,1)}, u32[]{:S(2)}, u32[]{:S(2)}) async-start(bf16[4,240,320]{1,2,0:T(8,128)(2,1)} %copy.150), calls=%async_computation | async-start | bytes 1310720 | tf_op jit(solution)/shard_map/all_to_all | solution.py:539
  14.8 79.2 %all-gather.11.cloned.1.call-start = ((), (), s32[]{:S(2)}) async-start(), calls=%async_computation.16 | async-start | bytes 3072000 | tf_op jit(solution)/shard_map/all_gather | solution.py:570
  38.2 27.9 %all-to-all-start.1 = ((bf16[4,720,320]{1,2,0:T(8,128)(2,1)}), bf16[4,720,320]{1,2,0:T(8,128)(2,1)S(1)}, u32[]{:S(2)}, u32[]{:S(2)}) async-start(bf16[4,720,320]{1,2,0:T(8,128)(2,1)} %pad_maximum_fusion), calls=%async_computation.1 | async-start | bytes 3932160 | tf_op jit(solution)/shard_map/all_to_all | solution.py:539
  41.8 174.3 %all-gather.13.cloned.1.call-start = ((), (), s32[]{:S(2)}) async-start(), calls=%async_computation.17 | async-start | bytes 4096000 | tf_op jit(solution)/shard_map/all_gather | solution.py:581
  70.4 209.6 %all-gather.15.cloned.1.call-start = ((), (), s32[]{:S(2)}) async-start(), calls=%async_computation.18 | async-start | bytes 4096000 | tf_op jit(solution)/shard_map/all_gather | solution.py:582
  100.8 115.3 %all-to-all-start.2 = ((bf16[4,240,1024]{2,1,0:T(8,128)(2,1)}), bf16[4,240,1024]{2,1,0:T(8,128)(2,1)S(1)}, u32[]{:S(2)}, u32[]{:S(2)}) async-start(bf16[4,240,1024]{2,1,0:T(8,128)(2,1)} %add_convert_fusion), calls=%async_computation.2 | async-start | bytes 3932160 | tf_op jit(solution)/shard_map/all_to_all | solution.py:586
  106.7 200.8 %all-gather.19.cloned.1.call-start = ((), (), s32[]{:S(2)}) async-start(), calls=%async_computation.25 | async-start | bytes 3276800 | tf_op jit(solution)/shard_map/all_gather | solution.py:536
  216.1 62.2 %copy-start = (bf16[4,240,1024]{2,1,0:T(8,128)(2,1)}, bf16[4,240,1024]{2,1,0:T(8,128)(2,1)S(1)}, u32[]{:S(2)}) copy-start(bf16[4,240,1024]{2,1,0:T(8,128)(2,1)S(1)} %all-to-all-done.2.q_ref.k_ref.v_ref) | copy-start | bytes 5898244
  280.1 30.5 %copy-start.1 = (bf16[320,1280]{1,0:T(8,128)(2,1)S(1)}, bf16[320,1280]{1,0:T(8,128)(2,1)}, u32[]{:S(2)}) copy-start(bf16[320,1280]{1,0:T(8,128)(2,1)} %all_gather.33.weight_ref) | copy-start | bytes 2457604
  280.1 29.6 %all-to-all-start.3 = ((bf16[4,80,1024]{2,1,0:T(8,128)(2,1)}), bf16[4,80,1024]{2,1,0:T(8,128)(2,1)S(1)}, u32[]{:S(2)}, u32[]{:S(2)}) async-start(bf16[4,80,1024]{2,1,0:T(8,128)(2,1)} %get-tuple-element.43), calls=%async_computation.3 | async-start | bytes 1310720 | tf_op jit(solution)/shard_map/all_to_all | solution.py:590
  285.9 345.8 %reduce-scatter.10.cloned.1.call-start = ((), (), s32[]{:S(2)}) async-start(), calls=%async_computation.21 | async-start | bytes 1024000 | tf_op jit(solution)/shard_map/reduce_scatter | solution.py:637
  287.5 65.8 %copy-start.2 = (bf16[1,256,1280]{2,1,0:T(8,128)(2,1)}, bf16[1,256,1280]{2,1,0:T(8,128)(2,1)S(1)}, u32[]{:S(2)}) copy-start(bf16[1,256,1280]{2,1,0:T(8,128)(2,1)S(1)} %copy.157) | copy-start | bytes 1966084
  353.4 19.7 %copy-start.19 = (f32[1024,1280]{1,0:T(8,128)}, f32[1024,1280]{1,0:T(8,128)S(1)}, u32[]{:S(2)}) copy-start(f32[1024,1280]{1,0:T(8,128)S(1)} %fusion.54) | copy-start | bytes 15728644
  373.1 40.8 %copy-start.6 = (bf16[4,80,1024]{2,1,0:T(8,128)(2,1)S(1)}, bf16[4,80,1024]{2,1,0:T(8,128)(2,1)}, u32[]{:S(2)}) copy-start(bf16[4,80,1024]{2,1,0:T(8,128)(2,1)} %copy-done.4) | copy-start | bytes 1966084
  415.9 221.7 %reduce-scatter.12.cloned.1.call-start = ((), (), s32[]{:S(2)}) async-start(), calls=%async_computation.22 | async-start | bytes 4096000 | tf_op jit(solution)/shard_map/reduce_scatter | solution.py:637
  443.4 204.0 %reduce-scatter.14.cloned.1.call-start = ((), (), s32[]{:S(2)}) async-start(), calls=%async_computation.23 | async-start | bytes 4096000 | tf_op jit(solution)/shard_map/reduce_scatter | solution.py:637
  457.2 36.1 %all-to-all-start.5 = ((bf16[4,80,1024]{2,1,0:T(8,128)(2,1)}), bf16[4,80,1024]{2,1,0:T(8,128)(2,1)S(1)}, u32[]{:S(2)}, u32[]{:S(2)}) async-start(bf16[4,80,1024]{2,1,0:T(8,128)(2,1)} %bitcast.25), calls=%async_computation.6 | async-start | bytes 1310720 | tf_op jit(solution)/shard_map/all_to_all | solution.py:626
  462.3 204.7 %reduce-scatter.6.cloned.1.call-start = ((), (), s32[]{:S(2)}) async-start(), calls=%async_computation.19 | async-start | bytes 3276800 | tf_op jit(solution)/shard_map/reduce_scatter | solution.py:599
  470.2 281.1 %reduce-scatter.8.cloned.1.call-start = ((), (), s32[]{:S(2)}) async-start(), calls=%async_computation.20 | async-start | bytes 3072000 | tf_op jit(solution)/shard_map/reduce_scatter | solution.py:637
  497.4 127.0 %copy-start.20 = (bf16[1024,1280]{0,1:T(8,128)(2,1)S(1)}, bf16[1024,1280]{0,1:T(8,128)(2,1)}, u32[]{:S(2)}) copy-start(bf16[1024,1280]{0,1:T(8,128)(2,1)} %fusion.6) | copy-start | bytes 7864324
  633.7 31.7 %copy-start.29 = (f32[3840]{0:T(1024)S(1)}, f32[3840]{0:T(1024)}, u32[]{:S(2)}) copy-start(f32[3840]{0:T(1024)} %reshape.230) | copy-start | bytes 46084
  633.7 33.3 %copy-start.30 = (f32[1280]{0:T(1024)S(1)}, f32[1280]{0:T(1024)}, u32[]{:S(2)}) copy-start(f32[1280]{0:T(1024)} %get-tuple-element.138) | copy-start | bytes 15364
  633.7 9.4 %all-to-all-start.8 = ((bf16[4,80,320]{2,1,0:T(8,128)(2,1)}), bf16[4,80,320]{2,1,0:T(8,128)(2,1)S(1)}, u32[]{:S(2)}, u32[]{:S(2)}) async-start(bf16[4,80,320]{2,1,0:T(8,128)(2,1)} %bitcast.212), calls=%async_computation.11 | async-start | bytes 491520 | tf_op jit(solution)/shard_map/all_to_all | solution.py:639
  643.1 18.1 %all-to-all-start.9 = ((bf16[4,320,320]{2,1,0:T(8,128)(2,1)}), bf16[4,320,320]{2,1,0:T(8,128)(2,1)}, u32[]{:S(2)}, u32[]{:S(2)}) async-start(bf16[4,320,320]{2,1,0:T(8,128)(2,1)} %bitcast.211), calls=%async_computation.13 | async-start | bytes 1966080 | tf_op jit(solution)/shard_map/all_to_all | solution.py:639
  661.2 18.1 %all-to-all-start.10 = ((bf16[4,320,320]{1,2,0:T(8,128)(2,1)}), bf16[4,320,320]{1,2,0:T(8,128)(2,1)}, u32[]{:S(2)}, u32[]{:S(2)}) async-start(bf16[4,320,320]{1,2,0:T(8,128)(2,1)} %bitcast.56), calls=%async_computation.15 | async-start | bytes 1966080 | tf_op jit(solution)/shard_map/all_to_all | solution.py:639
  665.4 17.5 %collective-permute-start.1 = (bf16[4,80,320]{2,1,0:T(8,128)(2,1)S(1)}, bf16[4,80,320]{2,1,0:T(8,128)(2,1)S(1)}, u32[]{:S(2)}, u32[]{:S(2)}) collective-permute-start(bf16[4,80,320]{2,1,0:T(8,128)(2,1)S(1)} %all-to-all-done.8), channel_id=1, source_target_pairs={{0,16},{16,0},{1,17},{17,1},{2,18},{18,2},{3,19},{19,3},{4,20},{20... | collective-permute-start | bytes 614408 | tf_op jit(solution)/shard_map/ppermute | solution.py:642
  679.2 74.3 %all-to-all-start.4 = ((bf16[4,256,320]{1,2,0:T(8,128)(2,1)}), bf16[4,256,320]{1,2,0:T(8,128)(2,1)S(1)}, u32[]{:S(2)}, u32[]{:S(2)}) async-start(bf16[4,256,320]{1,2,0:T(8,128)(2,1)} %bitcast.19), calls=%async_computation.5 | async-start | bytes 1310720 | tf_op jit(solution)/shard_map/all_to_all | solution.py:614
  683.8 84.5 %collective-permute-start.2 = (bf16[4,320,320]{2,1,0:T(8,128)(2,1)}, bf16[4,320,320]{2,1,0:T(8,128)(2,1)}, u32[]{:S(2)}, u32[]{:S(2)}) collective-permute-start(bf16[4,320,320]{2,1,0:T(8,128)(2,1)} %all-to-all-done.9), channel_id=1, source_target_pairs={{0,16},{16,0},{1,17},{17,1},{2,18},{18,2},{3,19},{19,3},{4,20},{20... | collective-permute-start | bytes 2457608 | tf_op jit(solution)/shard_map/ppermute | solution.py:642
  749.8 24.9 %collective-permute-start.3 = (bf16[4,320,320]{1,2,0:T(8,128)(2,1)}, bf16[4,320,320]{1,2,0:T(8,128)(2,1)}, u32[]{:S(2)}, u32[]{:S(2)}) collective-permute-start(bf16[4,320,320]{1,2,0:T(8,128)(2,1)} %all-to-all-done.10), channel_id=1, source_target_pairs={{0,16},{16,0},{1,17},{17,1},{2,18},{18,2},{3,19},{19,3},{4,20},{20... | collective-permute-start | bytes 2457608 | tf_op jit(solution)/shard_map/ppermute | solution.py:642
  753.5 14.2 %all-to-all-start.7 = ((bf16[4,240,320]{1,2,0:T(8,128)(2,1)}), bf16[4,240,320]{1,2,0:T(8,128)(2,1)S(1)}, u32[]{:S(2)}, u32[]{:S(2)}) async-start(bf16[4,240,320]{1,2,0:T(8,128)(2,1)} %bitcast.30), calls=%async_computation.9 | async-start | bytes 1310720 | tf_op jit(solution)/shard_map/all_to_all | solution.py:639
  767.7 20.2 %collective-permute-start = (bf16[4,240,320]{1,2,0:T(8,128)(2,1)S(1)}, bf16[4,240,320]{1,2,0:T(8,128)(2,1)}, u32[]{:S(2)}, u32[]{:S(2)}) collective-permute-start(bf16[4,240,320]{1,2,0:T(8,128)(2,1)S(1)} %all-to-all-done.7), channel_id=1, source_target_pairs={{0,16},{16,0},{1,17},{17,1},{2,18},{18,2},{3,19},{19,3},{4,20},{20... | collective-permute-start | bytes 1843208 | tf_op jit(solution)/shard_map/ppermute | solution.py:642
  (36 other events, 239.2 us)
Sparse Core Ops, SparseCore 0:
  9.6 31.2 all-gather.16
  43.0 50.9 all-gather.10
  96.2 113.2 all-gather.12
  211.4 67.9 all-gather.14
  280.8 26.5 all-gather.18
  416.0 21.8 reduce-scatter.9
  443.5 75.9 reduce-scatter.11
  521.9 74.6 reduce-scatter.13
  599.1 36.9 reduce-scatter.5
  638.3 48.5 reduce-scatter.7

commit v3 on v2

v3 whole, which is shorter than its diff:
```python
import math
from functools import partial

import jax
import jax.numpy as jnp
from jax import lax
from jax.experimental import pallas as pl
from jax.experimental.pallas import tpu as pltpu
from jax.sharding import PartitionSpec as P

D = 1280
HEAD_DIM = 80
GRID = 64
EPSILON = 1e-06

LINES = 4
QUERIES = LINES * GRID
KEYS = 512
LOG2E = math.log2(math.e)
SCALE = HEAD_DIM**-0.5
BF16 = jnp.bfloat16
F32 = jnp.float32
MESH = pl.DeviceIdType.MESH


def mm(left, right):
    return jnp.dot(left, right, preferred_element_type=F32)


def mm_nt(left, right):
    return lax.dot_general(left, right, (((1,), (1,)), ((), ())), preferred_element_type=F32)


def split(values, parts):
    terms = []
    for _ in range(parts):
        term = values.astype(BF16)
        terms.append(term)
        values = values - term.astype(F32)
    return terms


def skew(values, shift):
    n = values.shape[1]
    for bit, rows in ((32, 96), (16, 80), (8, 72)):
        take = jnp.broadcast_to(shift, (rows, n)) & bit
        values = jnp.where(take != 0, values[bit : bit + rows], values[:rows])
    for bit in (4, 2, 1):
        take = jnp.broadcast_to(shift, values.shape) & bit
        values = jnp.where(take != 0, pltpu.roll(values, values.shape[0] - bit, 0), values)
    return values[:GRID]


def unskew(values, shift):
    n = values.shape[1]
    values = jnp.concatenate([values, jnp.zeros((8, n), F32)], 0)
    for bit in (1, 2, 4):
        take = jnp.broadcast_to(shift, values.shape) & bit
        values = jnp.where(take != 0, pltpu.roll(values, bit, 0), values)
    for bit in (8, 16, 32):
        zeros = jnp.zeros((bit, n), F32)
        take = jnp.broadcast_to(shift, (values.shape[0] + bit, n)) & bit
        values = jnp.where(
            take != 0,
            jnp.concatenate([zeros, values], 0),
            jnp.concatenate([values, zeros], 0),
        )
    return values


def token_shifts(step):
    lane = lax.broadcasted_iota(jnp.int32, (1, QUERIES), 1)
    return (GRID - 1) - (step * LINES + lane // GRID), (GRID - 1) - lane % GRID


def query_columns(q, tab, step, tail):
    shift_rows, shift_cols = token_shifts(step)
    both = mm(tab, q)
    rel_rows = skew(both[: 2 * GRID], shift_rows)
    rel_cols = skew(both[2 * GRID :], shift_cols)
    rel = jnp.concatenate([rel_rows, rel_cols], 0) * (1.0 / SCALE)
    return jnp.concatenate([rel.astype(BF16), q, tail], 0)


def col_peer(step):
    me = lax.axis_index("col")
    odd, high = step % 2, step // 2
    return lax.rem(me + odd - 2 * odd * lax.rem(me, 2) + 2 * high, 4)


def col_barrier():
    barrier = pltpu.get_barrier_semaphore()
    for step in range(1, 4):
        pl.semaphore_signal(barrier, device_id={"col": col_peer(step)}, device_id_type=MESH)
    pl.semaphore_wait(barrier, 3)


def col_copy(source, target, sems, kind, step):
    return pltpu.make_async_remote_copy(
        src_ref=source,
        dst_ref=target,
        send_sem=sems.at[0, kind, step],
        recv_sem=sems.at[1, kind, step],
        device_id={"col": col_peer(step)},
        device_id_type=MESH,
    )


def attend_kernel(
    given_ref, tab_ref, proj_ref, merged_ref, qkv_ref, exact_ref, stat_ref, proj_all_ref,
    kaug, columns, acc, top, total, box, sems,
):
    me = lax.axis_index("col")
    width = given_ref.shape[2]
    blocks = width // QUERIES
    col_barrier()

    def part_copy(step):
        return col_copy(given_ref.at[col_peer(step)], qkv_ref.at[me], sems, 0, step)

    def merged_copy(step):
        return col_copy(box.at[col_peer(step)], merged_ref.at[me], sems, 1, step)

    def proj_copy(step):
        return col_copy(proj_ref, proj_all_ref.at[me], sems, 2, step)

    for step in range(1, 4):
        part_copy(step).start()
    for step in range(1, 4):
        proj_copy(step).start()
    qkv_ref[me] = given_ref[me]
    proj_all_ref[me] = proj_ref[...]

    pad = jnp.zeros((128 - HEAD_DIM, width), F32)
    token = lax.broadcasted_iota(jnp.int32, (width, 2 * GRID), 0)
    lane = lax.broadcasted_iota(jnp.int32, (width, 2 * GRID), 1)
    tail = jnp.zeros((128 - HEAD_DIM, QUERIES), BF16)
    factor = SCALE * LOG2E

    def prepare(part):
        at = token + part * width
        hot = jnp.where(jnp.where(lane < GRID, at // GRID, at % GRID + GRID) == lane, 1.0, 0.0)
        key = qkv_ref[part, HEAD_DIM : 2 * HEAD_DIM]
        kaug[part, :, 0:128] = hot.astype(BF16)
        kaug[part, :, 128:256] = jnp.concatenate([key.astype(F32), pad], 0).T.astype(BF16)
        for block in range(blocks):
            at = slice(block * QUERIES, (block + 1) * QUERIES)
            columns[part, :, at] = query_columns(
                qkv_ref[part, 0:HEAD_DIM, at], tab_ref[...], part * blocks + block, tail
            )
        acc[part] = jnp.zeros((HEAD_DIM, width), F32)
        top[part] = jnp.full((8, width), -1e30, F32)
        total[part] = jnp.zeros((8, width), F32)

    def finish(part):
        whole, best = total[part, 0:1], top[part, 0:1]
        result = acc[part] * (1.0 / whole)
        exact_ref[part] = result
        box[part] = result.astype(BF16)
        stat_ref[part] = jnp.broadcast_to(best + jnp.log2(whole) * (1.0 / factor), (8, width))

    def pair(turn, carry):
        newest = (turn + 15) // 16 + (turn + 12) // 16 + (turn + 7) // 16
        place = turn - newest * newest
        q_step = jnp.where(place < newest, place, newest)
        k_step = jnp.where(place < newest, newest, place - newest)
        q_part, k_part = col_peer(q_step), col_peer(k_step)

        @pl.when(jnp.logical_and(place == 0, newest > 0))
        def _():
            part_copy(newest).wait_recv()

        @pl.when(place == 0)
        def _():
            prepare(col_peer(newest))

        for block in range(blocks):
            at = slice(block * QUERIES, (block + 1) * QUERIES)
            best, whole, result = top[q_part, 0:1, at], total[q_part, 0:1, at], acc[q_part, :, at]
            for start in range(0, width, KEYS):
                keys = slice(start, start + KEYS)
                scores = mm(kaug[k_part, keys], columns[q_part, :, at])
                new_best = jnp.maximum(best, jnp.max(scores, 0, keepdims=True))
                weights = jnp.exp2((scores - new_best) * factor)
                keep = jnp.exp2((best - new_best) * factor)
                whole = whole * keep + jnp.sum(weights, 0, keepdims=True)
                value = qkv_ref[k_part, 2 * HEAD_DIM : 3 * HEAD_DIM, keys]
                result = result * keep + mm(value, weights.astype(BF16))
                best = new_best
            top[q_part, :, at] = jnp.broadcast_to(best, (8, QUERIES))
            total[q_part, :, at] = jnp.broadcast_to(whole, (8, QUERIES))
            acc[q_part, :, at] = result

        @pl.when(jnp.logical_and(turn >= 9, jnp.logical_or(place < 3, turn == 15)))
        def _():
            finish(q_part)

        @pl.when(jnp.logical_and(turn >= 9, jnp.logical_or(jnp.logical_and(turn > 9, place < 3), turn == 15)))
        def _():
            merged_copy(q_step).start()

        return carry

    lax.fori_loop(0, 16, pair, 0)
    merged_ref[me] = box[me]
    for step in range(1, 4):
        part_copy(step).wait_send()
        proj_copy(step).wait()
        merged_copy(step).wait()


GRADS, QUERY_OUT, KEY_OUT, PROJ_OUT = range(4)
KEY_ROWS = slice(HEAD_DIM, 3 * HEAD_DIM)


def attend_back_kernel(
    images, qkv_ref, tab_ref, tab_t_ref, given_ref, exact_ref, stat_ref, proj_ref, fc2_ref,
    out_ref, tab_grad_ref, bias_out, proj_out, fc2_out,
    bias_ref, proj_rows, proj_box, grads, kaug, kaug_t, vaug, key_sum, value_sum, spread, columns,
    grad_columns, grad_rows, q_rows, box, sems, *weight_parts,
):
    me = lax.axis_index("col")
    width = qkv_ref.shape[2]
    blocks = width // QUERIES
    meet(
        ("row", row_peers()),
        ("col", [col_peer(step) for step in range(1, 4)]),
        ("batch", image_peers(images) if images == 2 else ()),
    )

    def write_proj(place, values):
        proj_out[place] = values

    def write_fc2(place, values):
        fc2_out[place] = values

    fc2 = weight_steps(fc2_ref, images, weight_parts[:4], write_fc2)
    proj = weight_steps(proj_rows, images, weight_parts[4:], write_proj)

    def grad_copy(step):
        return col_copy(given_ref.at[col_peer(step)], grads.at[me], sems, GRADS, step)

    def query_copy(step):
        at = col_peer(step)
        return col_copy(box.at[at, 0:HEAD_DIM], out_ref.at[me, 0:HEAD_DIM], sems, QUERY_OUT, step)

    def key_copy(step):
        at = col_peer(step)
        return col_copy(box.at[at, KEY_ROWS], out_ref.at[me, KEY_ROWS], sems, KEY_OUT, step)

    def proj_copy(step):
        return col_copy(proj_ref.at[col_peer(step)], proj_box.at[me], sems, PROJ_OUT, step)

    for step in range(1, 4):
        grad_copy(step).start()
    for step in range(1, 4):
        proj_copy(step).start()
    next(fc2)
    grads[me] = given_ref[me]
    proj_box[me] = proj_ref[me]

    tail_row = lax.broadcasted_iota(jnp.int32, (128 - HEAD_DIM, width), 0)
    pad = jnp.where(tail_row < 3, 1.0, 0.0)
    token = lax.broadcasted_iota(jnp.int32, (width, 2 * GRID), 0)
    lane = lax.broadcasted_iota(jnp.int32, (width, 2 * GRID), 1)

    def fill(part, carry):
        at = token + part * width
        hot = jnp.where(jnp.where(lane < GRID, at // GRID, at % GRID + GRID) == lane, 1.0, 0.0)
        key, value = qkv_ref[part, HEAD_DIM : 2 * HEAD_DIM], qkv_ref[part, 2 * HEAD_DIM : 3 * HEAD_DIM]
        kaug[part, :, 0:128] = hot.astype(BF16)
        kaug[part, :, 128:256] = jnp.concatenate([key.astype(F32), pad], 0).T.astype(BF16)
        vaug[part] = jnp.concatenate([value.astype(F32), pad], 0).T.astype(BF16)
        kaug_t[part, 0:128] = hot.T.astype(BF16)
        kaug_t[part, 128:208] = key
        kaug_t[part, 208:256] = jnp.zeros((48, width), BF16)
        return carry

    lax.fori_loop(0, 4, fill, 0)
    key_sum[...] = jnp.zeros_like(key_sum)
    value_sum[...] = jnp.zeros_like(value_sum)
    spread[...] = jnp.zeros_like(spread)
    tab_grad_ref[...] = jnp.zeros_like(tab_grad_ref)
    bias_ref[...] = jnp.zeros_like(bias_ref)

    block_row = lax.broadcasted_iota(jnp.int32, (128 - HEAD_DIM, QUERIES), 0)

    def tail(row):
        out = jnp.zeros((128 - HEAD_DIM, QUERIES), F32)
        for place, term in enumerate(split(row, 3)):
            out = jnp.where(block_row == place, term.astype(F32), out)
        return out.astype(BF16)

    zero_tail = jnp.zeros((128 - HEAD_DIM, QUERIES), F32)

    def prepare(part):
        for block in range(blocks):
            at = slice(block * QUERIES, (block + 1) * QUERIES)
            q, grad = qkv_ref[part, 0:HEAD_DIM, at], grads[part, :, at]
            inner = jnp.sum(grad.astype(F32) * exact_ref[part, :, at], 0, keepdims=True)
            columns[part, :, at] = query_columns(
                q, tab_ref[...], part * blocks + block, tail(-stat_ref[part, 0:1, at])
            )
            grad_columns[part, :, at] = jnp.concatenate([grad, tail(-inner)], 0)
            grad_rows[part, at] = jnp.concatenate([grad.astype(F32), zero_tail], 0).T.astype(BF16)
            q_rows[part, at] = jnp.concatenate([q.astype(F32), zero_tail], 0).T.astype(BF16)

    def add_bias(first, values):
        total = jnp.sum(values.astype(F32), 1, keepdims=True)
        bias_ref[first : first + values.shape[0]] += jnp.broadcast_to(total, (values.shape[0], 128))

    def finish_queries(part):
        for block in range(blocks):
            at = slice(block * QUERIES, (block + 1) * QUERIES)
            rows, cols = token_shifts(part * blocks + block)
            lifted = jnp.concatenate(
                [unskew(spread[part, 0:GRID, at], rows), unskew(spread[part, GRID : 2 * GRID, at], cols)], 0
            )
            high, low = split(lifted, 2)
            query_grad = spread[part, 128 : 128 + HEAD_DIM, at] * SCALE
            query_grad = query_grad + (mm(tab_t_ref[...], high) + mm(tab_t_ref[...], low))
            q = qkv_ref[part, 0:HEAD_DIM, at]
            tab_grad_ref[...] += mm_nt(q, high) + mm_nt(q, low)
            box[part, 0:HEAD_DIM, at] = query_grad.astype(BF16)
        add_bias(0, box[part, 0:HEAD_DIM])

    def finish_keys(part):
        key_grad = (key_sum[part] * SCALE).T[:HEAD_DIM].astype(BF16)
        value_grad = value_sum[part].T[:HEAD_DIM].astype(BF16)
        box[part, HEAD_DIM : 2 * HEAD_DIM] = key_grad
        box[part, 2 * HEAD_DIM : 3 * HEAD_DIM] = value_grad
        add_bias(HEAD_DIM, key_grad)
        add_bias(2 * HEAD_DIM, value_grad)

    def pair(turn, carry):
        outer, inner = turn // 4, turn % 4
        q_step = inner + (outer // 3) * (3 - 2 * inner)
        k_step = 3 - outer
        q_part, k_part = col_peer(q_step), col_peer(k_step)

        @pl.when(jnp.logical_and(turn > 0, turn < 4))
        def _():
            grad_copy(q_step).wait_recv()

        @pl.when(turn < 4)
        def _():
            prepare(q_part)

        for block in range(blocks):
            at = slice(block * QUERIES, (block + 1) * QUERIES)
            total = None
            for start in range(0, width, KEYS):
                keys = slice(start, start + KEYS)
                weights = jnp.exp2(mm(kaug[k_part, keys], columns[q_part, :, at]) * (SCALE * LOG2E))
                score_grad = (weights * mm(vaug[k_part, keys], grad_columns[q_part, :, at])).astype(BF16)
                value_sum[k_part, keys] += mm(weights.astype(BF16), grad_rows[q_part, at])
                key_sum[k_part, keys] += mm(score_grad, q_rows[q_part, at])
                result = mm(kaug_t[k_part, :, keys], score_grad)
                total = result if total is None else total + result
            spread[q_part, :, at] += total

        @pl.when(inner == 3)
        def _():
            finish_keys(k_part)

        @pl.when(jnp.logical_and(inner == 3, outer < 3))
        def _():
            key_copy(k_step).start()

        @pl.when(outer == 3)
        def _():
            finish_queries(q_part)

        @pl.when(jnp.logical_and(outer == 3, inner < 3))
        def _():
            query_copy(q_step).start()

        return carry

    lax.fori_loop(0, 4, pair, 0)
    for step in range(1, 4):
        proj_copy(step).wait()
    total = proj_box[0].astype(F32)
    for source in range(1, 4):
        total = total + proj_box[source].astype(F32)
    proj_rows[...] = total.astype(BF16)
    next(fc2)
    next(proj)
    lax.fori_loop(4, 8, pair, 0)
    next(proj)
    next(fc2, None)
    lax.fori_loop(8, 16, pair, 0)
    next(proj, None)
    out_ref[me] = box[me]
    for step in range(1, 4):
        grad_copy(step).wait_send()
        query_copy(step).wait()
        key_copy(step).wait()
    bias_out[0:1] = bias_ref[0:128].T[0:1]
    bias_out[1:2] = bias_ref[2 * HEAD_DIM : 2 * HEAD_DIM + 128].T[0:1]


MIX_SUBS = 2
TO_NEAR, PASS_ON, TO_FAR, OUT_NEAR, OUT_FAR, OUT_ON = range(6)


def normal(values):
    center, inv = moments(values)
    return (values - center) * inv, inv


def normal_back(grad, scaled, inv, gain):
    grad = grad * gain
    return inv * (
        grad
        - jnp.mean(grad, -1, keepdims=True)
        - scaled * jnp.mean(grad * scaled, -1, keepdims=True)
    )


def add_sums(sums_ref, piece, terms):
    for place, term in enumerate(terms):
        total = jnp.sum(term, 0, keepdims=True)
        if piece:
            total = total + sums_ref[place : place + 1]
        sums_ref[place : place + 1] = total


def forward_finish(total, piece, rows, vec_ref, first_ref, out_refs):
    middle = first_ref[rows].astype(F32) + (total + vec_ref[2:3])
    out_refs[0][rows] = middle
    scaled, _ = normal(middle)
    return (scaled * vec_ref[0:1] + vec_ref[1:2]).astype(BF16)


def backward_finish(total, piece, rows, vec_ref, first_ref, add_ref, out_refs):
    scaled, inv = normal(first_ref[rows].astype(F32))
    result = add_ref[rows].astype(F32) + normal_back(total, scaled, inv, vec_ref[0:1])
    branch = result.astype(BF16)
    out_refs[0][rows] = result
    add_sums(out_refs[1], piece, (total * scaled, total, branch.astype(F32)))
    return branch


def last_finish(total, piece, rows, vec_ref, first_ref, add_ref, out_refs):
    scaled, inv = normal(first_ref[rows].astype(F32))
    add_sums(out_refs[1], piece, (total * scaled, total))
    return add_ref[rows] + normal_back(total, scaled, inv, vec_ref[0:1])


def row_peers():
    me = lax.axis_index("row")
    near = me + 1 - 2 * lax.rem(me, 2)
    return near, lax.rem(me + 2, 4), lax.rem(near + 2, 4)


def meet(*groups):
    barrier = pltpu.get_barrier_semaphore()
    for axis, peers in groups:
        for peer in peers:
            pl.semaphore_signal(barrier, device_id={axis: peer}, device_id_type=MESH)
    pl.semaphore_wait(barrier, sum(len(peers) for _, peers in groups))


def row_mix_steps(left_ref, weight_ref, gathered, finish, left_t, to_features, scratch):
    far_keep, own_keep, out_box, in_box, sems, *more = scratch
    own = far_keep.shape[0]
    sub = own // MIX_SUBS
    me = lax.axis_index("row")
    near, far, diag = row_peers()
    started = []

    def send(source, target, kind, piece, peer):
        copy = pltpu.make_async_remote_copy(
            src_ref=source,
            dst_ref=target,
            send_sem=sems.at[0, kind, piece],
            recv_sem=sems.at[1, kind, piece],
            device_id={"row": peer},
            device_id_type=MESH,
        )
        copy.start()
        started.append(copy)
        return copy

    def product(owner, piece):
        at = pl.ds(pl.multiple_of(owner * own + piece * sub, sub), sub)
        if left_t:
            left = left_ref[:, at].astype(F32).T.astype(BF16)
        else:
            left = left_ref[at, :]
        return mm(left, weight_ref[...])

    pieces = [slice(piece * sub, (piece + 1) * sub) for piece in range(MIX_SUBS)]
    passed, direct, summed = [], [], []
    for piece, rows in enumerate(pieces):
        out_box[0, rows] = product(diag, piece).astype(BF16)
        passed.append(send(out_box.at[0, rows], in_box.at[0, rows], PASS_ON, piece, near))
        far_keep[rows] = product(far, piece)
    yield
    for piece, rows in enumerate(pieces):
        out_box[1, rows] = product(near, piece).astype(BF16)
        direct.append(send(out_box.at[1, rows], in_box.at[1, rows], TO_NEAR, piece, near))
        passed[piece].wait_recv()
        out_box[2, rows] = (far_keep[rows] + in_box[0, rows].astype(F32)).astype(BF16)
        summed.append(send(out_box.at[2, rows], in_box.at[2, rows], TO_FAR, piece, far))
    yield
    for piece, rows in enumerate(pieces):
        own_keep[rows] = product(me, piece)
    yield
    near_out, far_out, on_out = [], [], []
    for piece, rows in enumerate(pieces):
        direct[piece].wait_recv()
        summed[piece].wait_recv()
        total = own_keep[rows] + in_box[1, rows].astype(F32) + in_box[2, rows].astype(F32)
        result = finish(total, piece, rows)
        if to_features:
            boxes, arrived = more
            part = gathered.shape[1]
            for place in range(4):
                boxes[place, rows] = result[:, place * part : (place + 1) * part].astype(BF16)
            arrived[me, rows] = boxes[me, rows]
            for kind, peer, copies in (
                (OUT_NEAR, near, near_out), (OUT_FAR, far, far_out), (OUT_ON, diag, on_out)
            ):
                copies.append(send(boxes.at[peer, rows], arrived.at[me, rows], kind, piece, peer))
        else:
            gathered[me, rows] = result
            near_out.append(send(gathered.at[me, rows], gathered.at[me, rows], OUT_NEAR, piece, near))
            far_out.append(send(gathered.at[me, rows], gathered.at[me, rows], OUT_FAR, piece, far))
    yield
    for piece, rows in enumerate(pieces):
        far_out[piece].wait_recv()
        if not to_features:
            on_out.append(send(gathered.at[far, rows], gathered.at[far, rows], OUT_ON, piece, near))
    for copy in near_out + on_out:
        copy.wait_recv()
    if to_features:
        boxes, arrived = more
        for source in range(4):
            gathered[source * own : (source + 1) * own, :] = arrived[source].astype(gathered.dtype)
    for copy in started:
        copy.wait_send()


def mix_scratch(own, model, to_features):
    boxes = [pltpu.VMEM((4, own, model // 4), BF16)] * 2 if to_features else []
    return [
        pltpu.VMEM((own, model), F32),
        pltpu.VMEM((own, model), F32),
        pltpu.VMEM((3, own, model), BF16),
        pltpu.VMEM((3, own, model), BF16),
        pltpu.SemaphoreType.DMA((2, 6, MIX_SUBS)),
        *boxes,
    ]


def row_mix_kernel(finish, extra, outs, left_t, left_ref, weight_ref, *refs):
    extra_refs, refs = refs[:extra], refs[extra:]
    (gathered, *out_refs), scratch = refs[:outs], refs[outs:]
    near, far, _ = row_peers()
    meet(("row", (near, far)))

    def last(total, piece, rows):
        return finish(total, piece, rows, *extra_refs, out_refs)

    for _ in row_mix_steps(left_ref, weight_ref, gathered, last, left_t, False, scratch):
        pass


def row_mix(finish, name, number, left, weight, extra, out_shapes, left_t):
    tokens = left.shape[1] if left_t else left.shape[0]
    model = weight.shape[1]
    own = tokens // 4
    vmem = pl.BlockSpec(memory_space=pltpu.VMEM)
    return pl.pallas_call(
        partial(row_mix_kernel, finish, len(extra), 1 + len(out_shapes), left_t),
        out_shape=[jax.ShapeDtypeStruct((4, own, model), BF16), *out_shapes],
        in_specs=[vmem] * (2 + len(extra)),
        out_specs=[vmem] * (1 + len(out_shapes)),
        scratch_shapes=mix_scratch(own, model, False),
        compiler_params=pltpu.CompilerParams(
            collective_id=number, has_side_effects=True, vmem_limit_bytes=48 << 20
        ),
        cost_estimate=pl.CostEstimate(
            flops=2 * tokens * weight.size, bytes_accessed=16 * own * model, transcendentals=0
        ),
        name=name,
    )(left, weight, *extra)


def weight_steps(values_ref, images, scratch, write):
    boxes, arrived, other, sems = scratch
    me, part = lax.axis_index("row"), boxes.shape[2]
    for place in range(4):
        boxes[place] = values_ref[:, place * part : (place + 1) * part]
    arrived[me] = boxes[me]
    copies = []
    for order, peer in enumerate(row_peers()):
        copy = pltpu.make_async_remote_copy(
            src_ref=boxes.at[peer],
            dst_ref=arrived.at[me],
            send_sem=sems.at[0, order],
            recv_sem=sems.at[1, order],
            device_id={"row": peer},
            device_id_type=MESH,
        )
        copy.start()
        copies.append(copy)
    yield
    for copy in copies:
        copy.wait()
    if images == 2:
        swap = pltpu.make_async_remote_copy(
            src_ref=arrived,
            dst_ref=other,
            send_sem=sems.at[0, 3],
            recv_sem=sems.at[1, 3],
            device_id={"batch": 1 - lax.axis_index("batch")},
            device_id_type=MESH,
        )
        swap.start()
        yield
        swap.wait()
        for place in range(4):
            write(place, arrived[place].astype(F32) + other[place].astype(F32))
    else:
        yield
        for place in range(4):
            write(place, arrived[place].astype(F32))


def weight_scratch(n, part):
    return [*[pltpu.VMEM((4, n, part), BF16)] * 3, pltpu.SemaphoreType.DMA((2, 4))]


def image_peers(images):
    me = lax.axis_index("batch")
    return [lax.rem(me + step, images) for step in range(1, images)]


def sum_steps(total, axes, scratch):
    *slots, sends, recvs = scratch
    for order, (name, size) in enumerate(axes):
        me, slot = lax.axis_index(name), slots[order]
        slot[me] = total[...]
        copies = []
        for step in range(1, size):
            copy = pltpu.make_async_remote_copy(
                src_ref=total,
                dst_ref=slot.at[me],
                send_sem=sends.at[order, step],
                recv_sem=recvs.at[order, step],
                device_id={name: lax.rem(me + step, size)},
                device_id_type=MESH,
            )
            copy.start()
            copies.append(copy)
        yield
        for copy in copies:
            copy.wait()
        whole = slot[0]
        for source in range(1, size):
            whole = whole + slot[source]
        total[...] = whole


def sum_scratch(rows, axes):
    most = max(size for _, size in axes)
    return [
        *[pltpu.VMEM((size, rows, 128), F32) for _, size in axes],
        *[pltpu.SemaphoreType.DMA((len(axes), most))] * 2,
    ]


def column_steps(grad_ref, normed_ref, box, arrived, own_keep, out, sems):
    me = lax.axis_index("col")
    copies = []
    for step in range(1, 4):
        box[step - 1] = mm(grad_ref[col_peer(step)], normed_ref[...]).astype(BF16)
        copy = col_copy(box.at[step - 1], arrived.at[step - 1], sems, 0, step)
        copy.start()
        copies.append(copy)
    yield
    own_keep[...] = mm(grad_ref[me], normed_ref[...])
    yield
    for copy in copies:
        copy.wait()
    total = own_keep[...]
    for step in range(3):
        total = total + arrived[step].astype(F32)
    out[...] = total.astype(BF16)


EARLY_ROWS, TABLE_ROWS, BIAS_ROWS, LAST_ROWS = 80, 160, 32, 24


def tail_kernel(
    axes,
    qkv_grad_ref, grads_ref, weight_qkv_ref, normed1_ref, first_ref, middle_grad_ref, gain_ref,
    activated_ref, weight_fc2_ref, middle_ref, bias_fc2_ref, fc1_ref, early_ref, table_ref, bias_ref,
    patches_out, block_out, qkv_out, fc1_out, small,
    *scratch,
):
    sums1, qkv_rows, box, arrived, own_keep, col_sems, *scratch = scratch
    mix1, mix2 = scratch[:7], scratch[7:14]
    qkv_scratch, fc1_scratch, sum_parts = scratch[14:18], scratch[18:22], scratch[22:]
    row, col = lax.axis_index("row"), lax.axis_index("col")
    images = dict(axes)["batch"]
    meet(
        ("row", row_peers()),
        ("col", [col_peer(step) for step in range(1, 4)]),
        ("batch", image_peers(images)),
    )

    def finish1(total, piece, rows):
        return last_finish(total, piece, rows, gain_ref, first_ref, middle_grad_ref, (None, sums1))

    def finish2(total, piece, rows):
        return middle_ref[rows] + (total + bias_fc2_ref[0:1])

    def write_fc1(place, values):
        n = values.shape[0]
        fc1_out[place * n : (place + 1) * n] = values

    head_grads = []

    def write_qkv(place, values):
        head_grads.append(values)

    qkv_sum = column_steps(grads_ref, normed1_ref, box, arrived, own_keep, qkv_rows, col_sems)
    patches = row_mix_steps(qkv_grad_ref, weight_qkv_ref, patches_out, finish1, True, True, mix1)
    block = row_mix_steps(activated_ref, weight_fc2_ref, block_out, finish2, False, True, mix2)
    fc1 = weight_steps(fc1_ref, images, fc1_scratch, write_fc1)
    qkv = weight_steps(qkv_rows, images, qkv_scratch, write_qkv)
    sums = sum_steps(small, axes, sum_parts)

    def go(*steps):
        for step in steps:
            next(step, None)

    go(qkv_sum, patches, block, fc1)
    go(patches, block, patches, block, qkv_sum)
    go(patches)

    small[0:EARLY_ROWS] = early_ref[...]
    at = EARLY_ROWS
    for half in range(2):
        small[at : at + TABLE_ROWS // 2] = table_ref[:, half * 128 : (half + 1) * 128]
        at += TABLE_ROWS // 2
    place = lax.broadcasted_iota(jnp.int32, (BIAS_ROWS, 128), 0) - 2 * (col * 4 + row)
    small[at : at + BIAS_ROWS] = jnp.where(
        place == 0, bias_ref[0:1], jnp.where(place == 1, bias_ref[1:2], 0.0)
    )
    at += BIAS_ROWS
    lines = sums1.shape[1] // 128
    last = [sums1[i : i + 1, j * 128 : (j + 1) * 128] for i in range(2) for j in range(lines)]
    spare = jnp.zeros((LAST_ROWS - len(last), 128), F32)
    small[at : at + LAST_ROWS] = jnp.concatenate([*last, spare], 0)

    go(sums, block, fc1, qkv_sum, qkv)
    go(sums, patches, block, qkv, sums, fc1, sums, qkv)
    count = len(head_grads)
    for kind in range(3):
        rows = slice(kind * HEAD_DIM, (kind + 1) * HEAD_DIM)
        qkv_out[kind] = jnp.concatenate([values[rows] for values in head_grads], 0).T


def tail(
    qkv_grad, weight_qkv, normed1, first, middle_grad, gain, activated, weight_fc2, middle, bias_fc2, fc1, early, table, bias
):
    cols, n, tokens = qkv_grad.shape
    model = weight_qkv.shape[1]
    own, part = tokens // 4, model // 4
    axes = tuple((name, lax.axis_size(name)) for name in ("row", "batch", "col"))
    small_rows = EARLY_ROWS + TABLE_ROWS + BIAS_ROWS + LAST_ROWS
    vmem = pl.BlockSpec(memory_space=pltpu.VMEM)
    return pl.pallas_call(
        partial(tail_kernel, axes),
        in_specs=[vmem] * 15,
        out_specs=[vmem] * 5,
        out_shape=[
            jax.ShapeDtypeStruct((tokens, part), F32),
            jax.ShapeDtypeStruct((tokens, part), BF16),
            jax.ShapeDtypeStruct((3, part, 4 * HEAD_DIM), F32),
            jax.ShapeDtypeStruct((4 * fc1.shape[0], part), F32),
            jax.ShapeDtypeStruct((small_rows, 128), F32),
        ],
        scratch_shapes=[
            pltpu.VMEM((3, model), F32),
            pltpu.VMEM((n, model), BF16),
            pltpu.VMEM((3, n, model), BF16),
            pltpu.VMEM((3, n, model), BF16),
            pltpu.VMEM((n, model), F32),
            pltpu.SemaphoreType.DMA((2, 1, 4)),
            *mix_scratch(own, model, True),
            *mix_scratch(own, model, True),
            *weight_scratch(n, part),
            *weight_scratch(fc1.shape[0], part),
            *sum_scratch(small_rows, axes),
        ],
        compiler_params=pltpu.CompilerParams(
            collective_id=3, has_side_effects=True, vmem_limit_bytes=60 << 20
        ),
        name="tail",
    )(
        qkv_grad.reshape(cols * n, tokens), qkv_grad, weight_qkv, normed1, first, middle_grad, gain,
        activated, weight_fc2, middle, bias_fc2, fc1, early, table, bias,
    )


HIDDEN = 256
ROWS = 256


def hidden_kernel(x_ref, w1_ref, bias_ref, cot_ref, w2_ref, act_ref, grad_ref, bias_grad_ref):
    total = None
    for start in range(0, x_ref.shape[0], ROWS):
        rows = slice(start, start + ROWS)
        preact = mm_nt(x_ref[rows], w1_ref[...]) + bias_ref[...]
        act_grad = mm_nt(cot_ref[rows], w2_ref[...])
        below = 0.5 + 0.5 * lax.erf(preact * (0.5**0.5))
        density = jnp.exp(preact * preact * -0.5) * ((2 * math.pi) ** -0.5)
        act_ref[rows] = (preact * below).astype(BF16)
        grad = (act_grad * (below + preact * density)).astype(BF16)
        grad_ref[rows] = grad
        part = jnp.sum(grad.astype(F32), 0, keepdims=True)
        total = part if total is None else total + part
    bias_grad_ref[...] = total


def feed_forward(x, w1, bias, cotangent, w2):
    tokens, model = x.shape
    hidden = w1.shape[0]
    step = HIDDEN if hidden % HIDDEN == 0 else hidden
    whole = pl.BlockSpec((tokens, model), lambda i: (0, 0), pipeline_mode=pl.Buffered(1))
    weight = pl.BlockSpec((step, model), lambda i: (i, 0))
    vector = pl.BlockSpec((1, step), lambda i: (0, i))
    columns = pl.BlockSpec((tokens, step), lambda i: (0, i))
    return pl.pallas_call(
        hidden_kernel,
        grid=(hidden // step,),
        in_specs=[whole, weight, vector, whole, weight],
        out_specs=[columns, columns, vector],
        out_shape=[
            jax.ShapeDtypeStruct((tokens, hidden), BF16),
            jax.ShapeDtypeStruct((tokens, hidden), BF16),
            jax.ShapeDtypeStruct((1, hidden), F32),
        ],
        compiler_params=pltpu.CompilerParams(vmem_limit_bytes=40 << 20),
        cost_estimate=pl.CostEstimate(
            flops=4 * tokens * hidden * model,
            bytes_accessed=4 * (tokens + hidden) * model + 4 * tokens * hidden,
            transcendentals=2 * tokens * hidden,
        ),
        name="feed_forward",
    )(x, w1, bias, cotangent, w2)


def attention(qkv, table, proj):
    count, _, width = qkv.shape
    tokens = count * width
    vmem = pl.BlockSpec(memory_space=pltpu.VMEM)
    return pl.pallas_call(
        attend_kernel,
        in_specs=[vmem] * 3,
        out_specs=[vmem] * 5,
        out_shape=[
            jax.ShapeDtypeStruct((count, HEAD_DIM, width), BF16),
            jax.ShapeDtypeStruct(qkv.shape, BF16),
            jax.ShapeDtypeStruct((count, HEAD_DIM, width), F32),
            jax.ShapeDtypeStruct((count, 8, width), F32),
            jax.ShapeDtypeStruct((count, *proj.shape), BF16),
        ],
        scratch_shapes=[
            pltpu.VMEM((count, width, 256), BF16),
            pltpu.VMEM((count, 256, width), BF16),
            pltpu.VMEM((count, HEAD_DIM, width), F32),
            pltpu.VMEM((count, 8, width), F32),
            pltpu.VMEM((count, 8, width), F32),
            pltpu.VMEM((count, HEAD_DIM, width), BF16),
            pltpu.SemaphoreType.DMA((2, 3, 4)),
        ],
        compiler_params=pltpu.CompilerParams(
            collective_id=5, has_side_effects=True, vmem_limit_bytes=48 << 20
        ),
        cost_estimate=pl.CostEstimate(
            flops=2 * tokens * tokens * 512,
            bytes_accessed=6 * tokens * HEAD_DIM * 2,
            transcendentals=tokens * tokens,
        ),
        name="attend",
    )(qkv, table, proj)


def attention_back(qkv, table, grad, exact, stat, proj, fc2):
    count, _, width = qkv.shape
    tokens = count * width
    images, part = lax.axis_size("batch"), fc2.shape[1] // 4
    vmem = pl.BlockSpec(memory_space=pltpu.VMEM)
    return pl.pallas_call(
        partial(attend_back_kernel, images),
        in_specs=[vmem] * 8,
        out_specs=[vmem] * 5,
        out_shape=[
            jax.ShapeDtypeStruct((count, 3 * HEAD_DIM, width), BF16),
            jax.ShapeDtypeStruct(table.shape[::-1], F32),
            jax.ShapeDtypeStruct((2, 128), F32),
            jax.ShapeDtypeStruct((4, proj.shape[1], part), F32),
            jax.ShapeDtypeStruct((4, fc2.shape[0], part), F32),
        ],
        scratch_shapes=[
            pltpu.VMEM((384, 128), F32),
            pltpu.VMEM(proj.shape[1:], BF16),
            pltpu.VMEM(proj.shape, BF16),
            pltpu.VMEM((count, HEAD_DIM, width), BF16),
            pltpu.VMEM((count, width, 256), BF16),
            pltpu.VMEM((count, 256, width), BF16),
            pltpu.VMEM((count, width, 128), BF16),
            pltpu.VMEM((count, width, 128), F32),
            pltpu.VMEM((count, width, 128), F32),
            pltpu.VMEM((count, 256, width), F32),
            pltpu.VMEM((count, 256, width), BF16),
            pltpu.VMEM((count, 128, width), BF16),
            pltpu.VMEM((count, width, 128), BF16),
            pltpu.VMEM((count, width, 128), BF16),
            pltpu.VMEM((count, 3 * HEAD_DIM, width), BF16),
            pltpu.SemaphoreType.DMA((2, 4, 4)),
            *weight_scratch(fc2.shape[0], part),
            *weight_scratch(proj.shape[1], part),
        ],
        compiler_params=pltpu.CompilerParams(
            collective_id=4, has_side_effects=True, vmem_limit_bytes=60 << 20
        ),
        cost_estimate=pl.CostEstimate(
            flops=2 * tokens * tokens * 1280,
            bytes_accessed=12 * tokens * HEAD_DIM * 2,
            transcendentals=tokens * tokens,
        ),
        name="attend_back",
    )(qkv, table, table.T, grad, exact, stat, proj, fc2)


def moments(values):
    center = jnp.mean(values, -1, keepdims=True)
    spread = jnp.mean(values * values, -1, keepdims=True)
    return center, lax.rsqrt(spread - center * center + EPSILON)


def shards(
    patches,
    qkv_weight,
    qv_bias,
    proj_weight,
    proj_bias,
    norm1_gain,
    norm1_shift,
    norm2_gain,
    norm2_shift,
    fc1_weight,
    fc1_bias,
    fc2_weight,
    fc2_bias,
    height_table,
    width_table,
    out_grad,
):
    rows, cols = lax.axis_size("row"), lax.axis_size("col")
    row, col = lax.axis_index("row"), lax.axis_index("col")
    width = patches.shape[1]
    part = patches.shape[2]
    model = part * rows
    own = width // rows
    hidden = fc1_bias.shape[0] // rows
    head = HEAD_DIM

    def over_row(values):
        return lax.all_gather(values, "row", axis=1, tiled=True)

    def spread_rows(values):
        moved = lax.all_to_all(values, "row", 0, 0, tiled=True)
        return moved.transpose(1, 0, 2).reshape(values.shape[1], model)

    images = lax.axis_size("batch")

    residual = over_row(patches[0])
    cotangent = over_row(out_grad[0])
    vectors = lax.all_gather(
        jnp.stack([norm1_gain, norm1_shift, norm2_gain, norm2_shift, proj_bias, fc2_bias]),
        "row", axis=1, tiled=True,
    )
    gain1, shift1, gain2, shift2, bias_proj, bias_fc2 = [vectors[i] for i in range(6)]
    by_col = lax.all_gather(
        jnp.concatenate([qv_bias.reshape(-1), fc1_bias]), "col", axis=0, tiled=False
    )
    bias_qv = by_col[:, : 2 * rows * head].reshape(cols, 2, rows, head)
    bias_qv = lax.dynamic_index_in_dim(bias_qv, row, 2, keepdims=False)
    bias_fc1 = by_col[:, 2 * rows * head :].reshape(cols, rows, hidden)
    bias_fc1 = lax.dynamic_index_in_dim(bias_fc1, row, 1, keepdims=False)
    bias_fc1 = bias_fc1.reshape(cols * hidden)

    local_qkv = qkv_weight.reshape(part, 3, rows, head).transpose(2, 1, 3, 0)
    local_rest = jnp.concatenate(
        [
            proj_weight.reshape(rows, head, part),
            fc1_weight.T.reshape(rows, hidden, part),
            fc2_weight.reshape(rows, hidden, part),
        ],
        1,
    )
    spread_qkv = spread_rows(local_qkv.reshape(rows, 3 * head, part))
    local_rest, spread_qkv = lax.optimization_barrier((local_rest, spread_qkv))
    spread_rest = spread_rows(local_rest)
    weight_qkv = lax.all_gather(spread_qkv, "col", axis=0, tiled=True)

    zero_row = jnp.zeros((1, head), BF16)
    table = jnp.concatenate([height_table[::-1], zero_row, width_table[::-1], zero_row], 0)

    first = residual.astype(F32)
    center1, inv1 = moments(first)
    scaled1 = (first - center1) * inv1
    normed1 = (scaled1 * gain1 + shift1).astype(BF16)
    normed1, spread_rest = lax.optimization_barrier((normed1, spread_rest))
    bias = jnp.stack([bias_qv[:, 0], jnp.zeros_like(bias_qv[:, 0]), bias_qv[:, 1]], 1)
    qkv = mm_nt(weight_qkv, normed1)
    qkv = (qkv.reshape(cols, 3 * head, width) + bias.reshape(cols, 3 * head, 1)).astype(BF16)
    qkv, spread_rest = lax.optimization_barrier((qkv, spread_rest))
    weight_fc1 = lax.all_gather(spread_rest[head : head + hidden], "col", axis=0, tiled=True)
    weight_fc2 = lax.all_gather(spread_rest[head + hidden :], "col", axis=0, tiled=True)
    merged, qkv, exact, stat, weight_proj = attention(qkv, table, spread_rest[:head])
    weight_proj = weight_proj.reshape(cols * head, model)
    merged, weight_fc1 = lax.optimization_barrier((merged, weight_fc1))
    merged = merged.reshape(cols * head, width)

    def contract_rows(left, right):
        return lax.dot_general(left, right, (((0,), (0,)), ((), ())), preferred_element_type=F32)

    def sum_columns(values):
        return lax.psum_scatter(values, "col", scatter_dimension=0, tiled=False)

    def tokens_of_row(values):
        return lax.dynamic_slice_in_dim(values, row * own, own, 0)

    def sum_tokens(values):
        return lax.psum_scatter(values.astype(BF16), "row", scatter_dimension=0, tiled=True)

    own_shape = (own, model)
    vec2 = jnp.stack([gain2, shift2, bias_proj])
    normed2, middle = row_mix(
        forward_finish, "middle_and_norm2", 1, merged, weight_proj,
        (vec2, tokens_of_row(residual)), [jax.ShapeDtypeStruct(own_shape, F32)], True,
    )
    normed2 = normed2.reshape(width, model)
    activated, preact_grad, fc1_bias_part = feed_forward(
        normed2, weight_fc1, bias_fc1[None], cotangent, weight_fc2
    )
    fc2_grad = contract_rows(activated, cotangent).astype(BF16)
    fc2_grad, preact_grad = lax.optimization_barrier((fc2_grad, preact_grad))

    own_and_sums = [jax.ShapeDtypeStruct(own_shape, F32), jax.ShapeDtypeStruct((3, model), F32)]
    branch_grad, middle_grad, sums2 = row_mix(
        backward_finish, "middle_grad", 2, preact_grad, weight_fc1,
        (vec2, middle, tokens_of_row(cotangent)), own_and_sums, False,
    )
    branch_grad = branch_grad.reshape(width, model)

    merged_grad = mm_nt(weight_proj, branch_grad).astype(BF16).reshape(cols, head, width)
    merged_grad, activated, preact_grad, normed2, branch_grad = lax.optimization_barrier(
        (merged_grad, activated, preact_grad, normed2, branch_grad)
    )
    fc1_grad = contract_rows(preact_grad, normed2).astype(BF16)
    proj_grad = mm(merged, branch_grad).astype(BF16)
    fc2_grad = sum_columns(fc2_grad.reshape(cols, hidden, model))
    early = jnp.concatenate(
        [
            lax.dynamic_update_slice(jnp.zeros((rows, cols * hidden), F32), fc1_bias_part, (row, 0)).reshape(-1),
            lax.dynamic_update_slice(
                jnp.zeros((model,), F32), jnp.sum(out_grad[0], 0, dtype=F32), (row * part,)
            ),
            sums2.reshape(-1),
        ]
    ).reshape(-1, 128)
    merged_grad, fc1_grad, proj_grad, fc2_grad, early = lax.optimization_barrier(
        (merged_grad, fc1_grad, proj_grad, fc2_grad, early)
    )
    fc1_grad = sum_columns(fc1_grad.reshape(cols, hidden, model))
    qkv_grad, table_grad, bias_grad, proj_grad, fc2_grad = attention_back(
        qkv, table, merged_grad, exact, stat, proj_grad.reshape(cols, head, model), fc2_grad
    )
    input_grad, final, qkv_weight_grad, fc1_grad, small = tail(
        qkv_grad, weight_qkv, normed1, tokens_of_row(residual), middle_grad, gain1[None],
        activated, weight_fc2, middle, bias_fc2[None], fc1_grad, early, table_grad, bias_grad,
    )

    def sum_images(values):
        return values if images == 2 else lax.psum(values.astype(BF16), "batch").astype(F32)

    fc2_grad = sum_images(fc2_grad).reshape(rows * hidden, part)
    proj_grad = sum_images(proj_grad).reshape(rows * head, part)
    fc1_grad = sum_images(fc1_grad).T
    qkv_weight_grad = sum_images(qkv_weight_grad).transpose(1, 0, 2)

    lines = model // 128
    fc1_bias_grad = small[: 4 * lines].reshape(rows, cols, hidden)
    fc1_bias_grad = lax.dynamic_index_in_dim(fc1_bias_grad, col, 1, keepdims=False).reshape(rows * hidden)
    fc2_bias_grad = small[4 * lines : 5 * lines].reshape(-1)
    gain2_grad, shift2_grad, proj_bias_grad = small[5 * lines : 8 * lines].reshape(3, model)
    at = EARLY_ROWS
    table_grad = jnp.concatenate([small[at : at + TABLE_ROWS // 2], small[at + TABLE_ROWS // 2 : at + TABLE_ROWS]], 1)
    table_grad = table_grad.T
    at += TABLE_ROWS
    bias_total = small[at : at + BIAS_ROWS].reshape(cols, rows, 2, 128)
    bias_total = lax.dynamic_index_in_dim(bias_total, col, 0, keepdims=False)[:, :, :head]
    bias_total = bias_total.transpose(1, 0, 2).reshape(2, rows * head)
    at += BIAS_ROWS
    gain1_grad, shift1_grad = small[at : at + 2 * lines].reshape(2, model)

    def features_of_row(values):
        return lax.dynamic_slice_in_dim(values, row * part, part, 0)

    side = 2 * GRID - 1
    return (
        final[None],
        input_grad[None],
        qkv_weight_grad,
        bias_total,
        proj_grad,
        features_of_row(proj_bias_grad),
        features_of_row(gain1_grad),
        features_of_row(shift1_grad),
        features_of_row(gain2_grad),
        features_of_row(shift2_grad),
        fc1_grad,
        fc1_bias_grad,
        fc2_grad,
        features_of_row(fc2_bias_grad),
        table_grad[:side][::-1],
        table_grad[2 * GRID : 2 * GRID + side][::-1],
    )


def solution(mesh):
    in_specs = (
        P("batch", "col", "row"),
        P("row", None, "col"),
        P(None, "col"),
        P("col", "row"),
        P("row"),
        P("row"),
        P("row"),
        P("row"),
        P("row"),
        P("row", "col"),
        P("col"),
        P("col", "row"),
        P("row"),
        P(),
        P(),
        P("batch", "col", "row"),
    )
    out_specs = (
        P("batch", "col", "row"),
        P("batch", "col", "row"),
        P("row", None, "col"),
        P(None, "col"),
        P("col", "row"),
        P("row"),
        P("row"),
        P("row"),
        P("row"),
        P("row"),
        P("row", "col"),
        P("col"),
        P("col", "row"),
        P("row"),
        P(),
        P(),
    )
    return jax.shard_map(shards, mesh=mesh, in_specs=in_specs, out_specs=out_specs, check_vma=False)
```

time: 809 us -> 696 us (0.86)
  Pallas kernels: 257 us -> 475 us
  blocking collectives: 190 us -> 19 us
  waiting for transfers between devices: 115 us -> 71 us
  starting transfers between devices: 49.9 us -> 9.64 us
  matrix products: 60.9 us -> 21.3 us
  other arithmetic: 39.7 us -> 9.02 us
    pallas_call x3 -> x4, Pallas kernels: 153 us -> 392 us  [the longest x1 142 us: attention_back(): pl.pallas_call(partial(attend_back_kernel, images), in_specs=[vmem] * 8,...]
    all_gather x1 -> x0, blocking collectives: 108 us -> none  [shards(): weight_proj = lax.all_gather(spread_rest[:head], 'col', axis=0, tiled=True)]
    all_to_all x1 -> x0, blocking collectives: 63 us -> none  [shards(): lax.all_to_all(qkv_grad, 'col', 0, 0, tiled=True)]
    all_to_all x8 -> x0, waiting for transfers between devices: 48.3 us -> none  [the longest x4 25.3 us: weight_back(): values = lax.all_to_all(values, 'row', 0, 0, tiled=True)]
    all_to_all x8 -> x0, starting transfers between devices: 36.6 us -> none  [the longest x4 16 us: weight_back(): values = lax.all_to_all(values, 'row', 0, 0, tiled=True)]
    dot_general x4 -> x2, matrix products: 34.1 us -> 7.32 us  [mm_nt(): lax.dot_general(left, right, (((1,), (1,)), ((), ())), preferred_element_...]
    pallas_call x3 -> x2, Pallas kernels: 105 us -> 82.8 us  [row_mix(): pl.pallas_call(partial(row_mix_kernel, finish, len(extra), 1 + len(out_sh...]
    convert_element_type x3 -> x0, other arithmetic: 21.4 us -> none  [the longest x1 15.2 us: shards(): preact_grad = gelu_back(act_grad)[0].astype(BF16)]
  transfers between devices with their start and end apart: 24 -> 9, of which waited for: 11 -> 6; matrix products, arithmetic and copies ran while one was open for 16% -> 8% of each run, Pallas kernels for 23% -> 52%
where the time goes in v3:
time: 696 us; the launch traced here: 685 us
  Pallas kernels  475 us (68%)
  waiting for transfers between devices  71 us (10%)
  local copies, waits for them, and re-layouts  64.6 us (9%)
  matrix products  21.3 us (3%)
  blocking collectives  19 us (3%)
  between operations  15.3 us (2%)
  starting transfers between devices  9.64 us (1%)
  other arithmetic  9.02 us (1%)
    pallas_call x1, Pallas kernels, attention_back(): pl.pallas_call(partial(attend_back_kernel, images), in_specs=[vmem] * 8,...  142 us
    pallas_call x1, Pallas kernels, attention(): pl.pallas_call(attend_kernel, in_specs=[vmem] * 3, out_specs=[vmem] * 5,...  133 us
    pallas_call x1, Pallas kernels, tail(): pl.pallas_call(partial(tail_kernel, axes), in_specs=[vmem] * 15, out_spec...  107 us
    pallas_call x2, Pallas kernels, row_mix(): pl.pallas_call(partial(row_mix_kernel, finish, len(extra), 1 + len(out_sh...  82.8 us
    all_to_all x2, waiting for transfers between devices, spread_rows(): moved = lax.all_to_all(values, 'row', 0, 0, tiled=True)  27.7 us
    unnamed x82, local copies, waits for them, and re-layouts  24.4 us
    all_gather x2, waiting for transfers between devices, over_row(): return lax.all_gather(values, 'row', axis=1, tiled=True)  14.4 us
  transfers between devices with their start and end apart: 9, of which 6 were waited for; matrix products, arithmetic and copies ran while one was open for 8% of the time, Pallas kernels for 52%

profile of v3, /device:TPU:8, one launch (start us, length us, event | category | flops | bytes accessed | tf_op | source)
XLA Modules:
  0.0 684.5 jit_solution(11328017776711804652)
XLA Ops:
  10.7 4.3 all-to-all-start
  17.8 2.3 pad_maximum_fusion
  20.1 10.0 %all-to-all-done = bf16[4,240,320]{1,2,0:T(8,128)(2,1)} async-done(((bf16[4,240,320]{1,2,0:T(8,128)(2,1)}), bf16[4,240,320]{1,2,0:T(8,128)(2,1)}, u32[]{:S(2)}, u32[]{:S(2)}) %all-to-all-start) | async-done | bytes 614432 | tf_op jit(solution)/shard_map/all_to_all | solution.py:981
  30.1 2.1 copy.85
  33.2 5.4 all-gather.3
  38.8 13.5 %all-gather.4 = f32[4,1,1920]{2,1,0:T(1,128)S(1)} all-gather(f32[1,1,1920]{2,1,0:T(1,128)S(1)} %reshape.195), channel_id=3, replica_groups=mesh['batch'=2,'row'=4,'col'=4] {'col'}, dimensions={0}, use_global_device_ids=true | all-gather | bytes 38400 | tf_op jit(solution)/shard_map/all_gather | solution.py:993
  53.4 4.4 all-to-all-start.1
  57.9 3.0 copy.86
  61.9 2.5 fusion.6.normed1_ref
  64.5 17.7 %all-to-all-done.1 = bf16[4,720,320]{1,2,0:T(8,128)(2,1)} async-done(((bf16[4,720,320]{1,2,0:T(8,128)(2,1)}), bf16[4,720,320]{1,2,0:T(8,128)(2,1)}, u32[]{:S(2)}, u32[]{:S(2)}) %all-to-all-start.1) | async-done | bytes 1843232 | tf_op jit(solution)/shard_map/all_to_all | solution.py:981
  82.2 11.7 %all-gather.11.cloned.1.call-done.weight_qkv_ref = bf16[960,1280]{1,0:T(8,128)(2,1)} async-done(((bf16[240,1280]{1,0:T(8,128)(2,1)}), bf16[960,1280]{1,0:T(8,128)(2,1)}) %all-gather.11.cloned.1.call-update) | async-done | bytes 2457616 | tf_op jit(solution)/shard_map/all_gather | solution.py:1014
  93.9 5.2 fusion.13
  100.6 2.9 copy.88
  107.1 14.4 %all-gather.19.cloned.1.call-done = bf16[1,1024,1280]{1,2,0:T(8,128)(2,1)} async-done(((bf16[1,1024,320]{1,2,0:T(8,128)(2,1)}), bf16[1,1024,1280]{1,2,0:T(8,128)(2,1)}) %all-gather.19.cloned.1.call-update) | async-done | bytes 2621456 | tf_op jit(solution)/shard_map/all_gather | solution.py:978
  121.5 2.2 constant_dynamic-slice_fusion
  124.0 4.7 copy.92
  129.6 133.1 %attend.1 = (bf16[4,80,1024]{2,1,0:T(8,128)(2,1)S(1)}, bf16[4,240,1024]{2,1,0:T(8,128)(2,1)S(1)}, f32[4,80,1024]{2,1,0:T(8,128)S(1)}, f32[4,8,1024]{2,1,0:T(8,128)S(1)}, bf16[4,80,1280]{2,1,0:T(8,128)(2,1)S(1)}) custom-call(bf16[4,240,1024]{2,1,0:T(8,128)(2,1)} %add_convert_fusion.given_ref, bf16[256,80]{1,0:T(8,128)(2,1)S(1)} %copy.89.tab_ref, ...), custom_call_target="tpu_custom_call" | custom-call | flops 17179869184 | bytes 3932160 | tf_op jit(solution)/shard_map/attend/pallas_call | solution.py:864
  265.1 44.4 %middle_and_norm2.1 = (bf16[4,256,1280]{2,1,0:T(8,128)(2,1)S(1)}, f32[256,1280]{1,0:T(8,128)S(1)}) custom-call(bf16[320,1024]{1,0:T(8,128)(2,1)S(1)} %bitcast.109, bf16[320,1280]{1,0:T(8,128)(2,1)S(1)} %bitcast.107, f32[3,1280]{1,0:T(4,128)S(1)} %slice.98.refs_0_, bf16[256,1280]{1,0:T(8,128)(2,1)S(1)} %bitcast.99), custom_call_target="tpu_custom_call" | custom-call | flops 838860800 | bytes 5242880 | tf_op jit(solution)/shard_map/middle_and_norm2/pallas_call | solution.py:576
  312.0 3.7 all-gather.15.cloned.1.call-done.w2_ref.weight_fc2_ref
  317.5 1.9 copy-done.7
  321.2 10.2 %feed_forward.1 = (bf16[1024,1280]{1,0:T(8,128)(2,1)S(1)}, bf16[1024,1280]{1,0:T(8,128)(2,1)S(1)}, f32[1,1280]{1,0:T(1,128)S(1)}) custom-call(bf16[1024,1280]{1,0:T(8,128)(2,1)S(1)} %bitcast.103, bf16[1280,1280]{1,0:T(8,128)(2,1)S(1)} %copy-done.7, f32[1,1280]{1,0:T(1,128)S(1)} %broadcast_in_dim_reshape.3.bias_ref, bf16[1024,1280]{1,0:T(8,128)(2,1)S(1)} %bitcast.101, ...), custom_call_target="tpu_custom_call" | custom-call | flops 6710886400 | bytes 17039360 | tf_op jit(solution)/shard_map/feed_forward/pallas_call | solution.py:840
  331.4 5.1 convolution_convert_fusion.1
  339.4 38.4 %middle_grad.1 = (bf16[4,256,1280]{2,1,0:T(8,128)(2,1)S(1)}, f32[256,1280]{1,0:T(8,128)S(1)}, f32[3,1280]{1,0:T(4,128)S(1)}) custom-call(bf16[1024,1280]{1,0:T(8,128)(2,1)} %copy-done.12, bf16[1280,1280]{1,0:T(8,128)(2,1)} %all-gather.13.cloned.1.call-done.w1_ref.weight_ref, f32[3,1280]{1,0:T(4,128)S(1)} %slice.98.refs_0_, f32[256,1280]{1,0:T(8,128)S(1)} %copy-done.4, ...), custom_call_target="tpu_custom_call" | custom-call | flops 3355443200 | bytes 5242880 | tf_op jit(solution)/shard_map/middle_grad/pallas_call | solution.py:576
  377.9 2.1 convolution_convert_fusion.3
  380.9 3.8 convolution_convert_fusion.2
  384.7 5.1 convolution_convert_fusion
  389.8 11.4 %reduce-scatter.3.cloned.1.call-done = bf16[1,320,1280]{2,1,0:T(8,128)(2,1)} async-done(((bf16[4,320,1280]{2,1,0:T(8,128)(2,1)}), bf16[1,320,1280]{2,1,0:T(8,128)(2,1)}) %reduce-scatter.3.cloned.1.call-update) | async-done | bytes 819216 | tf_op jit(solution)/shard_map/reduce_scatter | solution.py:1039
  401.2 141.9 %attend_back.1 = (bf16[4,240,1024]{2,1,0:T(8,128)(2,1)}, f32[80,256]{1,0:T(8,128)}, f32[2,128]{1,0:T(2,128)}, f32[4,80,320]{2,1,0:T(8,128)}, f32[4,320,320]{2,1,0:T(8,128)}) custom-call(bf16[4,240,1024]{2,1,0:T(8,128)(2,1)} %copy-done.14, bf16[256,80]{1,0:T(8,128)(2,1)} %copy-done.6, bf16[80,256]{1,0:T(8,128)(2,1)} %get-tuple-element.180.tab_t_ref, ...), custom_call_target="tpu_custom_call" | custom-call | flops 42949672960 | bytes 7864320 | tf_op jit(solution)/shard_map/attend_back/pallas_call | solution.py:901
  543.1 3.0 copy.100
  546.1 106.8 %tail.1 = (f32[1024,320]{1,0:T(8,128)}, bf16[1024,320]{1,0:T(8,128)(2,1)}, f32[3,320,320]{2,1,0:T(8,128)}, f32[1280,320]{1,0:T(8,128)}, f32[296,128]{1,0:T(8,128)}) custom-call(bf16[960,1024]{1,0:T(8,128)(2,1)} %bitcast.111, bf16[4,240,1024]{2,1,0:T(8,128)(2,1)} %get-tuple-element.88.grads_ref, ...), custom_call_target="tpu_custom_call" | custom-call | tf_op jit(solution)/shard_map/tail/pallas_call | solution.py:778
  657.4 2.2 copy.97
  659.6 2.9 copy.98
  (167 shorter events, 46.7 us)
Async XLA Ops:
  7.2 50.7 %all-gather.17.cloned.1.call-start = ((), (), s32[]{:S(2)}) async-start(), calls=%async_computation.9 | async-start | bytes 3276800 | tf_op jit(solution)/shard_map/all_gather | solution.py:978
  7.9 7.1 %copy-start.22 = (bf16[1280,320]{0,1:T(8,128)(2,1)S(1)}, bf16[1280,320]{0,1:T(8,128)(2,1)}, u32[]{:S(2)}) copy-start(bf16[1280,320]{0,1:T(8,128)(2,1)} %param.27) | copy-start | bytes 2457604
  10.7 5.6 copy-start.23
  10.7 19.4 %all-to-all-start = ((bf16[4,240,320]{1,2,0:T(8,128)(2,1)}), bf16[4,240,320]{1,2,0:T(8,128)(2,1)}, u32[]{:S(2)}, u32[]{:S(2)}) async-start(bf16[4,240,320]{1,2,0:T(8,128)(2,1)} %copy.84), calls=%async_computation | async-start | bytes 1310720 | tf_op jit(solution)/shard_map/all_to_all | solution.py:981
  15.0 78.9 %all-gather.11.cloned.1.call-start = ((), (), s32[]{:S(2)}) async-start(), calls=%async_computation.4 | async-start | bytes 3072000 | tf_op jit(solution)/shard_map/all_gather | solution.py:1014
  17.7 15.3 %copy-start.30 = (f32[320]{0:T(512)S(1)}, f32[320]{0:T(512)}, u32[]{:S(2)}) copy-start(f32[320]{0:T(512)} %param.21) | copy-start | bytes 3844
  17.7 15.4 %copy-start.31 = (f32[320]{0:T(512)S(1)}, f32[320]{0:T(512)}, u32[]{:S(2)}) copy-start(f32[320]{0:T(512)} %param.22) | copy-start | bytes 3844
  17.7 15.4 %copy-start.32 = (f32[320]{0:T(512)S(1)}, f32[320]{0:T(512)}, u32[]{:S(2)}) copy-start(f32[320]{0:T(512)} %param.23) | copy-start | bytes 3844
  17.7 15.4 %copy-start.33 = (f32[320]{0:T(512)S(1)}, f32[320]{0:T(512)}, u32[]{:S(2)}) copy-start(f32[320]{0:T(512)} %param.24) | copy-start | bytes 3844
  17.7 15.4 %copy-start.34 = (f32[320]{0:T(512)S(1)}, f32[320]{0:T(512)}, u32[]{:S(2)}) copy-start(f32[320]{0:T(512)} %param.20) | copy-start | bytes 3844
  17.8 15.4 %copy-start.35 = (f32[320]{0:T(512)S(1)}, f32[320]{0:T(512)}, u32[]{:S(2)}) copy-start(f32[320]{0:T(512)} %param.28) | copy-start | bytes 3844
  17.8 21.0 %copy-start.29 = (f32[2,320]{1,0:T(2,128)S(1)}, f32[2,320]{1,0:T(2,128)}, u32[]{:S(2)}) copy-start(f32[2,320]{1,0:T(2,128)} %param.18) | copy-start | bytes 7684
  17.8 21.0 %copy-start.28 = (f32[1280]{0:T(1024)S(1)}, f32[1280]{0:T(1024)}, u32[]{:S(2)}) copy-start(f32[1280]{0:T(1024)} %param.26) | copy-start | bytes 15364
  32.3 89.2 %all-gather.19.cloned.1.call-start = ((), (), s32[]{:S(2)}) async-start(), calls=%async_computation.10 | async-start | bytes 3276800 | tf_op jit(solution)/shard_map/all_gather | solution.py:978
  53.4 28.8 %all-to-all-start.1 = ((bf16[4,720,320]{1,2,0:T(8,128)(2,1)}), bf16[4,720,320]{1,2,0:T(8,128)(2,1)}, u32[]{:S(2)}, u32[]{:S(2)}) async-start(bf16[4,720,320]{1,2,0:T(8,128)(2,1)} %pad_maximum_fusion), calls=%async_computation.1 | async-start | bytes 3932160 | tf_op jit(solution)/shard_map/all_to_all | solution.py:981
  57.8 207.3 %all-gather.13.cloned.1.call-start = ((), (), s32[]{:S(2)}) async-start(), calls=%async_computation.5 | async-start | bytes 4096000 | tf_op jit(solution)/shard_map/all_gather | solution.py:1028
  103.5 2.4 copy-start.27
  105.0 210.8 %all-gather.15.cloned.1.call-start = ((), (), s32[]{:S(2)}) async-start(), calls=%async_computation.6 | async-start | bytes 4096000 | tf_op jit(solution)/shard_map/all_gather | solution.py:1029
  105.6 295.6 %reduce-scatter.3.cloned.1.call-start = ((), (), s32[]{:S(2)}) async-start(), calls=%async_computation.7 | async-start | bytes 4096000 | tf_op jit(solution)/shard_map/reduce_scatter | solution.py:1039
  106.9 22.7 %copy-start.6 = (bf16[256,80]{1,0:T(8,128)(2,1)}, bf16[256,80]{1,0:T(8,128)(2,1)S(1)}, u32[]{:S(2)}) copy-start(bf16[256,80]{1,0:T(8,128)(2,1)S(1)} %copy.89.tab_ref) | copy-start | bytes 122884
  124.0 141.1 %copy-start = (bf16[1,256,1280]{2,1,0:T(8,128)(2,1)}, bf16[1,256,1280]{2,1,0:T(8,128)(2,1)S(1)}, u32[]{:S(2)}) copy-start(bf16[1,256,1280]{2,1,0:T(8,128)(2,1)S(1)} %copy.91) | copy-start | bytes 1966084
  265.1 66.3 %copy-start.16 = (f32[4,8,1024]{2,1,0:T(8,128)}, f32[4,8,1024]{2,1,0:T(8,128)S(1)}, u32[]{:S(2)}) copy-start(f32[4,8,1024]{2,1,0:T(8,128)S(1)} %get-tuple-element.85.stat_ref) | copy-start | bytes 393220
  321.2 10.3 %copy-start.18 = (bf16[1,1024,1280]{1,2,0:T(8,128)(2,1)S(1)}, bf16[1,1024,1280]{1,2,0:T(8,128)(2,1)}, u32[]{:S(2)}) copy-start(bf16[1,1024,1280]{1,2,0:T(8,128)(2,1)} %all-gather.19.cloned.1.call-done) | copy-start | bytes 7864324
  331.4 5.1 copy-start.1
  331.4 5.1 copy-start.12
  336.5 2.9 copy-start.4
  336.6 209.6 %reduce-scatter.5.cloned.1.call-start = ((), (), s32[]{:S(2)}) async-start(), calls=%async_computation.8 | async-start | bytes 4096000 | tf_op jit(solution)/shard_map/reduce_scatter | solution.py:1039
  380.9 3.8 copy-start.10
  380.9 3.8 copy-start.13
  652.9 17.8 %copy-start.20 = (f32[1280,320]{1,0:T(8,128)S(1)}, f32[1280,320]{1,0:T(8,128)}, u32[]{:S(2)}) copy-start(f32[1280,320]{1,0:T(8,128)} %get-tuple-element.100) | copy-start | bytes 4915204
  662.5 12.8 %copy-start.21 = (f32[3,320,320]{2,1,0:T(8,128)S(1)}, f32[3,320,320]{2,1,0:T(8,128)}, u32[]{:S(2)}) copy-start(f32[3,320,320]{2,1,0:T(8,128)} %get-tuple-element.97) | copy-start | bytes 3686404
  672.4 4.0 copy-start.24
  (13 other events, 21.4 us)
Sparse Core Ops, SparseCore 0:
  9.6 31.4 all-gather.16
  43.2 50.6 all-gather.10
  95.5 26.0 all-gather.18
  123.5 124.4 all-gather.12
  250.0 65.7 all-gather.14
  336.7 64.4 reduce-scatter.2
  403.5 125.3 reduce-scatter.4

commit v4 on v3

--- a/solution.py
+++ b/solution.py
@@ -106,14 +106,268 @@
     )
 
 
+class Chain:
+    def __init__(self, view, sems, on_block=None):
+        self.view, self.sems, self.on_block = view, sems, on_block
+        self.me = lax.axis_index("col")
+
+    def copy(self, way, hop):
+        block = self.me + (hop - 1) * (2 * way - 1)
+        return pltpu.make_async_remote_copy(
+            src_ref=self.view(block),
+            dst_ref=self.view(block),
+            send_sem=self.sems.at[0, way, hop - 1],
+            recv_sem=self.sems.at[1, way, hop - 1],
+            device_id={"col": lax.rem(self.me + 1 + 2 * way, 4)},
+            device_id_type=MESH,
+        )
+
+    def sends(self, way, hop):
+        if way:
+            return jnp.logical_and(self.me > 0, self.me + hop - 1 < 4)
+        return jnp.logical_and(self.me < 3, self.me - hop + 1 >= 0)
+
+    def each(self, hop, act):
+        for way in range(2):
+
+            @pl.when(self.me + hop < 4 if way else self.me - hop >= 0)
+            def _():
+                act(self.me + hop * (2 * way - 1), way, hop)
+
+    def start(self, way, hop):
+        @pl.when(self.sends(way, hop))
+        def _():
+            self.copy(way, hop).start()
+
+    def begin(self, hop=1):
+        for way in range(2):
+            self.start(way, hop)
+
+    def hop(self, hop, last=3, tell=True):
+        def arrived(block, way, hop):
+            self.copy(way, hop).wait_recv()
+
+        self.each(hop, arrived)
+        if hop < last:
+            for way in range(2):
+                self.start(way, hop + 1)
+        if self.on_block and tell:
+            self.each(hop, self.on_block)
+
+    def end(self, hops=(1, 2, 3)):
+        for hop in hops:
+            for way in range(2):
+
+                @pl.when(self.sends(way, hop))
+                def _():
+                    self.copy(way, hop).wait_send()
+
+
+def image_copy(source, target, sems, *place):
+    return pltpu.make_async_remote_copy(
+        src_ref=source,
+        dst_ref=target,
+        send_sem=sems.at[(0, *place)],
+        recv_sem=sems.at[(1, *place)],
+        device_id={"batch": 1 - lax.axis_index("batch")},
+        device_id_type=MESH,
+    )
+
+
+def weight_chains(weight_all, images, chain_sems, swap_sems):
+    image = lax.axis_index("batch")
+
+    def swap_copy(block, way, hop):
+        return image_copy(weight_all.at[image, block], weight_all.at[image, block], swap_sems, way, hop - 1)
+
+    def swap(block, way, hop):
+        swap_copy(block, way, hop).start()
+
+    def swapped(block, way, hop):
+        swap_copy(block, way, hop).wait()
+
+    shared = images == 2
+    chains = [
+        Chain(lambda i, which=which: weight_all.at[which, i], chain_sems.at[order], swap if shared else None)
+        for order, which in enumerate([image] if shared else [0, 1])
+    ]
+    return chains, swapped if shared else None
+
+
+HALF = 128
+
+
+def half_start(image):
+    return pl.multiple_of(image * (3 * HEAD_DIM - HALF), 16)
+
+
+def row_copy(source, target, sems, kind, order, peer):
+    return pltpu.make_async_remote_copy(
+        src_ref=source,
+        dst_ref=target,
+        send_sem=sems.at[0, kind, order],
+        recv_sem=sems.at[1, kind, order],
+        device_id={"row": peer},
+        device_id_type=MESH,
+    )
+
+
+def beside(blocks):
+    return jnp.concatenate([block.astype(F32) for block in blocks], 1)
+
+
+def start_kernel(
+    images, patches_ref, qkv_ref, rest_ref, vector_ref, column_ref,
+    qkv_out, normed_out, first_out, weight_out, rest_out, vectors_out, columns_out,
+    patches_all, qkv_parts, rest_parts, vector_parts, halves, sems, col_sems, chain_sems, swap_sems,
+):
+    row, col, image = lax.axis_index("row"), lax.axis_index("col"), lax.axis_index("batch")
+    near, far, diag = row_peers()
+    own = first_out.shape[0]
+    shared = images == 2
+    meet(
+        ("row", (near, far, diag)),
+        ("col", [col_peer(step) for step in range(1, 4)]),
+        ("batch", image_peers(images) if shared else ()),
+    )
+
+    def to_row(source, parts, kind):
+        copies = [row_copy(source(peer), parts.at[row], sems, kind, i, peer) for i, peer in enumerate((near, far, diag))]
+        for copy in copies:
+            copy.start()
+        return copies
+
+    qkv_copies = to_row(lambda peer: qkv_ref.at[peer], qkv_parts, 0)
+    vector_copies = to_row(lambda peer: vector_ref, vector_parts, 1)
+    to_near = row_copy(patches_ref, patches_all.at[row], sems, 2, 0, near)
+    to_far = row_copy(patches_ref, patches_all.at[row], sems, 2, 1, far)
+    to_near.start()
+    column_copies = [col_copy(column_ref, columns_out.at[col], col_sems, 0, step) for step in range(1, 4)]
+    for copy in column_copies:
+        copy.start()
+    qkv_parts[row] = qkv_ref[row]
+    vector_parts[row] = vector_ref[...]
+    patches_all[row] = patches_ref[...]
+    columns_out[col] = column_ref[...]
+    for copy in qkv_copies:
+        copy.wait()
+    to_far.start()
+    weight = beside([qkv_parts[i] for i in range(4)]).astype(BF16)
+    weight_out[col] = weight
+
+    def swap_copy(block, way, hop):
+        return image_copy(halves.at[image, block], halves.at[image, block], swap_sems, way, hop - 1)
+
+    def swap(block, way, hop):
+        swap_copy(block, way, hop).start()
+
+    if shared:
+        halves[0, col] = weight[:HALF]
+        halves[1, col] = weight[3 * HEAD_DIM - HALF :]
+        chain = Chain(lambda i: halves.at[image, i], chain_sems, swap)
+    else:
+        chain = Chain(lambda i: weight_out.at[i], chain_sems)
+
+    def product(block, way=0, hop=0):
+        if hop and shared:
+            swap_copy(block, way, hop).wait()
+            weight_out[block, 0 : 3 * HEAD_DIM - HALF] = halves[0, block, 0 : 3 * HEAD_DIM - HALF]
+            weight_out[block, 3 * HEAD_DIM - HALF :] = halves[1, block]
+        bias = jnp.concatenate([columns_out[block][:, 0:256]] * 16, 0).T[: 3 * HEAD_DIM, 0:1]
+        qkv_out[block] = (mm_nt(weight_out[block], normed_out[...]) + bias).astype(BF16)
+
+    chain.begin()
+    for copy in vector_copies + column_copies:
+        copy.wait()
+    vectors_out[...] = beside([vector_parts[i] for i in range(4)])
+    to_far.wait_recv()
+    pass_on = row_copy(patches_all.at[far], patches_all.at[far], sems, 2, 2, near)
+    pass_on.start()
+    rest_copies = to_row(lambda peer: rest_ref.at[peer], rest_parts, 3)
+    rest_parts[row] = rest_ref[row]
+    chain.hop(1)
+    to_near.wait_recv()
+    pass_on.wait_recv()
+    for start in range(0, normed_out.shape[0], own):
+        rows = slice(start, start + own)
+        scaled, _ = normal(beside([patches_all[i, rows] for i in range(4)]))
+        normed_out[rows] = (scaled * vectors_out[0:1] + vectors_out[1:2]).astype(BF16)
+    chain.hop(2)
+    product(col)
+    chain.each(1, product)
+    chain.hop(3)
+    chain.each(2, product)
+    rows = pl.ds(pl.multiple_of(row * own, own), own)
+    first_out[...] = beside([patches_all[i, rows] for i in range(4)]).astype(BF16)
+    for copy in rest_copies:
+        copy.wait()
+    rest_out[...] = beside([rest_parts[i] for i in range(4)]).astype(BF16)
+    chain.each(3, product)
+    chain.end()
+    for copy in (to_near, to_far, pass_on):
+        copy.wait_send()
+
+
+def start(patches, local_qkv, local_rest, vectors, columns):
+    width, part = patches.shape
+    n, model = local_qkv.shape[1], part * 4
+    rest = local_rest.shape[1]
+    vmem = pl.BlockSpec(memory_space=pltpu.VMEM)
+    return pl.pallas_call(
+        partial(start_kernel, lax.axis_size("batch")),
+        in_specs=[vmem] * 5,
+        out_specs=[vmem] * 7,
+        out_shape=[
+            jax.ShapeDtypeStruct((4, n, width), BF16),
+            jax.ShapeDtypeStruct((width, model), BF16),
+            jax.ShapeDtypeStruct((width // 4, model), BF16),
+            jax.ShapeDtypeStruct((4, n, model), BF16),
+            jax.ShapeDtypeStruct((rest, model), BF16),
+            jax.ShapeDtypeStruct((vectors.shape[0], model), F32),
+            jax.ShapeDtypeStruct((4, *columns.shape), F32),
+        ],
+        scratch_shapes=[
+            pltpu.VMEM((4, width, part), BF16),
+            pltpu.VMEM((4, n, part), BF16),
+            pltpu.VMEM((4, rest, part), BF16),
+            pltpu.VMEM((4, *vectors.shape), F32),
+            pltpu.VMEM((2, 4, HALF, model), BF16),
+            pltpu.SemaphoreType.DMA((2, 4, 3)),
+            pltpu.SemaphoreType.DMA((2, 1, 4)),
+            pltpu.SemaphoreType.DMA((2, 2, 3)),
+            pltpu.SemaphoreType.DMA((2, 2, 3)),
+        ],
+        compiler_params=pltpu.CompilerParams(
+            collective_id=7, has_side_effects=True, vmem_limit_bytes=48 << 20
+        ),
+        name="start",
+    )(patches, local_qkv, local_rest, vectors, columns)
+
+
+CHAIN_TURNS = (4, 9)
+
+
 def attend_kernel(
-    given_ref, tab_ref, proj_ref, merged_ref, qkv_ref, exact_ref, stat_ref, proj_all_ref,
-    kaug, columns, acc, top, total, box, sems,
+    images, given_ref, tab_ref, proj_ref, cot_ref, weight_ref,
+    merged_ref, qkv_ref, exact_ref, stat_ref, proj_all_ref, cot_out, weight_all,
+    kaug, columns, acc, top, total, box, sems, cot_parts, cot_sems, local_sems, chain_sems, swap_sems,
 ):
     me = lax.axis_index("col")
     width = given_ref.shape[2]
     blocks = width // QUERIES
-    col_barrier()
+    row, image = lax.axis_index("row"), lax.axis_index("batch")
+    near, far, diag = row_peers()
+    shared = images == 2
+    meet(
+        ("row", (near, far)),
+        ("col", [col_peer(step) for step in range(1, 4)]),
+        ("batch", image_peers(images) if shared else ()),
+    )
+
+    chains, swapped = weight_chains(weight_all, images, chain_sems, swap_sems)
+    keep = [pltpu.make_async_copy(weight_ref.at[i], weight_all.at[i, me], local_sems.at[i]) for i in range(2)]
+    for copy in keep:
+        copy.start()
 
     def part_copy(step):
         return col_copy(given_ref.at[col_peer(step)], qkv_ref.at[me], sems, 0, step)
@@ -124,10 +378,14 @@
     def proj_copy(step):
         return col_copy(proj_ref, proj_all_ref.at[me], sems, 2, step)
 
-    for step in range(1, 4):
+    for step in (2, 1):
         part_copy(step).start()
-    for step in range(1, 4):
-        proj_copy(step).start()
+    to_near = row_copy(cot_ref, cot_parts.at[row], cot_sems, 0, 0, near)
+    to_far = row_copy(cot_ref, cot_parts.at[row], cot_sems, 0, 1, far)
+    pass_on = row_copy(cot_parts.at[far], cot_parts.at[far], cot_sems, 0, 2, near)
+    to_far.start()
+    to_near.start()
+    cot_parts[row] = cot_ref[...]
     qkv_ref[me] = given_ref[me]
     proj_all_ref[me] = proj_ref[...]
 
@@ -173,6 +431,21 @@
         @pl.when(place == 0)
         def _():
             prepare(col_peer(newest))
+
+        @pl.when(turn == CHAIN_TURNS[0])
+        def _():
+            part_copy(3).start()
+            for chain in chains:
+                chain.begin()
+
+        @pl.when(turn == CHAIN_TURNS[1])
+        def _():
+            for chain in chains:
+                chain.hop(1)
+            for step in range(1, 4):
+                proj_copy(step).start()
+            to_far.wait_recv()
+            pass_on.start()
 
         for block in range(blocks):
             at = slice(block * QUERIES, (block + 1) * QUERIES)
@@ -201,8 +474,23 @@
 
         return carry
 
+    for copy in keep:
+        copy.wait()
     lax.fori_loop(0, 16, pair, 0)
+    for chain in chains:
+        chain.hop(2, 2, False)
+    to_near.wait_recv()
+    pass_on.wait_recv()
+    for start in range(0, width, QUERIES):
+        rows = slice(start, start + QUERIES)
+        cot_out[rows] = beside([cot_parts[i, rows] for i in range(4)]).astype(BF16)
     merged_ref[me] = box[me]
+    for chain in chains:
+        chain.end((1, 2))
+        if shared:
+            chain.each(1, swapped)
+    for copy in (to_near, to_far, pass_on):
+        copy.wait_send()
     for step in range(1, 4):
         part_copy(step).wait_send()
         proj_copy(step).wait()
@@ -215,13 +503,16 @@
 
 def attend_back_kernel(
     images, qkv_ref, tab_ref, tab_t_ref, given_ref, exact_ref, stat_ref, proj_ref, fc2_ref,
-    out_ref, tab_grad_ref, bias_out, proj_out, fc2_out,
-    bias_ref, proj_rows, proj_box, grads, kaug, kaug_t, vaug, key_sum, value_sum, spread, columns,
+    activated_ref, weights_ref, middle_ref, bias_fc2_ref,
+    out_ref, tab_grad_ref, bias_out, proj_out, fc2_out, block_out,
+    held, held_sem, bias_ref, proj_rows, proj_box, grads, kaug, kaug_t, vaug, key_sum, value_sum, spread, columns,
     grad_columns, grad_rows, q_rows, box, sems, *weight_parts,
 ):
     me = lax.axis_index("col")
     width = qkv_ref.shape[2]
     blocks = width // QUERIES
+    weight_copy = fetch(weights_ref, 1, (held, held_sem))
+    weight_copy.start()
     meet(
         ("row", row_peers()),
         ("col", [col_peer(step) for step in range(1, 4)]),
@@ -235,7 +526,12 @@
         fc2_out[place] = values
 
     fc2 = weight_steps(fc2_ref, images, weight_parts[:4], write_fc2)
-    proj = weight_steps(proj_rows, images, weight_parts[4:], write_proj)
+    proj = weight_steps(proj_rows, images, weight_parts[4:8], write_proj)
+
+    def finish_block(total, piece, rows):
+        return middle_ref[rows] + (total + bias_fc2_ref[0:1])
+
+    block = row_mix_steps(activated_ref, held, block_out, finish_block, False, True, weight_parts[8:])
 
     def grad_copy(step):
         return col_copy(given_ref.at[col_peer(step)], grads.at[me], sems, GRADS, step)
@@ -253,8 +549,6 @@
 
     for step in range(1, 4):
         grad_copy(step).start()
-    for step in range(1, 4):
-        proj_copy(step).start()
     next(fc2)
     grads[me] = given_ref[me]
     proj_box[me] = proj_ref[me]
@@ -333,18 +627,23 @@
         add_bias(2 * HEAD_DIM, value_grad)
 
     def pair(turn, carry):
-        outer, inner = turn // 4, turn % 4
-        q_step = inner + (outer // 3) * (3 - 2 * inner)
-        k_step = 3 - outer
+        later = jnp.maximum(turn - 4, 0)
+        q_step = jnp.where(turn < 4, 0, 1 + later % 3)
+        k_step = jnp.where(turn < 4, 3 - turn, 3 - later // 3)
         q_part, k_part = col_peer(q_step), col_peer(k_step)
 
-        @pl.when(jnp.logical_and(turn > 0, turn < 4))
+        @pl.when(jnp.logical_and(turn >= 4, turn < 7))
         def _():
             grad_copy(q_step).wait_recv()
 
-        @pl.when(turn < 4)
+        @pl.when(jnp.logical_or(turn == 0, jnp.logical_and(turn >= 4, turn < 7)))
         def _():
             prepare(q_part)
+
+        @pl.when(turn == 7)
+        def _():
+            for step in range(1, 4):
+                proj_copy(step).start()
 
         for block in range(blocks):
             at = slice(block * QUERIES, (block + 1) * QUERIES)
@@ -359,43 +658,53 @@
                 total = result if total is None else total + result
             spread[q_part, :, at] += total
 
-        @pl.when(inner == 3)
+        keys_done = jnp.logical_and(turn >= 4, q_step == 3)
+        queries_done = jnp.logical_or(turn == 3, turn >= 13)
+
+        @pl.when(keys_done)
         def _():
             finish_keys(k_part)
 
-        @pl.when(jnp.logical_and(inner == 3, outer < 3))
+        @pl.when(jnp.logical_and(keys_done, k_step > 0))
         def _():
             key_copy(k_step).start()
 
-        @pl.when(outer == 3)
+        @pl.when(queries_done)
         def _():
             finish_queries(q_part)
 
-        @pl.when(jnp.logical_and(outer == 3, inner < 3))
+        @pl.when(jnp.logical_and(queries_done, q_step > 0))
         def _():
             query_copy(q_step).start()
 
         return carry
 
+    weight_copy.wait()
+    next(block)
+    next(block)
     lax.fori_loop(0, 4, pair, 0)
+    next(block)
+    next(block)
+    lax.fori_loop(4, 8, pair, 0)
+    next(fc2)
+    next(block, None)
+    lax.fori_loop(8, 12, pair, 0)
     for step in range(1, 4):
         proj_copy(step).wait()
     total = proj_box[0].astype(F32)
     for source in range(1, 4):
         total = total + proj_box[source].astype(F32)
     proj_rows[...] = total.astype(BF16)
-    next(fc2)
-    next(proj)
-    lax.fori_loop(4, 8, pair, 0)
     next(proj)
     next(fc2, None)
-    lax.fori_loop(8, 16, pair, 0)
-    next(proj, None)
+    lax.fori_loop(12, 16, pair, 0)
+    next(proj)
     out_ref[me] = box[me]
     for step in range(1, 4):
         grad_copy(step).wait_send()
         query_copy(step).wait()
         key_copy(step).wait()
+    next(proj, None)
     bias_out[0:1] = bias_ref[0:128].T[0:1]
     bias_out[1:2] = bias_ref[2 * HEAD_DIM : 2 * HEAD_DIM + 128].T[0:1]
 
@@ -555,41 +864,117 @@
     ]
 
 
-def row_mix_kernel(finish, extra, outs, left_t, left_ref, weight_ref, *refs):
+def row_mix_kernel(finish, extra, outs, left_t, share, images, left_ref, weight_ref, *refs):
     extra_refs, refs = refs[:extra], refs[extra:]
+    if images:
+        refs = refs[1:]
+    if share:
+        share_ref, refs = refs[0], refs[1:]
     (gathered, *out_refs), scratch = refs[:outs], refs[outs:]
+    if len(weight_ref.shape) == 3:
+        *scratch, held, held_sem = scratch
+        copy = fetch(weight_ref, 0, (held, held_sem))
+        copy.start()
     near, far, _ = row_peers()
-    meet(("row", (near, far)))
+    meet(
+        ("row", (near, far)),
+        ("col", [col_peer(step) for step in range(1, 4)] if images else ()),
+        ("batch", image_peers(2) if share or images == 2 else ()),
+    )
+    if images:
+        *out_refs, weight_all = out_refs
+        *scratch, chain_sems, pass_sems = scratch
+        chains, swapped = weight_chains(weight_all, images, chain_sems, pass_sems)
+        for chain in chains:
+            chain.begin(3)
+            if swapped:
+                chain.each(2, chain.on_block)
+    if share:
+        *out_refs, share_out = out_refs
+        *scratch, got, swap_sems = scratch
+        image, half = lax.axis_index("batch"), got.shape[1]
+        given = pl.ds(pl.multiple_of((1 - image) * half, 16), half)
+        kept = pl.ds(pl.multiple_of(image * half, 16), half)
+        swap = image_copy(share_ref.at[:, given], got, swap_sems, 0)
+        swap.start()
 
     def last(total, piece, rows):
         return finish(total, piece, rows, *extra_refs, out_refs)
 
+    if len(weight_ref.shape) == 3:
+        copy.wait()
+        weight_ref = held
     for _ in row_mix_steps(left_ref, weight_ref, gathered, last, left_t, False, scratch):
         pass
-
-
-def row_mix(finish, name, number, left, weight, extra, out_shapes, left_t):
+    if images:
+        for chain in chains:
+            chain.hop(3)
+        for chain in chains:
+            chain.end((3,))
+            if swapped:
+                chain.each(2, swapped)
+                chain.each(3, swapped)
+    if share:
+        swap.wait()
+        for place in range(4):
+            both = share_ref[place, kept].astype(F32) + got[place].astype(F32)
+            share_out[place] = both.astype(BF16)
+
+
+def fetch(stack_ref, which, scratch):
+    return pltpu.make_async_copy(stack_ref.at[which], scratch[0], scratch[1])
+
+
+def fetch_scratch(stack):
+    return [pltpu.VMEM(stack.shape[1:], stack.dtype), pltpu.SemaphoreType.DMA(())]
+
+
+def row_mix(finish, name, number, left, weight, extra, out_shapes, left_t, share=None, passing=None):
     tokens = left.shape[1] if left_t else left.shape[0]
-    model = weight.shape[1]
+    model = weight.shape[-1]
     own = tokens // 4
     vmem = pl.BlockSpec(memory_space=pltpu.VMEM)
-    return pl.pallas_call(
-        partial(row_mix_kernel, finish, len(extra), 1 + len(out_shapes), left_t),
-        out_shape=[jax.ShapeDtypeStruct((4, own, model), BF16), *out_shapes],
-        in_specs=[vmem] * (2 + len(extra)),
-        out_specs=[vmem] * (1 + len(out_shapes)),
-        scratch_shapes=mix_scratch(own, model, False),
+    shared = share is not None and lax.axis_size("batch") == 2
+    specs, outs, scratch = [vmem] * (2 + len(extra)), [*out_shapes], mix_scratch(own, model, False)
+    operands = (left, weight, *extra)
+    if shared:
+        cols, n, _ = share.shape
+        specs.append(vmem)
+        operands = (*operands, share)
+        outs.append(jax.ShapeDtypeStruct((cols, n // 2, model), BF16))
+        scratch += [pltpu.VMEM((cols, n // 2, model), BF16), pltpu.SemaphoreType.DMA((2, 1))]
+    out_specs = [vmem] * (1 + len(outs))
+    alias, images = {}, 0
+    if passing is not None:
+        images = lax.axis_size("batch")
+        alias = {len(operands): len(out_specs)}
+        operands = (*operands, passing)
+        specs.append(pl.BlockSpec(memory_space=pl.ANY))
+        out_specs.append(pl.BlockSpec(memory_space=pl.ANY))
+        outs.append(jax.ShapeDtypeStruct(passing.shape, passing.dtype))
+        scratch += [pltpu.SemaphoreType.DMA((2, 2, 2, 3)), pltpu.SemaphoreType.DMA((2, 2, 3))]
+    if weight.ndim == 3:
+        specs[1] = pl.BlockSpec(memory_space=pl.ANY)
+        scratch += fetch_scratch(weight)
+    results = pl.pallas_call(
+        partial(row_mix_kernel, finish, len(extra), 1 + len(outs), left_t, shared, images),
+        out_shape=[jax.ShapeDtypeStruct((4, own, model), BF16), *outs],
+        in_specs=specs,
+        out_specs=out_specs,
+        input_output_aliases=alias,
+        scratch_shapes=scratch,
         compiler_params=pltpu.CompilerParams(
             collective_id=number, has_side_effects=True, vmem_limit_bytes=48 << 20
         ),
         cost_estimate=pl.CostEstimate(
-            flops=2 * tokens * weight.size, bytes_accessed=16 * own * model, transcendentals=0
+            flops=2 * tokens * model * model, bytes_accessed=16 * own * model, transcendentals=0
         ),
         name=name,
-    )(left, weight, *extra)
-
-
-def weight_steps(values_ref, images, scratch, write):
+    )(*operands)
+    return results if share is None or shared else (*results, share)
+
+
+def weight_steps(values_ref, images, scratch, write, joined=False):
     boxes, arrived, other, sems = scratch
     me, part = lax.axis_index("row"), boxes.shape[2]
     for place in range(4):
@@ -623,7 +1008,10 @@
         yield
         swap.wait()
         for place in range(4):
-            write(place, arrived[place].astype(F32) + other[place].astype(F32))
+            if joined:
+                write(place, arrived[place].astype(F32), other[place].astype(F32))
+            else:
+                write(place, arrived[place].astype(F32) + other[place].astype(F32))
     else:
         yield
         for place in range(4):
@@ -673,23 +1061,47 @@
     ]
 
 
-def column_steps(grad_ref, normed_ref, box, arrived, own_keep, out, sems):
-    me = lax.axis_index("col")
+def column_steps(images, grad_ref, normed_ref, out, scratch):
+    keep, give, got, box, arrived, sems, swap_sems = scratch
+    image, rows = lax.axis_index("batch"), out.shape[0]
+    shared = images == 2
+    swaps = {}
+    for step in (1, 2, 3, 0):
+        keep[step] = mm(grad_ref[col_peer(step)], normed_ref[...])
+        if shared:
+            give[step] = keep[step, pl.ds(half_start(1 - image), rows)].astype(BF16)
+            swaps[step] = image_copy(give.at[step], got.at[step], swap_sems, step)
+            swaps[step].start()
+    yield
+
+    def total(step):
+        if not shared:
+            return keep[step]
+        swaps[step].wait()
+        return keep[step, pl.ds(half_start(image), rows)] + got[step].astype(F32)
+
     copies = []
     for step in range(1, 4):
-        box[step - 1] = mm(grad_ref[col_peer(step)], normed_ref[...]).astype(BF16)
+        box[step - 1] = total(step).astype(BF16)
         copy = col_copy(box.at[step - 1], arrived.at[step - 1], sems, 0, step)
         copy.start()
         copies.append(copy)
     yield
-    own_keep[...] = mm(grad_ref[me], normed_ref[...])
-    yield
-    for copy in copies:
+    whole = total(0)
+    for step, copy in enumerate(copies):
         copy.wait()
-    total = own_keep[...]
-    for step in range(3):
-        total = total + arrived[step].astype(F32)
-    out[...] = total.astype(BF16)
+        whole = whole + arrived[step].astype(F32)
+    out[...] = whole.astype(BF16)
+
+
+def column_scratch(n, rows, model):
+    return [
+        pltpu.VMEM((4, n, model), F32),
+        *[pltpu.VMEM((4, rows, model), BF16)] * 2,
+        *[pltpu.VMEM((3, rows, model), BF16)] * 2,
+        pltpu.SemaphoreType.DMA((2, 1, 4)),
+        pltpu.SemaphoreType.DMA((2, 4)),
+    ]
 
 
 EARLY_ROWS, TABLE_ROWS, BIAS_ROWS, LAST_ROWS = 80, 160, 32, 24
@@ -698,13 +1110,12 @@
 def tail_kernel(
     axes,
     qkv_grad_ref, grads_ref, weight_qkv_ref, normed1_ref, first_ref, middle_grad_ref, gain_ref,
-    activated_ref, weight_fc2_ref, middle_ref, bias_fc2_ref, fc1_ref, early_ref, table_ref, bias_ref,
-    patches_out, block_out, qkv_out, fc1_out, small,
+    fc1_ref, early_ref, table_ref, bias_ref, patches_out, qkv_out, fc1_out, small,
     *scratch,
 ):
-    sums1, qkv_rows, box, arrived, own_keep, col_sems, *scratch = scratch
-    mix1, mix2 = scratch[:7], scratch[7:14]
-    qkv_scratch, fc1_scratch, sum_parts = scratch[14:18], scratch[18:22], scratch[22:]
+    sums1, qkv_rows, *scratch = scratch
+    col_scratch, scratch = scratch[:7], scratch[7:]
+    mix, qkv_scratch, fc1_scratch, sum_parts = scratch[:7], scratch[7:11], scratch[11:15], scratch[15:]
     row, col = lax.axis_index("row"), lax.axis_index("col")
     images = dict(axes)["batch"]
     meet(
@@ -716,32 +1127,36 @@
     def finish1(total, piece, rows):
         return last_finish(total, piece, rows, gain_ref, first_ref, middle_grad_ref, (None, sums1))
 
-    def finish2(total, piece, rows):
-        return middle_ref[rows] + (total + bias_fc2_ref[0:1])
-
-    def write_fc1(place, values):
+    image = lax.axis_index("batch")
+    shared = images == 2
+
+    def write_fc1(place, values, others=None):
         n = values.shape[0]
-        fc1_out[place * n : (place + 1) * n] = values
+        if others is None:
+            fc1_out[place * n : (place + 1) * n] = values
+        else:
+            fc1_out[pl.ds(pl.multiple_of((2 * place + image) * n, 8), n)] = values
+            fc1_out[pl.ds(pl.multiple_of((2 * place + 1 - image) * n, 8), n)] = others
 
     head_grads = []
 
-    def write_qkv(place, values):
+    def write_qkv(place, values, others=None):
+        if others is not None:
+            first, second = jnp.where(image == 0, values, others), jnp.where(image == 0, others, values)
+            values = jnp.concatenate([first[: 3 * HEAD_DIM - HALF], second], 0)
         head_grads.append(values)
 
-    qkv_sum = column_steps(grads_ref, normed1_ref, box, arrived, own_keep, qkv_rows, col_sems)
-    patches = row_mix_steps(qkv_grad_ref, weight_qkv_ref, patches_out, finish1, True, True, mix1)
-    block = row_mix_steps(activated_ref, weight_fc2_ref, block_out, finish2, False, True, mix2)
-    fc1 = weight_steps(fc1_ref, images, fc1_scratch, write_fc1)
-    qkv = weight_steps(qkv_rows, images, qkv_scratch, write_qkv)
+    qkv_sum = column_steps(images, grads_ref, normed1_ref, qkv_rows, col_scratch)
+    patches = row_mix_steps(qkv_grad_ref, weight_qkv_ref, patches_out, finish1, True, True, mix)
+    fc1 = weight_steps(fc1_ref, images, fc1_scratch, write_fc1, shared)
+    qkv = weight_steps(qkv_rows, images, qkv_scratch, write_qkv, shared)
     sums = sum_steps(small, axes, sum_parts)
 
     def go(*steps):
         for step in steps:
             next(step, None)
 
-    go(qkv_sum, patches, block, fc1)
-    go(patches, block, patches, block, qkv_sum)
-    go(patches)
+    go(qkv_sum, patches, patches, patches, qkv_sum, patches)
 
     small[0:EARLY_ROWS] = early_ref[...]
     at = EARLY_ROWS
@@ -758,44 +1173,40 @@
     spare = jnp.zeros((LAST_ROWS - len(last), 128), F32)
     small[at : at + LAST_ROWS] = jnp.concatenate([*last, spare], 0)
 
-    go(sums, block, fc1, qkv_sum, qkv)
-    go(sums, patches, block, qkv, sums, fc1, sums, qkv)
-    count = len(head_grads)
+    go(sums, fc1, qkv_sum, qkv, sums, patches, fc1, sums, qkv, fc1, sums, qkv)
     for kind in range(3):
         rows = slice(kind * HEAD_DIM, (kind + 1) * HEAD_DIM)
         qkv_out[kind] = jnp.concatenate([values[rows] for values in head_grads], 0).T
 
 
 def tail(
-    qkv_grad, weight_qkv, normed1, first, middle_grad, gain, activated, weight_fc2, middle, bias_fc2, fc1, early, table, bias
+    qkv_grad, weight_qkv, normed1, first, middle_grad, gain, fc1, early, table, bias
 ):
     cols, n, tokens = qkv_grad.shape
     model = weight_qkv.shape[1]
     own, part = tokens // 4, model // 4
+    shared = lax.axis_size("batch") == 2
+    rows = HALF if shared else n
+    units = fc1.shape[0] * (2 if shared else 1)
     axes = tuple((name, lax.axis_size(name)) for name in ("row", "batch", "col"))
     small_rows = EARLY_ROWS + TABLE_ROWS + BIAS_ROWS + LAST_ROWS
     vmem = pl.BlockSpec(memory_space=pltpu.VMEM)
     return pl.pallas_call(
         partial(tail_kernel, axes),
-        in_specs=[vmem] * 15,
-        out_specs=[vmem] * 5,
+        in_specs=[vmem] * 11,
+        out_specs=[vmem] * 4,
         out_shape=[
             jax.ShapeDtypeStruct((tokens, part), F32),
-            jax.ShapeDtypeStruct((tokens, part), BF16),
             jax.ShapeDtypeStruct((3, part, 4 * HEAD_DIM), F32),
-            jax.ShapeDtypeStruct((4 * fc1.shape[0], part), F32),
+            jax.ShapeDtypeStruct((4 * units, part), F32),
             jax.ShapeDtypeStruct((small_rows, 128), F32),
         ],
         scratch_shapes=[
             pltpu.VMEM((3, model), F32),
-            pltpu.VMEM((n, model), BF16),
-            pltpu.VMEM((3, n, model), BF16),
-            pltpu.VMEM((3, n, model), BF16),
-            pltpu.VMEM((n, model), F32),
-            pltpu.SemaphoreType.DMA((2, 1, 4)),
+            pltpu.VMEM((rows, model), BF16),
+            *column_scratch(n, rows, model),
             *mix_scratch(own, model, True),
-            *mix_scratch(own, model, True),
-            *weight_scratch(n, part),
+            *weight_scratch(rows, part),
             *weight_scratch(fc1.shape[0], part),
             *sum_scratch(small_rows, axes),
         ],
@@ -805,7 +1216,7 @@
         name="tail",
     )(
         qkv_grad.reshape(cols * n, tokens), qkv_grad, weight_qkv, normed1, first, middle_grad, gain,
-        activated, weight_fc2, middle, bias_fc2, fc1, early, table, bias,
+        fc1, early, table, bias,
     )
 
 
@@ -829,18 +1240,18 @@
     bias_grad_ref[...] = total
 
 
-def feed_forward(x, w1, bias, cotangent, w2):
+def feed_forward(x, weights, bias, cotangent):
     tokens, model = x.shape
-    hidden = w1.shape[0]
+    hidden = weights.shape[1]
     step = HIDDEN if hidden % HIDDEN == 0 else hidden
     whole = pl.BlockSpec((tokens, model), lambda i: (0, 0), pipeline_mode=pl.Buffered(1))
-    weight = pl.BlockSpec((step, model), lambda i: (i, 0))
+    first, second = [pl.BlockSpec((None, step, model), lambda i, j=j: (j, i, 0)) for j in range(2)]
     vector = pl.BlockSpec((1, step), lambda i: (0, i))
     columns = pl.BlockSpec((tokens, step), lambda i: (0, i))
     return pl.pallas_call(
         hidden_kernel,
         grid=(hidden // step,),
-        in_specs=[whole, weight, vector, whole, weight],
+        in_specs=[whole, first, vector, whole, second],
         out_specs=[columns, columns, vector],
         out_shape=[
             jax.ShapeDtypeStruct((tokens, hidden), BF16),
@@ -854,23 +1265,26 @@
             transcendentals=2 * tokens * hidden,
         ),
         name="feed_forward",
-    )(x, w1, bias, cotangent, w2)
-
-
-def attention(qkv, table, proj):
+    )(x, weights, bias, cotangent, weights)
+
+
+def attention(qkv, table, proj, cotangent, weights):
     count, _, width = qkv.shape
     tokens = count * width
+    images = lax.axis_size("batch")
     vmem = pl.BlockSpec(memory_space=pltpu.VMEM)
     return pl.pallas_call(
-        attend_kernel,
-        in_specs=[vmem] * 3,
-        out_specs=[vmem] * 5,
+        partial(attend_kernel, images),
+        in_specs=[*[vmem] * 4, pl.BlockSpec(memory_space=pl.ANY)],
+        out_specs=[*[vmem] * 6, pl.BlockSpec(memory_space=pl.ANY)],
         out_shape=[
             jax.ShapeDtypeStruct((count, HEAD_DIM, width), BF16),
             jax.ShapeDtypeStruct(qkv.shape, BF16),
             jax.ShapeDtypeStruct((count, HEAD_DIM, width), F32),
             jax.ShapeDtypeStruct((count, 8, width), F32),
             jax.ShapeDtypeStruct((count, *proj.shape), BF16),
+            jax.ShapeDtypeStruct((width, 4 * cotangent.shape[1]), BF16),
+            jax.ShapeDtypeStruct((2, count, *weights.shape[1:]), BF16),
         ],
         scratch_shapes=[
             pltpu.VMEM((count, width, 256), BF16),
@@ -880,6 +1294,11 @@
             pltpu.VMEM((count, 8, width), F32),
             pltpu.VMEM((count, HEAD_DIM, width), BF16),
             pltpu.SemaphoreType.DMA((2, 3, 4)),
+            pltpu.VMEM((4, *cotangent.shape), BF16),
+            pltpu.SemaphoreType.DMA((2, 1, 3)),
+            pltpu.SemaphoreType.DMA((2,)),
+            pltpu.SemaphoreType.DMA((2, 2, 2, 3)),
+            pltpu.SemaphoreType.DMA((2, 2, 3)),
         ],
         compiler_params=pltpu.CompilerParams(
             collective_id=5, has_side_effects=True, vmem_limit_bytes=48 << 20
@@ -890,26 +1309,28 @@
             transcendentals=tokens * tokens,
         ),
         name="attend",
-    )(qkv, table, proj)
-
-
-def attention_back(qkv, table, grad, exact, stat, proj, fc2):
+    )(qkv, table, proj, cotangent, weights)
+
+
+def attention_back(qkv, table, grad, exact, stat, proj, fc2, activated, weights, middle, bias_fc2):
     count, _, width = qkv.shape
     tokens = count * width
     images, part = lax.axis_size("batch"), fc2.shape[1] // 4
     vmem = pl.BlockSpec(memory_space=pltpu.VMEM)
     return pl.pallas_call(
         partial(attend_back_kernel, images),
-        in_specs=[vmem] * 8,
-        out_specs=[vmem] * 5,
+        in_specs=[*[vmem] * 9, pl.BlockSpec(memory_space=pl.ANY), vmem, vmem],
+        out_specs=[vmem] * 6,
         out_shape=[
             jax.ShapeDtypeStruct((count, 3 * HEAD_DIM, width), BF16),
             jax.ShapeDtypeStruct(table.shape[::-1], F32),
             jax.ShapeDtypeStruct((2, 128), F32),
             jax.ShapeDtypeStruct((4, proj.shape[1], part), F32),
             jax.ShapeDtypeStruct((4, fc2.shape[0], part), F32),
+            jax.ShapeDtypeStruct((width, part), BF16),
         ],
         scratch_shapes=[
+            *fetch_scratch(weights),
             pltpu.VMEM((384, 128), F32),
             pltpu.VMEM(proj.shape[1:], BF16),
             pltpu.VMEM(proj.shape, BF16),
@@ -928,9 +1349,10 @@
             pltpu.SemaphoreType.DMA((2, 4, 4)),
             *weight_scratch(fc2.shape[0], part),
             *weight_scratch(proj.shape[1], part),
+            *mix_scratch(*middle.shape, True),
         ],
         compiler_params=pltpu.CompilerParams(
-            collective_id=4, has_side_effects=True, vmem_limit_bytes=60 << 20
+            collective_id=4, has_side_effects=True, vmem_limit_bytes=62 << 20
         ),
         cost_estimate=pl.CostEstimate(
             flops=2 * tokens * tokens * 1280,
@@ -938,7 +1360,7 @@
             transcendentals=tokens * tokens,
         ),
         name="attend_back",
-    )(qkv, table, table.T, grad, exact, stat, proj, fc2)
+    )(qkv, table, table.T, grad, exact, stat, proj, fc2, activated, weights, middle, bias_fc2)
 
 
 def moments(values):
@@ -974,32 +1396,16 @@
     hidden = fc1_bias.shape[0] // rows
     head = HEAD_DIM
 
-    def over_row(values):
-        return lax.all_gather(values, "row", axis=1, tiled=True)
-
-    def spread_rows(values):
-        moved = lax.all_to_all(values, "row", 0, 0, tiled=True)
-        return moved.transpose(1, 0, 2).reshape(values.shape[1], model)
-
     images = lax.axis_size("batch")
 
-    residual = over_row(patches[0])
-    cotangent = over_row(out_grad[0])
-    vectors = lax.all_gather(
-        jnp.stack([norm1_gain, norm1_shift, norm2_gain, norm2_shift, proj_bias, fc2_bias]),
-        "row", axis=1, tiled=True,
-    )
-    gain1, shift1, gain2, shift2, bias_proj, bias_fc2 = [vectors[i] for i in range(6)]
-    by_col = lax.all_gather(
-        jnp.concatenate([qv_bias.reshape(-1), fc1_bias]), "col", axis=0, tiled=False
-    )
-    bias_qv = by_col[:, : 2 * rows * head].reshape(cols, 2, rows, head)
-    bias_qv = lax.dynamic_index_in_dim(bias_qv, row, 2, keepdims=False)
-    bias_fc1 = by_col[:, 2 * rows * head :].reshape(cols, rows, hidden)
-    bias_fc1 = lax.dynamic_index_in_dim(bias_fc1, row, 1, keepdims=False)
-    bias_fc1 = bias_fc1.reshape(cols * hidden)
-
-    local_qkv = qkv_weight.reshape(part, 3, rows, head).transpose(2, 1, 3, 0)
+    vectors = jnp.stack([norm1_gain, norm1_shift, norm2_gain, norm2_shift, proj_bias, fc2_bias])
+    vectors = jnp.concatenate([vectors, jnp.zeros((2, part), F32)], 0)
+    bias_qkv = lax.dynamic_index_in_dim(qv_bias.reshape(2, rows, head), row, 1, keepdims=False)
+    bias_qkv = jnp.stack([bias_qkv[0], jnp.zeros_like(bias_qkv[0]), bias_qkv[1]]).reshape(1, -1)
+    bias_fc1 = lax.dynamic_index_in_dim(fc1_bias.reshape(rows, hidden), row, 0, keepdims=True)
+    columns = jnp.concatenate([jnp.pad(bias_qkv, ((0, 0), (0, 256 - 3 * head))), bias_fc1], 1)
+    columns = jnp.broadcast_to(columns, (8, 256 + hidden))
+    local_qkv = qkv_weight.reshape(part, 3, rows, head).transpose(2, 1, 3, 0).reshape(rows, 3 * head, part)
     local_rest = jnp.concatenate(
         [
             proj_weight.reshape(rows, head, part),
@@ -1008,28 +1414,20 @@
         ],
         1,
     )
-    spread_qkv = spread_rows(local_qkv.reshape(rows, 3 * head, part))
-    local_rest, spread_qkv = lax.optimization_barrier((local_rest, spread_qkv))
-    spread_rest = spread_rows(local_rest)
-    weight_qkv = lax.all_gather(spread_qkv, "col", axis=0, tiled=True)
+    qkv, normed1, first_own, weight_qkv, spread_rest, vectors, columns = start(
+        patches[0], local_qkv, local_rest, vectors, columns
+    )
+    gain1, shift1, gain2, shift2, bias_proj, bias_fc2 = [vectors[i] for i in range(6)]
+    weight_qkv = weight_qkv.reshape(cols * 3 * head, model)
+    bias_fc1 = columns[:, 0, 256:].reshape(cols * hidden)
 
     zero_row = jnp.zeros((1, head), BF16)
     table = jnp.concatenate([height_table[::-1], zero_row, width_table[::-1], zero_row], 0)
 
-    first = residual.astype(F32)
-    center1, inv1 = moments(first)
-    scaled1 = (first - center1) * inv1
-    normed1 = (scaled1 * gain1 + shift1).astype(BF16)
-    normed1, spread_rest = lax.optimization_barrier((normed1, spread_rest))
-    bias = jnp.stack([bias_qv[:, 0], jnp.zeros_like(bias_qv[:, 0]), bias_qv[:, 1]], 1)
-    qkv = mm_nt(weight_qkv, normed1)
-    qkv = (qkv.reshape(cols, 3 * head, width) + bias.reshape(cols, 3 * head, 1)).astype(BF16)
-    qkv, spread_rest = lax.optimization_barrier((qkv, spread_rest))
-    weight_fc1 = lax.all_gather(spread_rest[head : head + hidden], "col", axis=0, tiled=True)
-    weight_fc2 = lax.all_gather(spread_rest[head + hidden :], "col", axis=0, tiled=True)
-    merged, qkv, exact, stat, weight_proj = attention(qkv, table, spread_rest[:head])
+    merged, qkv, exact, stat, weight_proj, cotangent, weights = attention(
+        qkv, table, spread_rest[:head], out_grad[0], spread_rest[head:].reshape(2, hidden, model)
+    )
     weight_proj = weight_proj.reshape(cols * head, model)
-    merged, weight_fc1 = lax.optimization_barrier((merged, weight_fc1))
     merged = merged.reshape(cols * head, width)
 
     def contract_rows(left, right):
@@ -1041,34 +1439,27 @@
     def tokens_of_row(values):
         return lax.dynamic_slice_in_dim(values, row * own, own, 0)
 
-    def sum_tokens(values):
-        return lax.psum_scatter(values.astype(BF16), "row", scatter_dimension=0, tiled=True)
-
     own_shape = (own, model)
     vec2 = jnp.stack([gain2, shift2, bias_proj])
-    normed2, middle = row_mix(
+    normed2, middle, weights = row_mix(
         forward_finish, "middle_and_norm2", 1, merged, weight_proj,
-        (vec2, tokens_of_row(residual)), [jax.ShapeDtypeStruct(own_shape, F32)], True,
+        (vec2, first_own), [jax.ShapeDtypeStruct(own_shape, F32)], True, None, weights,
     )
     normed2 = normed2.reshape(width, model)
-    activated, preact_grad, fc1_bias_part = feed_forward(
-        normed2, weight_fc1, bias_fc1[None], cotangent, weight_fc2
-    )
+    weights = weights.reshape(2, cols * hidden, model)
+    activated, preact_grad, fc1_bias_part = feed_forward(normed2, weights, bias_fc1[None], cotangent)
     fc2_grad = contract_rows(activated, cotangent).astype(BF16)
     fc2_grad, preact_grad = lax.optimization_barrier((fc2_grad, preact_grad))
+    fc1_grad = contract_rows(preact_grad, normed2).astype(BF16).reshape(cols, hidden, model)
 
     own_and_sums = [jax.ShapeDtypeStruct(own_shape, F32), jax.ShapeDtypeStruct((3, model), F32)]
-    branch_grad, middle_grad, sums2 = row_mix(
-        backward_finish, "middle_grad", 2, preact_grad, weight_fc1,
-        (vec2, middle, tokens_of_row(cotangent)), own_and_sums, False,
+    branch_grad, middle_grad, sums2, fc1_grad = row_mix(
+        backward_finish, "middle_grad", 2, preact_grad, weights,
+        (vec2, middle, tokens_of_row(cotangent)), own_and_sums, False, fc1_grad,
     )
     branch_grad = branch_grad.reshape(width, model)
 
     merged_grad = mm_nt(weight_proj, branch_grad).astype(BF16).reshape(cols, head, width)
-    merged_grad, activated, preact_grad, normed2, branch_grad = lax.optimization_barrier(
-        (merged_grad, activated, preact_grad, normed2, branch_grad)
-    )
-    fc1_grad = contract_rows(preact_grad, normed2).astype(BF16)
     proj_grad = mm(merged, branch_grad).astype(BF16)
     fc2_grad = sum_columns(fc2_grad.reshape(cols, hidden, model))
     early = jnp.concatenate(
@@ -1083,13 +1474,13 @@
     merged_grad, fc1_grad, proj_grad, fc2_grad, early = lax.optimization_barrier(
         (merged_grad, fc1_grad, proj_grad, fc2_grad, early)
     )
-    fc1_grad = sum_columns(fc1_grad.reshape(cols, hidden, model))
-    qkv_grad, table_grad, bias_grad, proj_grad, fc2_grad = attention_back(
-        qkv, table, merged_grad, exact, stat, proj_grad.reshape(cols, head, model), fc2_grad
-    )
-    input_grad, final, qkv_weight_grad, fc1_grad, small = tail(
-        qkv_grad, weight_qkv, normed1, tokens_of_row(residual), middle_grad, gain1[None],
-        activated, weight_fc2, middle, bias_fc2[None], fc1_grad, early, table_grad, bias_grad,
+    fc1_grad = sum_columns(fc1_grad)
+    qkv_grad, table_grad, bias_grad, proj_grad, fc2_grad, final = attention_back(
+        qkv, table, merged_grad, exact, stat, proj_grad.reshape(cols, head, model), fc2_grad,
+        activated, weights, middle, bias_fc2[None],
+    )
+    input_grad, qkv_weight_grad, fc1_grad, small = tail(
+        qkv_grad, weight_qkv, normed1, first_own, middle_grad, gain1[None], fc1_grad, early, table_grad, bias_grad
     )
 
     def sum_images(values):

time: 696 us -> 588 us (0.84)
  waiting for transfers between devices: 71 us -> 20.5 us
  blocking collectives: 19 us -> 0 us
  local copies, waits for them, and re-layouts: 64.6 us -> 48 us
  starting transfers between devices: 9.64 us -> 0.08 us
    all_gather x5 -> x0, waiting for transfers between devices: 29.9 us -> none  [the longest x2 14.4 us: over_row(): return lax.all_gather(values, 'row', axis=1, tiled=True)]
    all_to_all x2 -> x0, waiting for transfers between devices: 27.7 us -> none  [spread_rows(): moved = lax.all_to_all(values, 'row', 0, 0, tiled=True)]
    all_gather x2 -> x0, blocking collectives: 19 us -> none  [the longest x1 13.5 us: shards(): lax.all_gather(jnp.concatenate([qv_bias.reshape(-1), fc1_bias]), 'col', a...]
    reduce_scatter x2, waiting for transfers between devices: 11.4 us -> 20.5 us  [sum_columns(): return lax.psum_scatter(values, 'col', scatter_dimension=0, tiled=False)]
    all_to_all x2 -> x0, starting transfers between devices: 8.74 us -> none  [spread_rows(): moved = lax.all_to_all(values, 'row', 0, 0, tiled=True)]
    all_gather x3 -> x0, local copies, waits for them, and re-layouts: 7.65 us -> none  [the longest x2 7.64 us: over_row(): return lax.all_gather(values, 'row', axis=1, tiled=True)]
    unnamed x82 -> x58, local copies, waits for them, and re-layouts: 24.4 us -> 20.5 us
    pallas_call x6 -> x7, Pallas kernels: 475 us -> 474 us  [the longest x1 124 us: attention(): pl.pallas_call(partial(attend_kernel, images), in_specs=[*[vmem] * 4, pl....]
  transfers between devices with their start and end apart: 9 -> 2, of which waited for: 6 -> 1; matrix products, arithmetic and copies ran while one was open for 8% -> 4% of each run, Pallas kernels for 52% -> 28%
where the time goes in v4:
time: 588 us; the launch traced here: 579 us
  Pallas kernels  474 us (81%)
  local copies, waits for them, and re-layouts  48 us (8%)
  waiting for transfers between devices  20.5 us (3%)
  matrix products  17.8 us (3%)
  between operations  14.9 us (3%)
    pallas_call x1, Pallas kernels, attention(): pl.pallas_call(partial(attend_kernel, images), in_specs=[*[vmem] * 4, pl....  124 us
    pallas_call x1, Pallas kernels, attention_back(): pl.pallas_call(partial(attend_back_kernel, images), in_specs=[*[vmem] * 9...  116 us
    pallas_call x2, Pallas kernels, row_mix(): pl.pallas_call(partial(row_mix_kernel, finish, len(extra), 1 + len(outs),...  80.8 us
    pallas_call x1, Pallas kernels, tail(): pl.pallas_call(partial(tail_kernel, axes), in_specs=[vmem] * 11, out_spec...  80.3 us
    pallas_call x1, Pallas kernels, start(): pl.pallas_call(partial(start_kernel, lax.axis_size('batch')), in_specs=[v...  60.8 us
    unnamed x58, local copies, waits for them, and re-layouts  20.5 us
    reduce_scatter x2, waiting for transfers between devices, sum_columns(): return lax.psum_scatter(values, 'col', scatter_dimension=0, tiled=False)  20.5 us
    dot_general x2, matrix products, contract_rows(): lax.dot_general(left, right, (((0,), (0,)), ((), ())), preferred_element_...  12.1 us
  transfers between devices with their start and end apart: 2, of which 1 were waited for; matrix products, arithmetic and copies ran while one was open for 4% of the time, Pallas kernels for 28%

profile of v4, /device:TPU:8, one launch (start us, length us, event | category | flops | bytes accessed | tf_op | source)
XLA Modules:
  0.0 579.4 jit_solution(11896808538590981198)
XLA Ops:
  13.2 1.5 copy.57
  15.1 1.6 copy.59
  16.7 2.2 copy.60
  19.0 2.8 pad_maximum_fusion.rest_ref
  21.8 60.8 %start.1 = (bf16[4,240,1024]{2,1,0:T(8,128)(2,1)S(1)}, bf16[1024,1280]{1,0:T(8,128)(2,1)}, bf16[256,1280]{1,0:T(8,128)(2,1)S(1)}, bf16[4,240,1280]{2,1,0:T(8,128...) custom-call(bf16[1024,320]{1,0:T(8,128)(2,1)S(1)} %bitcast.67, ...), custom_call_target="tpu_custom_call" | custom-call | tf_op jit(solution)/shard_map/start/pallas_call | solution.py:316
  82.6 1.4 copy-done.7
  85.7 1.5 copy.61
  87.3 124.5 %attend.1 = (bf16[4,80,1024]{2,1,0:T(8,128)(2,1)S(1)}, bf16[4,240,1024]{2,1,0:T(8,128)(2,1)}, f32[4,80,1024]{2,1,0:T(8,128)S(1)}, f32[4,8,1024]{2,1,0:T(8,128)S(...) custom-call(bf16[4,240,1024]{2,1,0:T(8,128)(2,1)} %copy-done.7, ...), custom_call_target="tpu_custom_call" | custom-call | flops 17179869184 | bytes 3932160 | tf_op jit(solution)/shard_map/attend/pallas_call | solution.py:1276
  211.9 37.5 %middle_and_norm2.1 = (bf16[4,256,1280]{2,1,0:T(8,128)(2,1)S(1)}, f32[256,1280]{1,0:T(8,128)S(1)}, bf16[2,4,320,1280]{3,2,1,0:T(8,128)(2,1)}) custom-call(bf16[320,1024]{1,0:T(8,128)(2,1)S(1)} %bitcast.75, bf16[320,1280]{1,0:T(8,128)(2,1)S(1)} %bitcast.73, f32[3,1280]{1,0:T(4,128)S(1)} %slice.75.refs_0_, ...), custom_call_target="tpu_custom_call", output_to_operand_aliasing={{2}: (4, {})} | custom-call | flops 3355443200 | bytes 5242880 | tf_op jit(solution)/shard_map/middle_and_norm2/pallas_call | solution.py:959
  249.5 11.1 %feed_forward.1 = (bf16[1024,1280]{1,0:T(8,128)(2,1)S(1)}, bf16[1024,1280]{1,0:T(8,128)(2,1)S(1)}, f32[1,1280]{1,0:T(1,128)S(1)}) custom-call(bf16[1024,1280]{1,0:T(8,128)(2,1)S(1)} %bitcast.71, bf16[2,1280,1280]{2,1,0:T(8,128)(2,1)} %bitcast.78, f32[1,1280]{1,0:T(1,128)S(1)} %broadcast_in_dim_reshape_squeeze.3.bias_ref, bf16[1024,1280]{1,0:T(8,128)(2,1)S(1)} %copy-done.5, ...), custom_call_target="tpu_custom_call" | custom-call | flops 6710886400 | bytes 17039360 | tf_op jit(solution)/shard_map/feed_forward/pallas_call | solution.py:1251
  260.6 5.1 convolution_convert_fusion.1
  266.3 1.1 constant_dynamic-slice_fusion.1.refs_2_
  267.5 7.0 %convolution_convert_fusion = bf16[1280,1280]{1,0:T(8,128)(2,1)} fusion(bf16[1024,1280]{1,0:T(8,128)(2,1)S(1)} %get-tuple-element.71.left_ref, bf16[1024,1280]{1,0:T(8,128)(2,1)} %bitcast.72), kind=kOutput, calls=%fused_computation | convolution fusion | flops 3357081600 | bytes 8519680 | tf_op jit(solution)/shard_map/dot_general | solution.py:1434
  274.4 43.3 %middle_grad.1 = (bf16[4,256,1280]{2,1,0:T(8,128)(2,1)}, f32[256,1280]{1,0:T(8,128)S(1)}, f32[3,1280]{1,0:T(4,128)S(1)}, bf16[4,160,1280]{2,1,0:T(8,128)(2,1)}) custom-call(bf16[1024,1280]{1,0:T(8,128)(2,1)} %copy-done, bf16[2,1280,1280]{2,1,0:T(8,128)(2,1)} %bitcast.80, f32[3,1280]{1,0:T(4,128)S(1)} %slice.75.refs_0_, f32[256,1280]{1,0:T(8,128)S(1)} %copy-done.2, ...), custom_call_target="tpu_custom_call" | custom-call | flops 3355443200 | bytes 5242880 | tf_op jit(solution)/shard_map/middle_grad/pallas_call | solution.py:959
  317.7 1.0 copy-done.3
  319.9 3.9 convolution_convert_fusion.2
  323.8 1.9 convolution_convert_fusion.3
  326.2 20.5 %reduce-scatter.3.cloned.1.call-done = bf16[1,320,1280]{2,1,0:T(8,128)(2,1)} async-done(((bf16[4,320,1280]{2,1,0:T(8,128)(2,1)}), bf16[1,320,1280]{2,1,0:T(8,128)(2,1)}) %reduce-scatter.3.cloned.1.call-update) | async-done | bytes 819216 | tf_op jit(solution)/shard_map/reduce_scatter | solution.py:1437
  346.7 116.2 %attend_back.1 = (bf16[4,240,1024]{2,1,0:T(8,128)(2,1)}, f32[80,256]{1,0:T(8,128)}, f32[2,128]{1,0:T(2,128)}, f32[4,80,320]{2,1,0:T(8,128)}, f32[4,320,320]{2,1,0:T(8,128)}, /*index=5*/bf16[1024,320]{1,0:T(8,128)(2,1)}) custom-call(bf16[4,240,1024]{2,1,0:T(8,128)(2,1)} %get-tuple-element.59.qkv_ref, bf16[256,80]{1,0:T(8,128)(2,1)} %copy-done.6, ...), custom_call_target="tpu_custom_call" | custom-call | flops 42949672960 | bytes 7864320 | tf_op jit(solution)/shard_map/attend_back/pallas_call | solution.py:1320
  463.0 2.2 copy.65
  465.2 3.0 copy.68
  468.2 80.3 %tail.1 = (f32[1024,320]{1,0:T(8,128)}, f32[3,320,320]{2,1,0:T(8,128)}, f32[1280,320]{1,0:T(8,128)}, f32[296,128]{1,0:T(8,128)}) custom-call(bf16[960,1024]{1,0:T(8,128)(2,1)} %bitcast.77, bf16[4,240,1024]{2,1,0:T(8,128)(2,1)} %get-tuple-element.84.grads_ref, bf16[960,1280]{1,0:T(8,128)(2,1)} %bitcast.87, bf16[1024,1280]{1,0:T(8,128)(2,1)} %get-tuple-element.86.normed1_ref, ...), custom_call_target="tpu_custom_call" | custom-call | tf_op jit(solution)/shard_map/tail/pallas_call | solution.py:1194
  548.5 1.5 slice.79
  550.7 1.5 slice_bitcast_fusion
  553.0 2.9 copy.66
  559.5 1.3 dynamic_slice.47
  561.6 1.3 dynamic_slice.45
  562.9 1.3 dynamic_slice.44
  564.3 1.3 dynamic_slice.43
  565.6 1.3 dynamic_slice.42
  568.3 1.7 copy.67
  570.0 1.1 copy.74
  (104 shorter events, 18.9 us)
Async XLA Ops:
  7.2 7.6 %copy-start.18 = (bf16[1,1024,320]{1,2,0:T(8,128)(2,1)S(1)}, bf16[1,1024,320]{1,2,0:T(8,128)(2,1)}, u32[]{:S(2)}) copy-start(bf16[1,1024,320]{1,2,0:T(8,128)(2,1)} %param.16) | copy-start | bytes 1966084
  7.2 339.5 %reduce-scatter.3.cloned.1.call-start = ((), (), s32[]{:S(2)}) async-start(), calls=%async_computation.2 | async-start | bytes 4096000 | tf_op jit(solution)/shard_map/reduce_scatter | solution.py:1437
  14.8 4.2 copy-start.20
  82.6 1.4 copy-start.7
  84.0 127.9 %copy-start.4 = (bf16[256,1280]{1,0:T(8,128)(2,1)}, bf16[256,1280]{1,0:T(8,128)(2,1)S(1)}, u32[]{:S(2)}) copy-start(bf16[256,1280]{1,0:T(8,128)(2,1)S(1)} %get-tuple-element.63.refs_1_.first_ref) | copy-start | bytes 1966084
  84.0 0.7 copy-start.21
  84.0 0.8 copy-start.22
  85.7 126.1 %copy-start.6 = (bf16[256,80]{1,0:T(8,128)(2,1)}, bf16[256,80]{1,0:T(8,128)(2,1)S(1)}, u32[]{:S(2)}) copy-start(bf16[256,80]{1,0:T(8,128)(2,1)S(1)} %copy.62.tab_ref) | copy-start | bytes 122884
  211.8 37.6 %copy-start.9 = (bf16[4,80,1280]{2,1,0:T(8,128)(2,1)}, bf16[4,80,1280]{2,1,0:T(8,128)(2,1)S(1)}, u32[]{:S(2)}) copy-start(bf16[4,80,1280]{2,1,0:T(8,128)(2,1)S(1)} %get-tuple-element.60) | copy-start | bytes 2457604
  211.8 37.6 %copy-start.11 = (bf16[4,80,1024]{2,1,0:T(8,128)(2,1)}, bf16[4,80,1024]{2,1,0:T(8,128)(2,1)S(1)}, u32[]{:S(2)}) copy-start(bf16[4,80,1024]{2,1,0:T(8,128)(2,1)S(1)} %get-tuple-element.61) | copy-start | bytes 1966084
  211.8 37.6 %copy-start.14 = (f32[4,80,1024]{2,1,0:T(8,128)}, f32[4,80,1024]{2,1,0:T(8,128)S(1)}, u32[]{:S(2)}) copy-start(f32[4,80,1024]{2,1,0:T(8,128)S(1)} %get-tuple-element.79.exact_ref) | copy-start | bytes 3932164
  211.8 37.6 %copy-start.15 = (f32[4,8,1024]{2,1,0:T(8,128)}, f32[4,8,1024]{2,1,0:T(8,128)S(1)}, u32[]{:S(2)}) copy-start(f32[4,8,1024]{2,1,0:T(8,128)S(1)} %get-tuple-element.80.stat_ref) | copy-start | bytes 393220
  211.8 37.6 %copy-start.5 = (bf16[1024,1280]{1,0:T(8,128)(2,1)S(1)}, bf16[1024,1280]{1,0:T(8,128)(2,1)}, u32[]{:S(2)}) copy-start(bf16[1024,1280]{1,0:T(8,128)(2,1)} %get-tuple-element.68.cot_ref) | copy-start | bytes 7864324
  249.4 11.1 %copy-start.1 = (f32[256,1280]{1,0:T(8,128)}, f32[256,1280]{1,0:T(8,128)S(1)}, u32[]{:S(2)}) copy-start(f32[256,1280]{1,0:T(8,128)S(1)} %get-tuple-element.72.refs_1_.middle_ref) | copy-start | bytes 3932164
  249.4 11.1 %copy-start.8 = (bf16[4,256,1280]{2,1,0:T(8,128)(2,1)}, bf16[4,256,1280]{2,1,0:T(8,128)(2,1)S(1)}, u32[]{:S(2)}) copy-start(bf16[4,256,1280]{2,1,0:T(8,128)(2,1)S(1)} %get-tuple-element.65) | copy-start | bytes 7864324
  260.6 5.1 copy-start.13
  260.6 6.9 %copy-start = (bf16[1024,1280]{1,0:T(8,128)(2,1)}, bf16[1024,1280]{1,0:T(8,128)(2,1)S(1)}, u32[]{:S(2)}) copy-start(bf16[1024,1280]{1,0:T(8,128)(2,1)S(1)} %get-tuple-element.71.left_ref) | copy-start | bytes 7864324
  265.7 202.5 %reduce-scatter.5.cloned.1.call-start = ((), (), s32[]{:S(2)}) async-start(), calls=%async_computation.3 | async-start | bytes 2048000 | tf_op jit(solution)/shard_map/reduce_scatter | solution.py:1437
  267.4 7.0 %copy-start.2 = (f32[256,1280]{1,0:T(8,128)S(1)}, f32[256,1280]{1,0:T(8,128)}, u32[]{:S(2)}) copy-start(f32[256,1280]{1,0:T(8,128)} %copy-done.1) | copy-start | bytes 3932164
  274.4 45.4 %copy-start.12 = (bf16[4,80,1024]{2,1,0:T(8,128)(2,1)S(1)}, bf16[4,80,1024]{2,1,0:T(8,128)(2,1)}, u32[]{:S(2)}) copy-start(bf16[4,80,1024]{2,1,0:T(8,128)(2,1)} %copy-done.11) | copy-start | bytes 1966084
  317.7 1.1 copy-start.3
  319.9 3.9 copy-start.10
  319.9 3.9 copy-start.23
  548.5 19.8 %copy-start.16 = (f32[1280,320]{1,0:T(8,128)S(1)}, f32[1280,320]{1,0:T(8,128)}, u32[]{:S(2)}) copy-start(f32[1280,320]{1,0:T(8,128)} %get-tuple-element.96) | copy-start | bytes 4915204
  555.9 14.1 %copy-start.17 = (f32[3,320,320]{2,1,0:T(8,128)S(1)}, f32[3,320,320]{2,1,0:T(8,128)}, u32[]{:S(2)}) copy-start(f32[3,320,320]{2,1,0:T(8,128)} %get-tuple-element.93) | copy-start | bytes 3686404
  570.0 1.4 copy-start.19
Sparse Core Ops, SparseCore 0:
  265.8 80.8 reduce-scatter.2
  349.0 72.6 reduce-scatter.4

commit v5 on v4

--- a/solution.py
+++ b/solution.py
@@ -194,11 +194,14 @@
     return chains, swapped if shared else None
 
 
-HALF = 128
+HALF = 2 * HEAD_DIM
 
 
 def half_start(image):
-    return pl.multiple_of(image * (3 * HEAD_DIM - HALF), 16)
+    return pl.multiple_of(image * (3 * HEAD_DIM - HALF_GRAD), 16)
+
+
+HALF_GRAD = 128
 
 
 def row_copy(source, target, sems, kind, order, peer):
@@ -216,10 +219,14 @@
     return jnp.concatenate([block.astype(F32) for block in blocks], 1)
 
 
+def upright(blocks):
+    return jnp.concatenate([block.astype(F32) for block in blocks], 0).T
+
+
 def start_kernel(
-    images, patches_ref, qkv_ref, rest_ref, vector_ref, column_ref,
-    qkv_out, normed_out, first_out, weight_out, rest_out, vectors_out, columns_out,
-    patches_all, qkv_parts, rest_parts, vector_parts, halves, sems, col_sems, chain_sems, swap_sems,
+    images, patches_ref, qkv_ref, proj_ref, fc1_ref, fc2_ref, vector_ref, column_ref,
+    qkv_out, normed_out, first_out, weight_out, proj_out, rest_out, vectors_out, columns_out,
+    patches_all, parts, rest_parts, vector_parts, halves, sems, col_sems, chain_sems, swap_sems,
 ):
     row, col, image = lax.axis_index("row"), lax.axis_index("col"), lax.axis_index("batch")
     near, far, diag = row_peers()
@@ -231,29 +238,31 @@
         ("batch", image_peers(images) if shared else ()),
     )
 
-    def to_row(source, parts, kind):
-        copies = [row_copy(source(peer), parts.at[row], sems, kind, i, peer) for i, peer in enumerate((near, far, diag))]
+    def to_row(source, target, kind):
+        copies = [row_copy(source(peer), target, sems, kind, i, peer) for i, peer in enumerate((near, far, diag))]
         for copy in copies:
             copy.start()
         return copies
 
-    qkv_copies = to_row(lambda peer: qkv_ref.at[peer], qkv_parts, 0)
-    vector_copies = to_row(lambda peer: vector_ref, vector_parts, 1)
+    n, units = 3 * HEAD_DIM, fc1_ref.shape[1]
+    weight_copies = to_row(lambda peer: qkv_ref.at[peer], parts.at[row, 0:n], 0)
+    weight_copies += to_row(lambda peer: proj_ref.at[peer], parts.at[row, n : n + HEAD_DIM], 4)
+    vector_copies = to_row(lambda peer: vector_ref, vector_parts.at[row], 1)
     to_near = row_copy(patches_ref, patches_all.at[row], sems, 2, 0, near)
     to_far = row_copy(patches_ref, patches_all.at[row], sems, 2, 1, far)
     to_near.start()
     column_copies = [col_copy(column_ref, columns_out.at[col], col_sems, 0, step) for step in range(1, 4)]
     for copy in column_copies:
         copy.start()
-    qkv_parts[row] = qkv_ref[row]
+    parts[row, 0:n] = qkv_ref[row]
+    parts[row, n : n + HEAD_DIM] = proj_ref[row]
     vector_parts[row] = vector_ref[...]
     patches_all[row] = patches_ref[...]
     columns_out[col] = column_ref[...]
-    for copy in qkv_copies:
+    for copy in weight_copies:
         copy.wait()
     to_far.start()
-    weight = beside([qkv_parts[i] for i in range(4)]).astype(BF16)
-    weight_out[col] = weight
+    weight = beside([parts[i] for i in range(4)]).astype(BF16)
 
     def swap_copy(block, way, hop):
         return image_copy(halves.at[image, block], halves.at[image, block], swap_sems, way, hop - 1)
@@ -261,95 +270,104 @@
     def swap(block, way, hop):
         swap_copy(block, way, hop).start()
 
-    if shared:
-        halves[0, col] = weight[:HALF]
-        halves[1, col] = weight[3 * HEAD_DIM - HALF :]
-        chain = Chain(lambda i: halves.at[image, i], chain_sems, swap)
-    else:
-        chain = Chain(lambda i: weight_out.at[i], chain_sems)
+    halves[0, col] = weight[:HALF]
+    halves[1, col] = weight[HALF:]
+    orders = [image] if shared else [0, 1]
+    chains = [
+        Chain(lambda i, which=which: halves.at[which, i], chain_sems.at[order], swap if shared else None)
+        for order, which in enumerate(orders)
+    ]
 
     def product(block, way=0, hop=0):
         if hop and shared:
             swap_copy(block, way, hop).wait()
-            weight_out[block, 0 : 3 * HEAD_DIM - HALF] = halves[0, block, 0 : 3 * HEAD_DIM - HALF]
-            weight_out[block, 3 * HEAD_DIM - HALF :] = halves[1, block]
-        bias = jnp.concatenate([columns_out[block][:, 0:256]] * 16, 0).T[: 3 * HEAD_DIM, 0:1]
+        weight_out[block, 0:HALF] = halves[0, block]
+        weight_out[block, HALF:] = halves[1, block, 0 : n - HALF]
+        proj_out[block] = halves[1, block, n - HALF :]
+        bias = jnp.concatenate([columns_out[block][:, 0:256]] * 16, 0).T[:n, 0:1]
         qkv_out[block] = (mm_nt(weight_out[block], normed_out[...]) + bias).astype(BF16)
 
-    chain.begin()
+    for chain in chains:
+        chain.begin()
     for copy in vector_copies + column_copies:
         copy.wait()
     vectors_out[...] = beside([vector_parts[i] for i in range(4)])
     to_far.wait_recv()
     pass_on = row_copy(patches_all.at[far], patches_all.at[far], sems, 2, 2, near)
     pass_on.start()
-    rest_copies = to_row(lambda peer: rest_ref.at[peer], rest_parts, 3)
-    rest_parts[row] = rest_ref[row]
-    chain.hop(1)
+    rest_copies = to_row(lambda peer: fc1_ref.at[peer], rest_parts.at[row, 0:units], 3)
+    rest_copies += to_row(lambda peer: fc2_ref.at[peer], rest_parts.at[row, units : 2 * units], 5)
+    rest_parts[row, 0:units] = fc1_ref[row]
+    rest_parts[row, units : 2 * units] = fc2_ref[row]
+    for chain in chains:
+        chain.hop(1)
     to_near.wait_recv()
     pass_on.wait_recv()
     for start in range(0, normed_out.shape[0], own):
-        rows = slice(start, start + own)
-        scaled, _ = normal(beside([patches_all[i, rows] for i in range(4)]))
-        normed_out[rows] = (scaled * vectors_out[0:1] + vectors_out[1:2]).astype(BF16)
-    chain.hop(2)
+        scaled, _ = normal(upright([patches_all[i, :, start : start + own] for i in range(4)]))
+        normed_out[start : start + own] = (scaled * vectors_out[0:1] + vectors_out[1:2]).astype(BF16)
+    for chain in chains:
+        chain.hop(2)
     product(col)
-    chain.each(1, product)
-    chain.hop(3)
-    chain.each(2, product)
-    rows = pl.ds(pl.multiple_of(row * own, own), own)
-    first_out[...] = beside([patches_all[i, rows] for i in range(4)]).astype(BF16)
+    chains[0].each(1, product)
+    for chain in chains:
+        chain.hop(3)
+    chains[0].each(2, product)
+    mine = pl.ds(pl.multiple_of(row * own, own), own)
+    first_out[...] = upright([patches_all[i, :, mine] for i in range(4)]).astype(BF16)
     for copy in rest_copies:
         copy.wait()
     rest_out[...] = beside([rest_parts[i] for i in range(4)]).astype(BF16)
-    chain.each(3, product)
-    chain.end()
+    chains[0].each(3, product)
+    for chain in chains:
+        chain.end()
     for copy in (to_near, to_far, pass_on):
         copy.wait_send()
 
 
-def start(patches, local_qkv, local_rest, vectors, columns):
-    width, part = patches.shape
+def start(patches, local_qkv, local_proj, local_fc1, local_fc2, vectors, columns):
+    part, width = patches.shape
     n, model = local_qkv.shape[1], part * 4
-    rest = local_rest.shape[1]
+    rest = local_fc1.shape[1] + local_fc2.shape[1]
     vmem = pl.BlockSpec(memory_space=pltpu.VMEM)
     return pl.pallas_call(
         partial(start_kernel, lax.axis_size("batch")),
-        in_specs=[vmem] * 5,
-        out_specs=[vmem] * 7,
+        in_specs=[vmem] * 7,
+        out_specs=[vmem] * 8,
         out_shape=[
             jax.ShapeDtypeStruct((4, n, width), BF16),
             jax.ShapeDtypeStruct((width, model), BF16),
             jax.ShapeDtypeStruct((width // 4, model), BF16),
             jax.ShapeDtypeStruct((4, n, model), BF16),
+            jax.ShapeDtypeStruct((4, HEAD_DIM, model), BF16),
             jax.ShapeDtypeStruct((rest, model), BF16),
             jax.ShapeDtypeStruct((vectors.shape[0], model), F32),
             jax.ShapeDtypeStruct((4, *columns.shape), F32),
         ],
         scratch_shapes=[
-            pltpu.VMEM((4, width, part), BF16),
-            pltpu.VMEM((4, n, part), BF16),
+            pltpu.VMEM((4, part, width), BF16),
+            pltpu.VMEM((4, n + HEAD_DIM, part), BF16),
             pltpu.VMEM((4, rest, part), BF16),
             pltpu.VMEM((4, *vectors.shape), F32),
             pltpu.VMEM((2, 4, HALF, model), BF16),
-            pltpu.SemaphoreType.DMA((2, 4, 3)),
+            pltpu.SemaphoreType.DMA((2, 6, 3)),
             pltpu.SemaphoreType.DMA((2, 1, 4)),
-            pltpu.SemaphoreType.DMA((2, 2, 3)),
+            pltpu.SemaphoreType.DMA((2, 2, 2, 3)),
             pltpu.SemaphoreType.DMA((2, 2, 3)),
         ],
         compiler_params=pltpu.CompilerParams(
             collective_id=7, has_side_effects=True, vmem_limit_bytes=48 << 20
         ),
         name="start",
-    )(patches, local_qkv, local_rest, vectors, columns)
-
-
-CHAIN_TURNS = (4, 9)
+    )(patches, local_qkv, local_proj, local_fc1, local_fc2, vectors, columns)
+
+
+CHAIN_TURNS = (6, 12)
 
 
 def attend_kernel(
-    images, given_ref, tab_ref, proj_ref, cot_ref, weight_ref,
-    merged_ref, qkv_ref, exact_ref, stat_ref, proj_all_ref, cot_out, weight_all,
+    images, given_ref, tab_ref, cot_ref, weight_ref,
+    merged_ref, qkv_ref, exact_ref, stat_ref, cot_out, weight_all,
     kaug, columns, acc, top, total, box, sems, cot_parts, cot_sems, local_sems, chain_sems, swap_sems,
 ):
     me = lax.axis_index("col")
@@ -375,9 +393,6 @@
     def merged_copy(step):
         return col_copy(box.at[col_peer(step)], merged_ref.at[me], sems, 1, step)
 
-    def proj_copy(step):
-        return col_copy(proj_ref, proj_all_ref.at[me], sems, 2, step)
-
     for step in (2, 1):
         part_copy(step).start()
     to_near = row_copy(cot_ref, cot_parts.at[row], cot_sems, 0, 0, near)
@@ -387,7 +402,6 @@
     to_near.start()
     cot_parts[row] = cot_ref[...]
     qkv_ref[me] = given_ref[me]
-    proj_all_ref[me] = proj_ref[...]
 
     pad = jnp.zeros((128 - HEAD_DIM, width), F32)
     token = lax.broadcasted_iota(jnp.int32, (width, 2 * GRID), 0)
@@ -432,9 +446,12 @@
         def _():
             prepare(col_peer(newest))
 
+        @pl.when(turn == 1)
+        def _():
+            part_copy(3).start()
+
         @pl.when(turn == CHAIN_TURNS[0])
         def _():
-            part_copy(3).start()
             for chain in chains:
                 chain.begin()
 
@@ -442,8 +459,6 @@
         def _():
             for chain in chains:
                 chain.hop(1)
-            for step in range(1, 4):
-                proj_copy(step).start()
             to_far.wait_recv()
             pass_on.start()
 
@@ -483,7 +498,7 @@
     pass_on.wait_recv()
     for start in range(0, width, QUERIES):
         rows = slice(start, start + QUERIES)
-        cot_out[rows] = beside([cot_parts[i, rows] for i in range(4)]).astype(BF16)
+        cot_out[rows] = upright([cot_parts[i, :, rows] for i in range(4)]).astype(BF16)
     merged_ref[me] = box[me]
     for chain in chains:
         chain.end((1, 2))
@@ -493,19 +508,18 @@
         copy.wait_send()
     for step in range(1, 4):
         part_copy(step).wait_send()
-        proj_copy(step).wait()
         merged_copy(step).wait()
 
 
-GRADS, QUERY_OUT, KEY_OUT, PROJ_OUT = range(4)
+GRADS, QUERY_OUT, KEY_OUT = range(3)
 KEY_ROWS = slice(HEAD_DIM, 3 * HEAD_DIM)
 
 
 def attend_back_kernel(
-    images, qkv_ref, tab_ref, tab_t_ref, given_ref, exact_ref, stat_ref, proj_ref, fc2_ref,
+    images, qkv_ref, tab_ref, tab_t_ref, given_ref, exact_ref, stat_ref, fc2_ref,
     activated_ref, weights_ref, middle_ref, bias_fc2_ref,
-    out_ref, tab_grad_ref, bias_out, proj_out, fc2_out, block_out,
-    held, held_sem, bias_ref, proj_rows, proj_box, grads, kaug, kaug_t, vaug, key_sum, value_sum, spread, columns,
+    out_ref, tab_grad_ref, bias_out, fc2_out, block_out,
+    held, held_sem, bias_ref, grads, kaug, kaug_t, vaug, key_sum, value_sum, spread, columns,
     grad_columns, grad_rows, q_rows, box, sems, *weight_parts,
 ):
     me = lax.axis_index("col")
@@ -519,19 +533,15 @@
         ("batch", image_peers(images) if images == 2 else ()),
     )
 
-    def write_proj(place, values):
-        proj_out[place] = values
-
     def write_fc2(place, values):
         fc2_out[place] = values
 
     fc2 = weight_steps(fc2_ref, images, weight_parts[:4], write_fc2)
-    proj = weight_steps(proj_rows, images, weight_parts[4:8], write_proj)
 
     def finish_block(total, piece, rows):
         return middle_ref[rows] + (total + bias_fc2_ref[0:1])
 
-    block = row_mix_steps(activated_ref, held, block_out, finish_block, False, True, weight_parts[8:])
+    block = row_mix_steps(activated_ref, held, block_out, finish_block, False, True, weight_parts[4:])
 
     def grad_copy(step):
         return col_copy(given_ref.at[col_peer(step)], grads.at[me], sems, GRADS, step)
@@ -543,15 +553,11 @@
     def key_copy(step):
         at = col_peer(step)
         return col_copy(box.at[at, KEY_ROWS], out_ref.at[me, KEY_ROWS], sems, KEY_OUT, step)
-
-    def proj_copy(step):
-        return col_copy(proj_ref.at[col_peer(step)], proj_box.at[me], sems, PROJ_OUT, step)
 
     for step in range(1, 4):
         grad_copy(step).start()
     next(fc2)
     grads[me] = given_ref[me]
-    proj_box[me] = proj_ref[me]
 
     tail_row = lax.broadcasted_iota(jnp.int32, (128 - HEAD_DIM, width), 0)
     pad = jnp.where(tail_row < 3, 1.0, 0.0)
@@ -640,11 +646,6 @@
         def _():
             prepare(q_part)
 
-        @pl.when(turn == 7)
-        def _():
-            for step in range(1, 4):
-                proj_copy(step).start()
-
         for block in range(blocks):
             at = slice(block * QUERIES, (block + 1) * QUERIES)
             total = None
@@ -688,23 +689,13 @@
     lax.fori_loop(4, 8, pair, 0)
     next(fc2)
     next(block, None)
-    lax.fori_loop(8, 12, pair, 0)
-    for step in range(1, 4):
-        proj_copy(step).wait()
-    total = proj_box[0].astype(F32)
-    for source in range(1, 4):
-        total = total + proj_box[source].astype(F32)
-    proj_rows[...] = total.astype(BF16)
-    next(proj)
+    lax.fori_loop(8, 16, pair, 0)
     next(fc2, None)
-    lax.fori_loop(12, 16, pair, 0)
-    next(proj)
     out_ref[me] = box[me]
     for step in range(1, 4):
         grad_copy(step).wait_send()
         query_copy(step).wait()
         key_copy(step).wait()
-    next(proj, None)
     bias_out[0:1] = bias_ref[0:128].T[0:1]
     bias_out[1:2] = bias_ref[2 * HEAD_DIM : 2 * HEAD_DIM + 128].T[0:1]
 
@@ -825,7 +816,7 @@
         result = finish(total, piece, rows)
         if to_features:
             boxes, arrived = more
-            part = gathered.shape[1]
+            part = gathered.shape[0]
             for place in range(4):
                 boxes[place, rows] = result[:, place * part : (place + 1) * part].astype(BF16)
             arrived[me, rows] = boxes[me, rows]
@@ -847,7 +838,7 @@
     if to_features:
         boxes, arrived = more
         for source in range(4):
-            gathered[source * own : (source + 1) * own, :] = arrived[source].astype(gathered.dtype)
+            gathered[:, source * own : (source + 1) * own] = arrived[source].astype(F32).T.astype(gathered.dtype)
     for copy in started:
         copy.wait_send()
 
@@ -904,11 +895,11 @@
     if len(weight_ref.shape) == 3:
         copy.wait()
         weight_ref = held
-    for _ in row_mix_steps(left_ref, weight_ref, gathered, last, left_t, False, scratch):
-        pass
+    for stage, _ in enumerate(row_mix_steps(left_ref, weight_ref, gathered, last, left_t, False, scratch)):
+        if images and stage == 3:
+            for chain in chains:
+                chain.hop(3)
     if images:
-        for chain in chains:
-            chain.hop(3)
         for chain in chains:
             chain.end((3,))
             if swapped:
@@ -1110,12 +1101,13 @@
 def tail_kernel(
     axes,
     qkv_grad_ref, grads_ref, weight_qkv_ref, normed1_ref, first_ref, middle_grad_ref, gain_ref,
-    fc1_ref, early_ref, table_ref, bias_ref, patches_out, qkv_out, fc1_out, small,
+    fc1_ref, proj_ref, early_ref, table_ref, bias_ref, patches_out, qkv_out, fc1_out, proj_out, small,
     *scratch,
 ):
     sums1, qkv_rows, *scratch = scratch
     col_scratch, scratch = scratch[:7], scratch[7:]
-    mix, qkv_scratch, fc1_scratch, sum_parts = scratch[:7], scratch[7:11], scratch[11:15], scratch[15:]
+    mix, qkv_scratch, fc1_scratch, sum_parts = scratch[:7], scratch[7:11], scratch[11:15], scratch[15:20]
+    proj_rows, proj_box, proj_sems, *proj_scratch = scratch[20:]
     row, col = lax.axis_index("row"), lax.axis_index("col")
     images = dict(axes)["batch"]
     meet(
@@ -1138,12 +1130,30 @@
             fc1_out[pl.ds(pl.multiple_of((2 * place + image) * n, 8), n)] = values
             fc1_out[pl.ds(pl.multiple_of((2 * place + 1 - image) * n, 8), n)] = others
 
+    def write_proj(place, values):
+        proj_out[place] = values
+
+    def proj_steps():
+        copies = []
+        for step in range(1, 4):
+            copies.append(col_copy(proj_ref.at[col_peer(step)], proj_box.at[col], proj_sems, 0, step))
+            copies[-1].start()
+        proj_box[col] = proj_ref[col]
+        yield
+        for copy in copies:
+            copy.wait()
+        total = proj_box[0].astype(F32)
+        for source in range(1, 4):
+            total = total + proj_box[source].astype(F32)
+        proj_rows[...] = total.astype(BF16)
+        yield from weight_steps(proj_rows, images, proj_scratch, write_proj)
+
     head_grads = []
 
     def write_qkv(place, values, others=None):
         if others is not None:
             first, second = jnp.where(image == 0, values, others), jnp.where(image == 0, others, values)
-            values = jnp.concatenate([first[: 3 * HEAD_DIM - HALF], second], 0)
+            values = jnp.concatenate([first[: 3 * HEAD_DIM - HALF_GRAD], second], 0)
         head_grads.append(values)
 
     qkv_sum = column_steps(images, grads_ref, normed1_ref, qkv_rows, col_scratch)
@@ -1156,7 +1166,8 @@
         for step in steps:
             next(step, None)
 
-    go(qkv_sum, patches, patches, patches, qkv_sum, patches)
+    proj = proj_steps()
+    go(proj, qkv_sum, patches, patches, patches, proj, qkv_sum, patches)
 
     small[0:EARLY_ROWS] = early_ref[...]
     at = EARLY_ROWS
@@ -1173,32 +1184,33 @@
     spare = jnp.zeros((LAST_ROWS - len(last), 128), F32)
     small[at : at + LAST_ROWS] = jnp.concatenate([*last, spare], 0)
 
-    go(sums, fc1, qkv_sum, qkv, sums, patches, fc1, sums, qkv, fc1, sums, qkv)
+    go(sums, fc1, proj, qkv_sum, qkv, sums, patches, fc1, proj, sums, qkv, fc1, sums, qkv)
     for kind in range(3):
         rows = slice(kind * HEAD_DIM, (kind + 1) * HEAD_DIM)
         qkv_out[kind] = jnp.concatenate([values[rows] for values in head_grads], 0).T
 
 
 def tail(
-    qkv_grad, weight_qkv, normed1, first, middle_grad, gain, fc1, early, table, bias
+    qkv_grad, weight_qkv, normed1, first, middle_grad, gain, fc1, proj, early, table, bias
 ):
     cols, n, tokens = qkv_grad.shape
     model = weight_qkv.shape[1]
     own, part = tokens // 4, model // 4
     shared = lax.axis_size("batch") == 2
-    rows = HALF if shared else n
+    rows = HALF_GRAD if shared else n
     units = fc1.shape[0] * (2 if shared else 1)
     axes = tuple((name, lax.axis_size(name)) for name in ("row", "batch", "col"))
     small_rows = EARLY_ROWS + TABLE_ROWS + BIAS_ROWS + LAST_ROWS
     vmem = pl.BlockSpec(memory_space=pltpu.VMEM)
     return pl.pallas_call(
         partial(tail_kernel, axes),
-        in_specs=[vmem] * 11,
-        out_specs=[vmem] * 4,
+        in_specs=[vmem] * 12,
+        out_specs=[vmem] * 5,
         out_shape=[
-            jax.ShapeDtypeStruct((tokens, part), F32),
+            jax.ShapeDtypeStruct((part, tokens), F32),
             jax.ShapeDtypeStruct((3, part, 4 * HEAD_DIM), F32),
             jax.ShapeDtypeStruct((4 * units, part), F32),
+            jax.ShapeDtypeStruct((4, proj.shape[1], part), F32),
             jax.ShapeDtypeStruct((small_rows, 128), F32),
         ],
         scratch_shapes=[
@@ -1209,6 +1221,10 @@
             *weight_scratch(rows, part),
             *weight_scratch(fc1.shape[0], part),
             *sum_scratch(small_rows, axes),
+            pltpu.VMEM(proj.shape[1:], BF16),
+            pltpu.VMEM(proj.shape, BF16),
+            pltpu.SemaphoreType.DMA((2, 1, 4)),
+            *weight_scratch(proj.shape[1], part),
         ],
         compiler_params=pltpu.CompilerParams(
             collective_id=3, has_side_effects=True, vmem_limit_bytes=60 << 20
@@ -1216,7 +1232,7 @@
         name="tail",
     )(
         qkv_grad.reshape(cols * n, tokens), qkv_grad, weight_qkv, normed1, first, middle_grad, gain,
-        fc1, early, table, bias,
+        fc1, proj, early, table, bias,
     )
 
 
@@ -1268,22 +1284,21 @@
     )(x, weights, bias, cotangent, weights)
 
 
-def attention(qkv, table, proj, cotangent, weights):
+def attention(qkv, table, cotangent, weights):
     count, _, width = qkv.shape
     tokens = count * width
     images = lax.axis_size("batch")
     vmem = pl.BlockSpec(memory_space=pltpu.VMEM)
     return pl.pallas_call(
         partial(attend_kernel, images),
-        in_specs=[*[vmem] * 4, pl.BlockSpec(memory_space=pl.ANY)],
-        out_specs=[*[vmem] * 6, pl.BlockSpec(memory_space=pl.ANY)],
+        in_specs=[*[vmem] * 3, pl.BlockSpec(memory_space=pl.ANY)],
+        out_specs=[*[vmem] * 5, pl.BlockSpec(memory_space=pl.ANY)],
         out_shape=[
             jax.ShapeDtypeStruct((count, HEAD_DIM, width), BF16),
             jax.ShapeDtypeStruct(qkv.shape, BF16),
             jax.ShapeDtypeStruct((count, HEAD_DIM, width), F32),
             jax.ShapeDtypeStruct((count, 8, width), F32),
-            jax.ShapeDtypeStruct((count, *proj.shape), BF16),
-            jax.ShapeDtypeStruct((width, 4 * cotangent.shape[1]), BF16),
+            jax.ShapeDtypeStruct((width, 4 * cotangent.shape[0]), BF16),
             jax.ShapeDtypeStruct((2, count, *weights.shape[1:]), BF16),
         ],
         scratch_shapes=[
@@ -1309,31 +1324,28 @@
             transcendentals=tokens * tokens,
         ),
         name="attend",
-    )(qkv, table, proj, cotangent, weights)
-
-
-def attention_back(qkv, table, grad, exact, stat, proj, fc2, activated, weights, middle, bias_fc2):
+    )(qkv, table, cotangent, weights)
+
+
+def attention_back(qkv, table, grad, exact, stat, fc2, activated, weights, middle, bias_fc2):
     count, _, width = qkv.shape
     tokens = count * width
     images, part = lax.axis_size("batch"), fc2.shape[1] // 4
     vmem = pl.BlockSpec(memory_space=pltpu.VMEM)
     return pl.pallas_call(
         partial(attend_back_kernel, images),
-        in_specs=[*[vmem] * 9, pl.BlockSpec(memory_space=pl.ANY), vmem, vmem],
-        out_specs=[vmem] * 6,
+        in_specs=[*[vmem] * 8, pl.BlockSpec(memory_space=pl.ANY), vmem, vmem],
+        out_specs=[vmem] * 5,
         out_shape=[
             jax.ShapeDtypeStruct((count, 3 * HEAD_DIM, width), BF16),
             jax.ShapeDtypeStruct(table.shape[::-1], F32),
             jax.ShapeDtypeStruct((2, 128), F32),
-            jax.ShapeDtypeStruct((4, proj.shape[1], part), F32),
             jax.ShapeDtypeStruct((4, fc2.shape[0], part), F32),
-            jax.ShapeDtypeStruct((width, part), BF16),
+            jax.ShapeDtypeStruct((part, width), BF16),
         ],
         scratch_shapes=[
             *fetch_scratch(weights),
             pltpu.VMEM((384, 128), F32),
-            pltpu.VMEM(proj.shape[1:], BF16),
-            pltpu.VMEM(proj.shape, BF16),
             pltpu.VMEM((count, HEAD_DIM, width), BF16),
             pltpu.VMEM((count, width, 256), BF16),
             pltpu.VMEM((count, 256, width), BF16),
@@ -1346,9 +1358,8 @@
             pltpu.VMEM((count, width, 128), BF16),
             pltpu.VMEM((count, width, 128), BF16),
             pltpu.VMEM((count, 3 * HEAD_DIM, width), BF16),
-            pltpu.SemaphoreType.DMA((2, 4, 4)),
+            pltpu.SemaphoreType.DMA((2, 3, 4)),
             *weight_scratch(fc2.shape[0], part),
-            *weight_scratch(proj.shape[1], part),
             *mix_scratch(*middle.shape, True),
         ],
         compiler_params=pltpu.CompilerParams(
@@ -1360,7 +1371,7 @@
             transcendentals=tokens * tokens,
         ),
         name="attend_back",
-    )(qkv, table, table.T, grad, exact, stat, proj, fc2, activated, weights, middle, bias_fc2)
+    )(qkv, table, table.T, grad, exact, stat, fc2, activated, weights, middle, bias_fc2)
 
 
 def moments(values):
@@ -1406,16 +1417,14 @@
     columns = jnp.concatenate([jnp.pad(bias_qkv, ((0, 0), (0, 256 - 3 * head))), bias_fc1], 1)
     columns = jnp.broadcast_to(columns, (8, 256 + hidden))
     local_qkv = qkv_weight.reshape(part, 3, rows, head).transpose(2, 1, 3, 0).reshape(rows, 3 * head, part)
-    local_rest = jnp.concatenate(
-        [
-            proj_weight.reshape(rows, head, part),
-            fc1_weight.T.reshape(rows, hidden, part),
-            fc2_weight.reshape(rows, hidden, part),
-        ],
-        1,
-    )
-    qkv, normed1, first_own, weight_qkv, spread_rest, vectors, columns = start(
-        patches[0], local_qkv, local_rest, vectors, columns
+    qkv, normed1, first_own, weight_qkv, weight_proj, local_rest, vectors, columns = start(
+        patches[0].T,
+        local_qkv,
+        proj_weight.reshape(rows, head, part),
+        fc1_weight.T.reshape(rows, hidden, part),
+        fc2_weight.reshape(rows, hidden, part),
+        vectors,
+        columns,
     )
     gain1, shift1, gain2, shift2, bias_proj, bias_fc2 = [vectors[i] for i in range(6)]
     weight_qkv = weight_qkv.reshape(cols * 3 * head, model)
@@ -1424,8 +1433,8 @@
     zero_row = jnp.zeros((1, head), BF16)
     table = jnp.concatenate([height_table[::-1], zero_row, width_table[::-1], zero_row], 0)
 
-    merged, qkv, exact, stat, weight_proj, cotangent, weights = attention(
-        qkv, table, spread_rest[:head], out_grad[0], spread_rest[head:].reshape(2, hidden, model)
+    merged, qkv, exact, stat, cotangent, weights = attention(
+        qkv, table, out_grad[0].T, local_rest.reshape(2, hidden, model)
     )
     weight_proj = weight_proj.reshape(cols * head, model)
     merged = merged.reshape(cols * head, width)
@@ -1475,12 +1484,12 @@
         (merged_grad, fc1_grad, proj_grad, fc2_grad, early)
     )
     fc1_grad = sum_columns(fc1_grad)
-    qkv_grad, table_grad, bias_grad, proj_grad, fc2_grad, final = attention_back(
-        qkv, table, merged_grad, exact, stat, proj_grad.reshape(cols, head, model), fc2_grad,
-        activated, weights, middle, bias_fc2[None],
-    )
-    input_grad, qkv_weight_grad, fc1_grad, small = tail(
-        qkv_grad, weight_qkv, normed1, first_own, middle_grad, gain1[None], fc1_grad, early, table_grad, bias_grad
+    qkv_grad, table_grad, bias_grad, fc2_grad, final = attention_back(
+        qkv, table, merged_grad, exact, stat, fc2_grad, activated, weights, middle, bias_fc2[None]
+    )
+    input_grad, qkv_weight_grad, fc1_grad, proj_grad, small = tail(
+        qkv_grad, weight_qkv, normed1, first_own, middle_grad, gain1[None],
+        fc1_grad, proj_grad.reshape(cols, head, model), early, table_grad, bias_grad,
     )
 
     def sum_images(values):
@@ -1511,8 +1520,8 @@
 
     side = 2 * GRID - 1
     return (
-        final[None],
-        input_grad[None],
+        final.T[None],
+        input_grad.T[None],
         qkv_weight_grad,
         bias_total,
         proj_grad,

time: 588 us -> 525 us (0.89)
  Pallas kernels: 474 us -> 436 us
  waiting for transfers between devices: 20.5 us -> 5.14 us
  local copies, waits for them, and re-layouts: 48 us -> 40.9 us
    pallas_call x3, Pallas kernels: 321 us -> 281 us  [the longest x1 107 us: attention(): pl.pallas_call(partial(attend_kernel, images), in_specs=[*[vmem] * 3, pl....]
    reduce_scatter x2, waiting for transfers between devices: 20.5 us -> 5.11 us  [sum_columns(): return lax.psum_scatter(values, 'col', scatter_dimension=0, tiled=False)]
    unnamed x58 -> x60, local copies, waits for them, and re-layouts: 20.5 us -> 19.9 us
  transfers between devices with their start and end apart: 2 -> 2, of which waited for: 1 -> 1; matrix products, arithmetic and copies ran while one was open for 4% -> 4% of each run, Pallas kernels for 28% -> 27%
where the time goes in v5:
time: 525 us; the launch traced here: 517 us
  Pallas kernels  436 us (83%)
  local copies, waits for them, and re-layouts  40.9 us (8%)
  matrix products  17.8 us (3%)
  between operations  14.9 us (3%)
    pallas_call x1, Pallas kernels, attention(): pl.pallas_call(partial(attend_kernel, images), in_specs=[*[vmem] * 3, pl....  107 us
    pallas_call x1, Pallas kernels, attention_back(): pl.pallas_call(partial(attend_back_kernel, images), in_specs=[*[vmem] * 8...  93.3 us
    pallas_call x1, Pallas kernels, tail(): pl.pallas_call(partial(tail_kernel, axes), in_specs=[vmem] * 12, out_spec...  80.9 us
    pallas_call x2, Pallas kernels, row_mix(): pl.pallas_call(partial(row_mix_kernel, finish, len(extra), 1 + len(outs),...  79.4 us
    pallas_call x1, Pallas kernels, start(): pl.pallas_call(partial(start_kernel, lax.axis_size('batch')), in_specs=[v...  65.1 us
    unnamed x60, local copies, waits for them, and re-layouts  19.9 us
    dot_general x2, matrix products, contract_rows(): lax.dot_general(left, right, (((0,), (0,)), ((), ())), preferred_element_...  12.1 us
    pallas_call x1, Pallas kernels, feed_forward(): pl.pallas_call(hidden_kernel, grid=(hidden // step,), in_specs=[whole, fi...  11.1 us
  transfers between devices with their start and end apart: 2, of which 1 were waited for; matrix products, arithmetic and copies ran while one was open for 4% of the time, Pallas kernels for 27%

profile of v5, /device:TPU:8, one launch (start us, length us, event | category | flops | bytes accessed | tf_op | source)
XLA Modules:
  0.0 516.7 jit_solution(8735074136682521058)
XLA Ops:
  13.2 0.8 rev.12
  14.0 0.8 rev.13
  15.7 1.5 copy.48
  18.0 1.6 copy.51
  19.6 0.9 copy-done.9
  20.6 65.1 %start.1 = (bf16[4,240,1024]{2,1,0:T(8,128)(2,1)}, bf16[1024,1280]{1,0:T(8,128)(2,1)}, bf16[256,1280]{1,0:T(8,128)(2,1)S(1)}, bf16[4,240,1280]{2,1,0:T(8,128)(2,...) custom-call(bf16[320,1024]{1,0:T(8,128)(2,1)S(1)} %bitcast.78, ...), custom_call_target="tpu_custom_call" | custom-call | tf_op jit(solution)/shard_map/start/pallas_call | solution.py:333
  85.7 0.8 copy-done.7
  86.5 0.9 copy-done.13
  87.5 1.1 copy-done.5
  88.6 1.4 copy-done.12
  90.1 106.5 %attend.1 = (bf16[4,80,1024]{2,1,0:T(8,128)(2,1)S(1)}, bf16[4,240,1024]{2,1,0:T(8,128)(2,1)}, f32[4,80,1024]{2,1,0:T(8,128)S(1)}, f32[4,8,1024]{2,1,0:T(8,128)S(...) custom-call(bf16[4,240,1024]{2,1,0:T(8,128)(2,1)} %get-tuple-element.57.given_ref, ...), custom_call_target="tpu_custom_call" | custom-call | flops 17179869184 | bytes 3932160 | tf_op jit(solution)/shard_map/attend/pallas_call | solution.py:1292
  196.6 1.0 copy-done.18
  197.7 35.0 %middle_and_norm2.1 = (bf16[4,256,1280]{2,1,0:T(8,128)(2,1)S(1)}, f32[256,1280]{1,0:T(8,128)S(1)}, bf16[2,4,320,1280]{3,2,1,0:T(8,128)(2,1)}) custom-call(bf16[320,1024]{1,0:T(8,128)(2,1)S(1)} %bitcast.86, bf16[320,1280]{1,0:T(8,128)(2,1)S(1)} %bitcast.82, f32[3,1280]{1,0:T(4,128)S(1)} %slice.67.refs_0_, ...), custom_call_target="tpu_custom_call", output_to_operand_aliasing={{2}: (4, {})} | custom-call | flops 3355443200 | bytes 5242880 | tf_op jit(solution)/shard_map/middle_and_norm2/pallas_call | solution.py:950
  232.7 11.1 %feed_forward.1 = (bf16[1024,1280]{1,0:T(8,128)(2,1)S(1)}, bf16[1024,1280]{1,0:T(8,128)(2,1)S(1)}, f32[1,1280]{1,0:T(1,128)S(1)}) custom-call(bf16[1024,1280]{1,0:T(8,128)(2,1)S(1)} %bitcast.84, bf16[2,1280,1280]{2,1,0:T(8,128)(2,1)} %bitcast.89, f32[1,1280]{1,0:T(1,128)S(1)} %broadcast_in_dim_reshape_squeeze.3.bias_ref, bf16[1024,1280]{1,0:T(8,128)(2,1)S(1)} %copy-done.10, ...), custom_call_target="tpu_custom_call" | custom-call | flops 6710886400 | bytes 17039360 | tf_op jit(solution)/shard_map/feed_forward/pallas_call | solution.py:1267
  243.8 5.1 convolution_convert_fusion.1
  249.5 1.1 constant_dynamic-slice_fusion.1.refs_2_
  250.7 7.0 %convolution_convert_fusion = bf16[1280,1280]{1,0:T(8,128)(2,1)} fusion(bf16[1024,1280]{1,0:T(8,128)(2,1)S(1)} %get-tuple-element.71.left_ref, bf16[1024,1280]{1,0:T(8,128)(2,1)} %bitcast.85), kind=kOutput, calls=%fused_computation | convolution fusion | flops 3357081600 | bytes 8519680 | tf_op jit(solution)/shard_map/dot_general | solution.py:1443
  257.7 44.4 %middle_grad.1 = (bf16[4,256,1280]{2,1,0:T(8,128)(2,1)}, f32[256,1280]{1,0:T(8,128)S(1)}, f32[3,1280]{1,0:T(4,128)S(1)}, bf16[4,160,1280]{2,1,0:T(8,128)(2,1)}) custom-call(bf16[1024,1280]{1,0:T(8,128)(2,1)} %copy-done, bf16[2,1280,1280]{2,1,0:T(8,128)(2,1)} %bitcast.91, f32[3,1280]{1,0:T(4,128)S(1)} %slice.67.refs_0_, f32[256,1280]{1,0:T(8,128)S(1)} %copy-done.2, ...), custom_call_target="tpu_custom_call" | custom-call | flops 3355443200 | bytes 5242880 | tf_op jit(solution)/shard_map/middle_grad/pallas_call | solution.py:950
  302.1 1.0 copy-done.3
  304.3 3.8 convolution_convert_fusion.2
  308.1 1.9 convolution_convert_fusion.3
  310.6 5.1 reduce-scatter.3.cloned.1.call-done
  315.7 93.3 %attend_back.1 = (bf16[4,240,1024]{2,1,0:T(8,128)(2,1)}, f32[80,256]{1,0:T(8,128)}, f32[2,128]{1,0:T(2,128)}, f32[4,320,320]{2,1,0:T(8,128)}, bf16[320,1024]{1,0:T(8,128)(2,1)}) custom-call(bf16[4,240,1024]{2,1,0:T(8,128)(2,1)} %get-tuple-element.59.qkv_ref, bf16[256,80]{1,0:T(8,128)(2,1)} %copy-done.11, bf16[80,256]{1,0:T(8,128)(2,1)} %get-tuple-element.156.tab_t_ref, ...), custom_call_target="tpu_custom_call" | custom-call | flops 42949672960 | bytes 7864320 | tf_op jit(solution)/shard_map/attend_back/pallas_call | solution.py:1335
  409.0 3.0 copy.56
  412.0 80.9 %tail.1 = (f32[320,1024]{1,0:T(8,128)}, f32[3,320,320]{2,1,0:T(8,128)}, f32[1280,320]{1,0:T(8,128)}, f32[4,80,320]{2,1,0:T(8,128)}, f32[296,128]{1,0:T(8,128)}) custom-call(bf16[960,1024]{1,0:T(8,128)(2,1)} %bitcast.88, bf16[4,240,1024]{2,1,0:T(8,128)(2,1)} %get-tuple-element.83.grads_ref, bf16[960,1280]{1,0:T(8,128)(2,1)} %bitcast.96, ...), custom_call_target="tpu_custom_call" | custom-call | tf_op jit(solution)/shard_map/tail/pallas_call | solution.py:1205
  492.9 0.8 slice.71
  494.4 0.9 slice_bitcast_fusion
  495.3 0.8 fusion.5
  502.9 2.7 copy.55
  505.6 0.8 copy.64
  506.5 1.1 copy.65
  507.5 1.1 copy.66
  (103 shorter events, 18.4 us)
Async XLA Ops:
  7.2 10.1 %copy-start.22 = (bf16[320,1280]{1,0:T(8,128)(2,1)S(1)}, bf16[320,1280]{1,0:T(8,128)(2,1)}, u32[]{:S(2)}) copy-start(bf16[320,1280]{1,0:T(8,128)(2,1)} %param.25) | copy-start | bytes 2457604
  7.2 308.5 %reduce-scatter.3.cloned.1.call-start = ((), (), s32[]{:S(2)}) async-start(), calls=%async_computation.2 | async-start | bytes 4096000 | tf_op jit(solution)/shard_map/reduce_scatter | solution.py:1446
  15.7 71.9 %copy-start.11 = (bf16[256,80]{1,0:T(8,128)(2,1)}, bf16[256,80]{1,0:T(8,128)(2,1)S(1)}, u32[]{:S(2)}) copy-start(bf16[256,80]{1,0:T(8,128)(2,1)S(1)} %copy.52.tab_ref) | copy-start | bytes 122884
  17.2 2.4 copy-start.4
  19.6 0.9 copy-start.9
  85.7 0.8 copy-start.7
  86.5 0.9 copy-start.13
  87.5 1.1 copy-start.5
  88.6 1.4 copy-start.12
  90.1 107.6 %copy-start.8 = (bf16[256,1280]{1,0:T(8,128)(2,1)S(1)}, bf16[256,1280]{1,0:T(8,128)(2,1)}, u32[]{:S(2)}) copy-start(bf16[256,1280]{1,0:T(8,128)(2,1)} %copy-done.7) | copy-start | bytes 1966084
  90.1 107.6 %copy-start.14 = (bf16[4,80,1280]{2,1,0:T(8,128)(2,1)S(1)}, bf16[4,80,1280]{2,1,0:T(8,128)(2,1)}, u32[]{:S(2)}) copy-start(bf16[4,80,1280]{2,1,0:T(8,128)(2,1)} %copy-done.13) | copy-start | bytes 2457604
  196.6 1.1 copy-start.18
  197.7 35.0 %copy-start.19 = (f32[4,8,1024]{2,1,0:T(8,128)}, f32[4,8,1024]{2,1,0:T(8,128)S(1)}, u32[]{:S(2)}) copy-start(f32[4,8,1024]{2,1,0:T(8,128)S(1)} %get-tuple-element.80.stat_ref) | copy-start | bytes 393220
  197.7 35.0 %copy-start.10 = (bf16[1024,1280]{1,0:T(8,128)(2,1)S(1)}, bf16[1024,1280]{1,0:T(8,128)(2,1)}, u32[]{:S(2)}) copy-start(bf16[1024,1280]{1,0:T(8,128)(2,1)} %get-tuple-element.68.cot_ref) | copy-start | bytes 7864324
  232.7 11.1 %copy-start.1 = (f32[256,1280]{1,0:T(8,128)}, f32[256,1280]{1,0:T(8,128)S(1)}, u32[]{:S(2)}) copy-start(f32[256,1280]{1,0:T(8,128)S(1)} %get-tuple-element.72.refs_1_.middle_ref) | copy-start | bytes 3932164
  232.7 11.1 %copy-start.16 = (bf16[4,256,1280]{2,1,0:T(8,128)(2,1)}, bf16[4,256,1280]{2,1,0:T(8,128)(2,1)S(1)}, u32[]{:S(2)}) copy-start(bf16[4,256,1280]{2,1,0:T(8,128)(2,1)S(1)} %get-tuple-element.65) | copy-start | bytes 7864324
  243.8 5.1 copy-start.17
  243.8 6.9 %copy-start = (bf16[1024,1280]{1,0:T(8,128)(2,1)}, bf16[1024,1280]{1,0:T(8,128)(2,1)S(1)}, u32[]{:S(2)}) copy-start(bf16[1024,1280]{1,0:T(8,128)(2,1)S(1)} %get-tuple-element.71.left_ref) | copy-start | bytes 7864324
  249.0 163.1 %reduce-scatter.5.cloned.1.call-start = ((), (), s32[]{:S(2)}) async-start(), calls=%async_computation.3 | async-start | bytes 2048000 | tf_op jit(solution)/shard_map/reduce_scatter | solution.py:1446
  250.7 7.0 %copy-start.2 = (f32[256,1280]{1,0:T(8,128)S(1)}, f32[256,1280]{1,0:T(8,128)}, u32[]{:S(2)}) copy-start(f32[256,1280]{1,0:T(8,128)} %copy-done.1) | copy-start | bytes 3932164
  257.7 45.5 %copy-start.6 = (bf16[1,1024,320]{1,2,0:T(8,128)(2,1)S(1)}, bf16[1,1024,320]{1,2,0:T(8,128)(2,1)}, u32[]{:S(2)}) copy-start(bf16[1,1024,320]{1,2,0:T(8,128)(2,1)} %param.31) | copy-start | bytes 1966084
  302.1 1.1 copy-start.3
  304.3 3.8 copy-start.15
  304.3 3.8 copy-start.25
  492.9 12.7 %copy-start.23 = (bf16[320,1024]{1,0:T(8,128)(2,1)S(1)}, bf16[320,1024]{1,0:T(8,128)(2,1)}, u32[]{:S(2)}) copy-start(bf16[320,1024]{1,0:T(8,128)(2,1)} %get-tuple-element.82) | copy-start | bytes 1966084
  498.2 8.2 %copy-start.21 = (f32[320,1024]{1,0:T(8,128)S(1)}, f32[320,1024]{1,0:T(8,128)}, u32[]{:S(2)}) copy-start(f32[320,1024]{1,0:T(8,128)} %get-tuple-element.92) | copy-start | bytes 3932164
  505.6 1.9 copy-start.20
  506.5 2.2 copy-start.24
Sparse Core Ops, SparseCore 0:
  249.1 66.5 reduce-scatter.2
  318.0 63.8 reduce-scatter.4

commit v6 on v5

--- a/solution.py
+++ b/solution.py
@@ -38,6 +38,18 @@
         terms.append(term)
         values = values - term.astype(F32)
     return terms
+
+
+def backwards(rows, columns):
+    first = lax.broadcasted_iota(jnp.int32, (rows, columns), 0)
+    second = lax.broadcasted_iota(jnp.int32, (rows, columns), 1)
+    return jnp.where(first + second == 2 * GRID - 2, 1.0, 0.0).astype(BF16)
+
+
+def fill_tables(height_ref, width_ref, tab_t):
+    flip = backwards(2 * GRID - 1, 2 * GRID)
+    tab_t[:, : 2 * GRID] = mm(height_ref[...], flip).astype(BF16)
+    tab_t[:, 2 * GRID :] = mm(width_ref[...], flip).astype(BF16)
 
 
 def skew(values, shift):
@@ -224,9 +236,9 @@
 
 
 def start_kernel(
-    images, patches_ref, qkv_ref, proj_ref, fc1_ref, fc2_ref, vector_ref, column_ref,
+    images, patches_ref, qkv_ref, proj_ref, fc1_ref, fc2_ref, qv_bias_ref, fc1_bias_ref, v0, v1, v2, v3, v4, v5,
     qkv_out, normed_out, first_out, weight_out, proj_out, rest_out, vectors_out, columns_out,
-    patches_all, parts, rest_parts, vector_parts, halves, sems, col_sems, chain_sems, swap_sems,
+    patches_all, parts, rest_parts, rest_own, column_ref, vector_ref, vector_parts, halves, sems, col_sems, chain_sems, swap_sems,
 ):
     row, col, image = lax.axis_index("row"), lax.axis_index("col"), lax.axis_index("batch")
     near, far, diag = row_peers()
@@ -244,7 +256,20 @@
             copy.start()
         return copies
 
-    n, units = 3 * HEAD_DIM, fc1_ref.shape[1]
+    n, units = 3 * HEAD_DIM, fc1_ref.shape[1] // 4
+
+    def mine(values, size):
+        piece = values[:, :size]
+        for place in range(1, 4):
+            piece = jnp.where(row == place, values[:, place * size : (place + 1) * size], piece)
+        return piece
+
+    bias = mine(qv_bias_ref[...], HEAD_DIM)
+    bias = [bias[0:1], jnp.zeros((1, HEAD_DIM), F32), bias[1:2], jnp.zeros((1, 256 - n), F32)]
+    bias = jnp.concatenate([*bias, mine(fc1_bias_ref[...].reshape(1, -1), units)], 1)
+    column_ref[...] = jnp.broadcast_to(bias, column_ref.shape)
+    vectors = [ref[...].reshape(1, -1) for ref in (v0, v1, v2, v3, v4, v5)]
+    vector_ref[...] = jnp.concatenate([*vectors, *vectors[:2]], 0)
     weight_copies = to_row(lambda peer: qkv_ref.at[peer], parts.at[row, 0:n], 0)
     weight_copies += to_row(lambda peer: proj_ref.at[peer], parts.at[row, n : n + HEAD_DIM], 4)
     vector_copies = to_row(lambda peer: vector_ref, vector_parts.at[row], 1)
@@ -295,10 +320,12 @@
     to_far.wait_recv()
     pass_on = row_copy(patches_all.at[far], patches_all.at[far], sems, 2, 2, near)
     pass_on.start()
-    rest_copies = to_row(lambda peer: fc1_ref.at[peer], rest_parts.at[row, 0:units], 3)
-    rest_copies += to_row(lambda peer: fc2_ref.at[peer], rest_parts.at[row, units : 2 * units], 5)
-    rest_parts[row, 0:units] = fc1_ref[row]
-    rest_parts[row, units : 2 * units] = fc2_ref[row]
+    for which, ref in enumerate((fc1_ref, fc2_ref)):
+        for place in range(4):
+            block = ref[:, place * units : (place + 1) * units].astype(F32).T
+            rest_own[place, which * units : (which + 1) * units] = block.astype(BF16)
+    rest_copies = to_row(lambda peer: rest_own.at[peer], rest_parts.at[row], 3)
+    rest_parts[row] = rest_own[row]
     for chain in chains:
         chain.hop(1)
     to_near.wait_recv()
@@ -325,14 +352,15 @@
         copy.wait_send()
 
 
-def start(patches, local_qkv, local_proj, local_fc1, local_fc2, vectors, columns):
+def start(patches, local_qkv, local_proj, local_fc1, local_fc2, qv_bias, fc1_bias, *vectors):
+    columns = (8, 256 + fc1_bias.shape[0] // 4)
     part, width = patches.shape
     n, model = local_qkv.shape[1], part * 4
-    rest = local_fc1.shape[1] + local_fc2.shape[1]
+    rest = 2 * (local_fc1.shape[1] // 4)
     vmem = pl.BlockSpec(memory_space=pltpu.VMEM)
     return pl.pallas_call(
         partial(start_kernel, lax.axis_size("batch")),
-        in_specs=[vmem] * 7,
+        in_specs=[vmem] * 13,
         out_specs=[vmem] * 8,
         out_shape=[
             jax.ShapeDtypeStruct((4, n, width), BF16),
@@ -341,14 +369,16 @@
             jax.ShapeDtypeStruct((4, n, model), BF16),
             jax.ShapeDtypeStruct((4, HEAD_DIM, model), BF16),
             jax.ShapeDtypeStruct((rest, model), BF16),
-            jax.ShapeDtypeStruct((vectors.shape[0], model), F32),
-            jax.ShapeDtypeStruct((4, *columns.shape), F32),
+            jax.ShapeDtypeStruct((8, model), F32),
+            jax.ShapeDtypeStruct((4, *columns), F32),
         ],
         scratch_shapes=[
             pltpu.VMEM((4, part, width), BF16),
             pltpu.VMEM((4, n + HEAD_DIM, part), BF16),
-            pltpu.VMEM((4, rest, part), BF16),
-            pltpu.VMEM((4, *vectors.shape), F32),
+            *[pltpu.VMEM((4, rest, part), BF16)] * 2,
+            pltpu.VMEM(columns, F32),
+            pltpu.VMEM((8, part), F32),
+            pltpu.VMEM((4, 8, part), F32),
             pltpu.VMEM((2, 4, HALF, model), BF16),
             pltpu.SemaphoreType.DMA((2, 6, 3)),
             pltpu.SemaphoreType.DMA((2, 1, 4)),
@@ -359,16 +389,17 @@
             collective_id=7, has_side_effects=True, vmem_limit_bytes=48 << 20
         ),
         name="start",
-    )(patches, local_qkv, local_proj, local_fc1, local_fc2, vectors, columns)
+    )(patches, local_qkv, local_proj, local_fc1, local_fc2, qv_bias, fc1_bias, *vectors)
 
 
 CHAIN_TURNS = (6, 12)
 
 
 def attend_kernel(
-    images, given_ref, tab_ref, cot_ref, weight_ref,
+    images, given_ref, height_ref, width_ref, cot_ref, weight_ref,
     merged_ref, qkv_ref, exact_ref, stat_ref, cot_out, weight_all,
     kaug, columns, acc, top, total, box, sems, cot_parts, cot_sems, local_sems, chain_sems, swap_sems,
+    tab_t, tab_ref,
 ):
     me = lax.axis_index("col")
     width = given_ref.shape[2]
@@ -407,6 +438,8 @@
     token = lax.broadcasted_iota(jnp.int32, (width, 2 * GRID), 0)
     lane = lax.broadcasted_iota(jnp.int32, (width, 2 * GRID), 1)
     tail = jnp.zeros((128 - HEAD_DIM, QUERIES), BF16)
+    fill_tables(height_ref, width_ref, tab_t)
+    tab_ref[...] = tab_t[...].astype(F32).T.astype(BF16)
     factor = SCALE * LOG2E
 
     def prepare(part):
@@ -516,10 +549,10 @@
 
 
 def attend_back_kernel(
-    images, qkv_ref, tab_ref, tab_t_ref, given_ref, exact_ref, stat_ref, fc2_ref,
+    images, qkv_ref, height_ref, width_ref, given_ref, exact_ref, stat_ref, fc2_ref,
     activated_ref, weights_ref, middle_ref, bias_fc2_ref,
     out_ref, tab_grad_ref, bias_out, fc2_out, block_out,
-    held, held_sem, bias_ref, grads, kaug, kaug_t, vaug, key_sum, value_sum, spread, columns,
+    tab_t_ref, tab_ref, held, held_sem, bias_ref, grads, kaug, kaug_t, vaug, key_sum, value_sum, spread, columns,
     grad_columns, grad_rows, q_rows, box, sems, *weight_parts,
 ):
     me = lax.axis_index("col")
@@ -533,8 +566,10 @@
         ("batch", image_peers(images) if images == 2 else ()),
     )
 
+    fc2_grads = []
+
     def write_fc2(place, values):
-        fc2_out[place] = values
+        fc2_grads.append(values)
 
     fc2 = weight_steps(fc2_ref, images, weight_parts[:4], write_fc2)
 
@@ -559,6 +594,8 @@
     next(fc2)
     grads[me] = given_ref[me]
 
+    fill_tables(height_ref, width_ref, tab_t_ref)
+    tab_ref[...] = tab_t_ref[...].astype(F32).T.astype(BF16)
     tail_row = lax.broadcasted_iota(jnp.int32, (128 - HEAD_DIM, width), 0)
     pad = jnp.where(tail_row < 3, 1.0, 0.0)
     token = lax.broadcasted_iota(jnp.int32, (width, 2 * GRID), 0)
@@ -686,11 +723,12 @@
     lax.fori_loop(0, 4, pair, 0)
     next(block)
     next(block)
-    lax.fori_loop(4, 8, pair, 0)
     next(fc2)
+    lax.fori_loop(4, 9, pair, 0)
     next(block, None)
-    lax.fori_loop(8, 16, pair, 0)
     next(fc2, None)
+    fc2_out[...] = jnp.concatenate(fc2_grads, 0).T
+    lax.fori_loop(9, 16, pair, 0)
     out_ref[me] = box[me]
     for step in range(1, 4):
         grad_copy(step).wait_send()
@@ -1101,13 +1139,12 @@
 def tail_kernel(
     axes,
     qkv_grad_ref, grads_ref, weight_qkv_ref, normed1_ref, first_ref, middle_grad_ref, gain_ref,
-    fc1_ref, proj_ref, early_ref, table_ref, bias_ref, patches_out, qkv_out, fc1_out, proj_out, small,
-    *scratch,
+    fc1_ref, proj_ref, early_ref, table_ref, bias_ref, patches_out, qkv_out, fc1_out, proj_out, tables_out, small, *rest,
 ):
-    sums1, qkv_rows, *scratch = scratch
+    vector_outs, (sums1, qkv_rows, *scratch) = rest[:6], rest[6:]
     col_scratch, scratch = scratch[:7], scratch[7:]
     mix, qkv_scratch, fc1_scratch, sum_parts = scratch[:7], scratch[7:11], scratch[11:15], scratch[15:20]
-    proj_rows, proj_box, proj_sems, *proj_scratch = scratch[20:]
+    proj_rows, proj_box, proj_sems, fc1_rows, *proj_scratch = scratch[20:]
     row, col = lax.axis_index("row"), lax.axis_index("col")
     images = dict(axes)["batch"]
     meet(
@@ -1125,10 +1162,10 @@
     def write_fc1(place, values, others=None):
         n = values.shape[0]
         if others is None:
-            fc1_out[place * n : (place + 1) * n] = values
+            fc1_rows[place * n : (place + 1) * n] = values
         else:
-            fc1_out[pl.ds(pl.multiple_of((2 * place + image) * n, 8), n)] = values
-            fc1_out[pl.ds(pl.multiple_of((2 * place + 1 - image) * n, 8), n)] = others
+            fc1_rows[pl.ds(pl.multiple_of((2 * place + image) * n, 8), n)] = values
+            fc1_rows[pl.ds(pl.multiple_of((2 * place + 1 - image) * n, 8), n)] = others
 
     def write_proj(place, values):
         proj_out[place] = values
@@ -1185,6 +1222,19 @@
     small[at : at + LAST_ROWS] = jnp.concatenate([*last, spare], 0)
 
     go(sums, fc1, proj, qkv_sum, qkv, sums, patches, fc1, proj, sums, qkv, fc1, sums, qkv)
+    firsts = [lines * i for i in (5, 6, 7, 4)] + [EARLY_ROWS + TABLE_ROWS + BIAS_ROWS + lines * i for i in range(2)]
+    part = vector_outs[0].shape[0]
+    for first, out in zip(firsts, vector_outs):
+        whole = jnp.concatenate([small[first + i : first + i + 1] for i in range(lines)], 1)
+        mine = whole[:, :part]
+        for place in range(1, 4):
+            mine = jnp.where(row == place, whole[:, place * part : (place + 1) * part], mine)
+        out[...] = mine.reshape(part)
+    fc1_out[...] = fc1_rows[...].T
+    flip = backwards(2 * GRID, 2 * GRID - 1)
+    for half in range(2):
+        table = small[EARLY_ROWS + half * HEAD_DIM : EARLY_ROWS + (half + 1) * HEAD_DIM]
+        tables_out[half] = sum(mm(term, flip) for term in split(table, 3))
     for kind in range(3):
         rows = slice(kind * HEAD_DIM, (kind + 1) * HEAD_DIM)
         qkv_out[kind] = jnp.concatenate([values[rows] for values in head_grads], 0).T
@@ -1205,13 +1255,15 @@
     return pl.pallas_call(
         partial(tail_kernel, axes),
         in_specs=[vmem] * 12,
-        out_specs=[vmem] * 5,
+        out_specs=[vmem] * 12,
         out_shape=[
             jax.ShapeDtypeStruct((part, tokens), F32),
             jax.ShapeDtypeStruct((3, part, 4 * HEAD_DIM), F32),
-            jax.ShapeDtypeStruct((4 * units, part), F32),
+            jax.ShapeDtypeStruct((part, 4 * units), F32),
             jax.ShapeDtypeStruct((4, proj.shape[1], part), F32),
+            jax.ShapeDtypeStruct((2, HEAD_DIM, 2 * GRID - 1), F32),
             jax.ShapeDtypeStruct((small_rows, 128), F32),
+            *[jax.ShapeDtypeStruct((part,), F32)] * 6,
         ],
         scratch_shapes=[
             pltpu.VMEM((3, model), F32),
@@ -1224,6 +1276,7 @@
             pltpu.VMEM(proj.shape[1:], BF16),
             pltpu.VMEM(proj.shape, BF16),
             pltpu.SemaphoreType.DMA((2, 1, 4)),
+            pltpu.VMEM((4 * units, part), F32),
             *weight_scratch(proj.shape[1], part),
         ],
         compiler_params=pltpu.CompilerParams(
@@ -1284,14 +1337,18 @@
     )(x, weights, bias, cotangent, weights)
 
 
-def attention(qkv, table, cotangent, weights):
+def table_scratch():
+    return [pltpu.VMEM((HEAD_DIM, 4 * GRID), BF16), pltpu.VMEM((4 * GRID, HEAD_DIM), BF16)]
+
+
+def attention(qkv, height, span, cotangent, weights):
     count, _, width = qkv.shape
     tokens = count * width
     images = lax.axis_size("batch")
     vmem = pl.BlockSpec(memory_space=pltpu.VMEM)
     return pl.pallas_call(
         partial(attend_kernel, images),
-        in_specs=[*[vmem] * 3, pl.BlockSpec(memory_space=pl.ANY)],
+        in_specs=[*[vmem] * 4, pl.BlockSpec(memory_space=pl.ANY)],
         out_specs=[*[vmem] * 5, pl.BlockSpec(memory_space=pl.ANY)],
         out_shape=[
             jax.ShapeDtypeStruct((count, HEAD_DIM, width), BF16),
@@ -1314,6 +1371,7 @@
             pltpu.SemaphoreType.DMA((2,)),
             pltpu.SemaphoreType.DMA((2, 2, 2, 3)),
             pltpu.SemaphoreType.DMA((2, 2, 3)),
+            *table_scratch(),
         ],
         compiler_params=pltpu.CompilerParams(
             collective_id=5, has_side_effects=True, vmem_limit_bytes=48 << 20
@@ -1324,10 +1382,10 @@
             transcendentals=tokens * tokens,
         ),
         name="attend",
-    )(qkv, table, cotangent, weights)
-
-
-def attention_back(qkv, table, grad, exact, stat, fc2, activated, weights, middle, bias_fc2):
+    )(qkv, height, span, cotangent, weights)
+
+
+def attention_back(qkv, height, span, grad, exact, stat, fc2, activated, weights, middle, bias_fc2):
     count, _, width = qkv.shape
     tokens = count * width
     images, part = lax.axis_size("batch"), fc2.shape[1] // 4
@@ -1338,12 +1396,13 @@
         out_specs=[vmem] * 5,
         out_shape=[
             jax.ShapeDtypeStruct((count, 3 * HEAD_DIM, width), BF16),
-            jax.ShapeDtypeStruct(table.shape[::-1], F32),
+            jax.ShapeDtypeStruct((HEAD_DIM, 4 * GRID), F32),
             jax.ShapeDtypeStruct((2, 128), F32),
-            jax.ShapeDtypeStruct((4, fc2.shape[0], part), F32),
+            jax.ShapeDtypeStruct((part, 4 * fc2.shape[0]), F32),
             jax.ShapeDtypeStruct((part, width), BF16),
         ],
         scratch_shapes=[
+            *table_scratch(),
             *fetch_scratch(weights),
             pltpu.VMEM((384, 128), F32),
             pltpu.VMEM((count, HEAD_DIM, width), BF16),
@@ -1371,7 +1430,7 @@
             transcendentals=tokens * tokens,
         ),
         name="attend_back",
-    )(qkv, table, table.T, grad, exact, stat, fc2, activated, weights, middle, bias_fc2)
+    )(qkv, height, span, grad, exact, stat, fc2, activated, weights, middle, bias_fc2)
 
 
 def moments(values):
@@ -1409,32 +1468,30 @@
 
     images = lax.axis_size("batch")
 
-    vectors = jnp.stack([norm1_gain, norm1_shift, norm2_gain, norm2_shift, proj_bias, fc2_bias])
-    vectors = jnp.concatenate([vectors, jnp.zeros((2, part), F32)], 0)
-    bias_qkv = lax.dynamic_index_in_dim(qv_bias.reshape(2, rows, head), row, 1, keepdims=False)
-    bias_qkv = jnp.stack([bias_qkv[0], jnp.zeros_like(bias_qkv[0]), bias_qkv[1]]).reshape(1, -1)
-    bias_fc1 = lax.dynamic_index_in_dim(fc1_bias.reshape(rows, hidden), row, 0, keepdims=True)
-    columns = jnp.concatenate([jnp.pad(bias_qkv, ((0, 0), (0, 256 - 3 * head))), bias_fc1], 1)
-    columns = jnp.broadcast_to(columns, (8, 256 + hidden))
     local_qkv = qkv_weight.reshape(part, 3, rows, head).transpose(2, 1, 3, 0).reshape(rows, 3 * head, part)
     qkv, normed1, first_own, weight_qkv, weight_proj, local_rest, vectors, columns = start(
         patches[0].T,
         local_qkv,
         proj_weight.reshape(rows, head, part),
-        fc1_weight.T.reshape(rows, hidden, part),
-        fc2_weight.reshape(rows, hidden, part),
-        vectors,
-        columns,
+        fc1_weight,
+        fc2_weight.T,
+        qv_bias,
+        fc1_bias,
+        norm1_gain,
+        norm1_shift,
+        norm2_gain,
+        norm2_shift,
+        proj_bias,
+        fc2_bias,
     )
     gain1, shift1, gain2, shift2, bias_proj, bias_fc2 = [vectors[i] for i in range(6)]
     weight_qkv = weight_qkv.reshape(cols * 3 * head, model)
     bias_fc1 = columns[:, 0, 256:].reshape(cols * hidden)
 
-    zero_row = jnp.zeros((1, head), BF16)
-    table = jnp.concatenate([height_table[::-1], zero_row, width_table[::-1], zero_row], 0)
+    height, span = height_table.T, width_table.T
 
     merged, qkv, exact, stat, cotangent, weights = attention(
-        qkv, table, out_grad[0].T, local_rest.reshape(2, hidden, model)
+        qkv, height, span, out_grad[0].T, local_rest.reshape(2, hidden, model)
     )
     weight_proj = weight_proj.reshape(cols * head, model)
     merged = merged.reshape(cols * head, width)
@@ -1485,9 +1542,9 @@
     )
     fc1_grad = sum_columns(fc1_grad)
     qkv_grad, table_grad, bias_grad, fc2_grad, final = attention_back(
-        qkv, table, merged_grad, exact, stat, fc2_grad, activated, weights, middle, bias_fc2[None]
-    )
-    input_grad, qkv_weight_grad, fc1_grad, proj_grad, small = tail(
+        qkv, height, span, merged_grad, exact, stat, fc2_grad, activated, weights, middle, bias_fc2[None]
+    )
+    input_grad, qkv_weight_grad, fc1_grad, proj_grad, tables, small, *vector_grads = tail(
         qkv_grad, weight_qkv, normed1, first_own, middle_grad, gain1[None],
         fc1_grad, proj_grad.reshape(cols, head, model), early, table_grad, bias_grad,
     )
@@ -1495,47 +1552,38 @@
     def sum_images(values):
         return values if images == 2 else lax.psum(values.astype(BF16), "batch").astype(F32)
 
-    fc2_grad = sum_images(fc2_grad).reshape(rows * hidden, part)
+    fc2_grad = sum_images(fc2_grad).T
     proj_grad = sum_images(proj_grad).reshape(rows * head, part)
-    fc1_grad = sum_images(fc1_grad).T
+    fc1_grad = sum_images(fc1_grad)
     qkv_weight_grad = sum_images(qkv_weight_grad).transpose(1, 0, 2)
 
     lines = model // 128
     fc1_bias_grad = small[: 4 * lines].reshape(rows, cols, hidden)
     fc1_bias_grad = lax.dynamic_index_in_dim(fc1_bias_grad, col, 1, keepdims=False).reshape(rows * hidden)
-    fc2_bias_grad = small[4 * lines : 5 * lines].reshape(-1)
-    gain2_grad, shift2_grad, proj_bias_grad = small[5 * lines : 8 * lines].reshape(3, model)
+    gain2_grad, shift2_grad, proj_bias_grad, fc2_bias_grad, gain1_grad, shift1_grad = vector_grads
     at = EARLY_ROWS
-    table_grad = jnp.concatenate([small[at : at + TABLE_ROWS // 2], small[at + TABLE_ROWS // 2 : at + TABLE_ROWS]], 1)
-    table_grad = table_grad.T
     at += TABLE_ROWS
     bias_total = small[at : at + BIAS_ROWS].reshape(cols, rows, 2, 128)
     bias_total = lax.dynamic_index_in_dim(bias_total, col, 0, keepdims=False)[:, :, :head]
     bias_total = bias_total.transpose(1, 0, 2).reshape(2, rows * head)
-    at += BIAS_ROWS
-    gain1_grad, shift1_grad = small[at : at + 2 * lines].reshape(2, model)
-
-    def features_of_row(values):
-        return lax.dynamic_slice_in_dim(values, row * part, part, 0)
-
-    side = 2 * GRID - 1
+
     return (
         final.T[None],
         input_grad.T[None],
         qkv_weight_grad,
         bias_total,
         proj_grad,
-        features_of_row(proj_bias_grad),
-        features_of_row(gain1_grad),
-        features_of_row(shift1_grad),
-        features_of_row(gain2_grad),
-        features_of_row(shift2_grad),
+        proj_bias_grad,
+        gain1_grad,
+        shift1_grad,
+        gain2_grad,
+        shift2_grad,
         fc1_grad,
         fc1_bias_grad,
         fc2_grad,
-        features_of_row(fc2_bias_grad),
-        table_grad[:side][::-1],
-        table_grad[2 * GRID : 2 * GRID + side][::-1],
+        fc2_bias_grad,
+        tables[0].T,
+        tables[1].T,
     )
 
 

time: 525 us -> 515 us (0.981)
  local copies, waits for them, and re-layouts: 40.9 us -> 27.3 us
    unnamed x60 -> x101, local copies, waits for them, and re-layouts: 19.9 us -> 18.9 us
  transfers between devices with their start and end apart: 2 -> 2, of which waited for: 1 -> 1; matrix products, arithmetic and copies ran while one was open for 4% -> 3% of each run, Pallas kernels for 27% -> 27%
where the time goes in v6:
time: 515 us; the launch traced here: 506 us
  Pallas kernels  440 us (85%)
  local copies, waits for them, and re-layouts  27.3 us (5%)
  matrix products  17.7 us (3%)
  between operations  15 us (3%)
  waiting for transfers between devices  5.5 us (1%)
    pallas_call x1, Pallas kernels, attention(): pl.pallas_call(partial(attend_kernel, images), in_specs=[*[vmem] * 4, pl....  107 us
    pallas_call x1, Pallas kernels, attention_back(): pl.pallas_call(partial(attend_back_kernel, images), in_specs=[*[vmem] * 8...  94.3 us
    pallas_call x1, Pallas kernels, tail(): pl.pallas_call(partial(tail_kernel, axes), in_specs=[vmem] * 12, out_spec...  81.9 us
    pallas_call x2, Pallas kernels, row_mix(): pl.pallas_call(partial(row_mix_kernel, finish, len(extra), 1 + len(outs),...  79.1 us
    pallas_call x1, Pallas kernels, start(): pl.pallas_call(partial(start_kernel, lax.axis_size('batch')), in_specs=[v...  66.4 us
    unnamed x101, local copies, waits for them, and re-layouts  18.9 us
    dot_general x2, matrix products, contract_rows(): lax.dot_general(left, right, (((0,), (0,)), ((), ())), preferred_element_...  12 us
    pallas_call x1, Pallas kernels, feed_forward(): pl.pallas_call(hidden_kernel, grid=(hidden // step,), in_specs=[whole, fi...  11.1 us
  transfers between devices with their start and end apart: 2, of which 1 were waited for; matrix products, arithmetic and copies ran while one was open for 3% of the time, Pallas kernels for 27%

profile of v6, /device:TPU:8, one launch (start us, length us, event | category | flops | bytes accessed | tf_op | source)
XLA Modules:
  0.0 506.1 jit_solution(7091377716880805983)
XLA Ops:
  7.4 2.4 copy.36
  9.8 1.3 copy.37
  11.2 66.4 %start.1 = (bf16[4,240,1024]{2,1,0:T(8,128)(2,1)}, bf16[1024,1280]{1,0:T(8,128)(2,1)}, bf16[256,1280]{1,0:T(8,128)(2,1)S(1)}, bf16[4,240,1280]{2,1,0:T(8,128)(2,...) custom-call(bf16[320,1024]{1,0:T(8,128)(2,1)S(1)} %bitcast.64, ...), custom_call_target="tpu_custom_call" | custom-call | tf_op jit(solution)/shard_map/start/pallas_call | solution.py:361
  77.6 0.8 copy-done.8
  78.4 0.9 copy-done.21
  79.5 1.4 copy-done.20
  80.9 106.8 %attend.1 = (bf16[4,80,1024]{2,1,0:T(8,128)(2,1)S(1)}, bf16[4,240,1024]{2,1,0:T(8,128)(2,1)}, f32[4,80,1024]{2,1,0:T(8,128)S(1)}, f32[4,8,1024]{2,1,0:T(8,128)S(...) custom-call(bf16[4,240,1024]{2,1,0:T(8,128)(2,1)} %get-tuple-element.64.given_ref, ...), custom_call_target="tpu_custom_call" | custom-call | flops 17179869184 | bytes 3932160 | tf_op jit(solution)/shard_map/attend/pallas_call | solution.py:1349
  187.7 1.0 copy-done.30
  188.8 35.0 %middle_and_norm2.1 = (bf16[4,256,1280]{2,1,0:T(8,128)(2,1)S(1)}, f32[256,1280]{1,0:T(8,128)S(1)}, bf16[2,4,320,1280]{3,2,1,0:T(8,128)(2,1)}) custom-call(bf16[320,1024]{1,0:T(8,128)(2,1)S(1)} %bitcast.75, bf16[320,1280]{1,0:T(8,128)(2,1)S(1)} %bitcast.67, f32[3,1280]{1,0:T(4,128)S(1)} %slice.30.refs_0_, ...), custom_call_target="tpu_custom_call", output_to_operand_aliasing={{2}: (4, {})} | custom-call | flops 3355443200 | bytes 5242880 | tf_op jit(solution)/shard_map/middle_and_norm2/pallas_call | solution.py:988
  223.8 11.1 %feed_forward.1 = (bf16[1024,1280]{1,0:T(8,128)(2,1)S(1)}, bf16[1024,1280]{1,0:T(8,128)(2,1)S(1)}, f32[1,1280]{1,0:T(1,128)S(1)}) custom-call(bf16[1024,1280]{1,0:T(8,128)(2,1)S(1)} %bitcast.73, bf16[2,1280,1280]{2,1,0:T(8,128)(2,1)} %bitcast.78, f32[1,1280]{1,0:T(1,128)S(1)} %broadcast_in_dim_reshape_squeeze.3.bias_ref, bf16[1024,1280]{1,0:T(8,128)(2,1)S(1)} %copy-done.11, ...), custom_call_target="tpu_custom_call" | custom-call | flops 6710886400 | bytes 17039360 | tf_op jit(solution)/shard_map/feed_forward/pallas_call | solution.py:1320
  235.0 5.0 convolution_convert_fusion.1
  240.6 1.1 constant_dynamic-slice_fusion.refs_2_
  241.8 7.0 %convolution_convert_fusion = bf16[1280,1280]{1,0:T(8,128)(2,1)} fusion(bf16[1024,1280]{1,0:T(8,128)(2,1)S(1)} %get-tuple-element.78.left_ref, bf16[1024,1280]{1,0:T(8,128)(2,1)} %bitcast.74), kind=kOutput, calls=%fused_computation | convolution fusion | flops 3357081600 | bytes 8519680 | tf_op jit(solution)/shard_map/dot_general | solution.py:1500
  248.8 44.2 %middle_grad.1 = (bf16[4,256,1280]{2,1,0:T(8,128)(2,1)}, f32[256,1280]{1,0:T(8,128)S(1)}, f32[3,1280]{1,0:T(4,128)S(1)}, bf16[4,160,1280]{2,1,0:T(8,128)(2,1)}) custom-call(bf16[1024,1280]{1,0:T(8,128)(2,1)} %copy-done, bf16[2,1280,1280]{2,1,0:T(8,128)(2,1)} %bitcast.80, f32[3,1280]{1,0:T(4,128)S(1)} %slice.30.refs_0_, f32[256,1280]{1,0:T(8,128)S(1)} %copy-done.2, ...), custom_call_target="tpu_custom_call" | custom-call | flops 3355443200 | bytes 5242880 | tf_op jit(solution)/shard_map/middle_grad/pallas_call | solution.py:988
  292.9 1.0 copy-done.3
  294.5 0.6 maximum_bitcast_fusion.early_ref
  295.1 3.8 convolution_convert_fusion.2
  298.9 1.9 convolution_convert_fusion.3
  301.4 5.4 %reduce-scatter.3.cloned.1.call-done = bf16[1,320,1280]{2,1,0:T(8,128)(2,1)} async-done(((bf16[4,320,1280]{2,1,0:T(8,128)(2,1)}), bf16[1,320,1280]{2,1,0:T(8,128)(2,1)}) %reduce-scatter.3.cloned.1.call-update) | async-done | bytes 819216 | tf_op jit(solution)/shard_map/reduce_scatter | solution.py:1503
  306.9 94.3 %attend_back.1 = (bf16[4,240,1024]{2,1,0:T(8,128)(2,1)}, f32[80,256]{1,0:T(8,128)}, f32[2,128]{1,0:T(2,128)}, f32[320,1280]{1,0:T(8,128)}, bf16[320,1024]{1,0:T(8,128)(2,1)}) custom-call(bf16[4,240,1024]{2,1,0:T(8,128)(2,1)} %get-tuple-element.66.qkv_ref, bf16[80,127]{1,0:T(8,128)(2,1)} %bitcast.69, bf16[80,127]{1,0:T(8,128)(2,1)} %bitcast.71, ...), custom_call_target="tpu_custom_call" | custom-call | flops 42949672960 | bytes 7864320 | tf_op jit(solution)/shard_map/attend_back/pallas_call | solution.py:1393
  401.2 81.9 %tail.1 = (f32[320,1024]{1,0:T(8,128)}, f32[3,320,320]{2,1,0:T(8,128)}, f32[320,1280]{1,0:T(8,128)}, f32[4,80,320]{2,1,0:T(8,128)}, f32[2,80,127]{2,1,0:T(8,128)...) custom-call(bf16[960,1024]{1,0:T(8,128)(2,1)} %bitcast.77, ...), custom_call_target="tpu_custom_call" | custom-call | tf_op jit(solution)/shard_map/tail/pallas_call | solution.py:1255
  483.1 0.8 slice.34
  484.0 0.7 slice.36
  484.7 0.7 reshape.121
  485.5 0.7 reshape.124
  486.2 1.4 slice_bitcast_fusion
  487.6 0.8 copy.54
  488.5 2.6 copy.55
  491.1 1.1 copy.56
  492.2 0.8 copy.57
  495.9 1.2 copy.63
  497.1 1.2 copy.64
  (110 shorter events, 5.6 us)
Async XLA Ops:
  7.2 3.8 copy-start.19
  7.2 3.8 copy-start.5
  7.2 3.8 copy-start.12
  7.2 3.8 copy-start.4
  7.2 3.8 copy-start.17
  7.2 3.8 copy-start.16
  7.2 3.8 copy-start.15
  7.3 3.8 copy-start.14
  7.3 3.8 copy-start.18
  7.3 3.8 copy-start.10
  7.3 299.5 %reduce-scatter.3.cloned.1.call-start = ((), (), s32[]{:S(2)}) async-start(), calls=%async_computation.2 | async-start | bytes 4096000 | tf_op jit(solution)/shard_map/reduce_scatter | solution.py:1503
  9.8 69.7 %copy-start.6 = (bf16[1,1024,320]{1,2,0:T(8,128)(2,1)S(1)}, bf16[1,1024,320]{1,2,0:T(8,128)(2,1)}, u32[]{:S(2)}) copy-start(bf16[1,1024,320]{1,2,0:T(8,128)(2,1)} %param.31) | copy-start | bytes 1966084
  9.8 69.7 %copy-start.24 = (bf16[127,80]{0,1:T(8,128)(2,1)S(1)}, bf16[127,80]{0,1:T(8,128)(2,1)}, u32[]{:S(2)}) copy-start(bf16[127,80]{0,1:T(8,128)(2,1)} %param.29) | copy-start | bytes 60964
  9.8 69.7 %copy-start.25 = (bf16[127,80]{0,1:T(8,128)(2,1)S(1)}, bf16[127,80]{0,1:T(8,128)(2,1)}, u32[]{:S(2)}) copy-start(bf16[127,80]{0,1:T(8,128)(2,1)} %param.30) | copy-start | bytes 60964
  80.9 107.9 %copy-start.9 = (bf16[256,1280]{1,0:T(8,128)(2,1)S(1)}, bf16[256,1280]{1,0:T(8,128)(2,1)}, u32[]{:S(2)}) copy-start(bf16[256,1280]{1,0:T(8,128)(2,1)} %copy-done.8) | copy-start | bytes 1966084
  80.9 107.9 %copy-start.22 = (bf16[4,80,1280]{2,1,0:T(8,128)(2,1)S(1)}, bf16[4,80,1280]{2,1,0:T(8,128)(2,1)}, u32[]{:S(2)}) copy-start(bf16[4,80,1280]{2,1,0:T(8,128)(2,1)} %copy-done.21) | copy-start | bytes 2457604
  188.8 35.0 %copy-start.27 = (bf16[4,80,1024]{2,1,0:T(8,128)(2,1)}, bf16[4,80,1024]{2,1,0:T(8,128)(2,1)S(1)}, u32[]{:S(2)}) copy-start(bf16[4,80,1024]{2,1,0:T(8,128)(2,1)S(1)} %get-tuple-element.68) | copy-start | bytes 1966084
  188.8 35.0 %copy-start.31 = (f32[4,8,1024]{2,1,0:T(8,128)}, f32[4,8,1024]{2,1,0:T(8,128)S(1)}, u32[]{:S(2)}) copy-start(f32[4,8,1024]{2,1,0:T(8,128)S(1)} %get-tuple-element.87.stat_ref) | copy-start | bytes 393220
  188.8 35.0 %copy-start.11 = (bf16[1024,1280]{1,0:T(8,128)(2,1)S(1)}, bf16[1024,1280]{1,0:T(8,128)(2,1)}, u32[]{:S(2)}) copy-start(bf16[1024,1280]{1,0:T(8,128)(2,1)} %get-tuple-element.75.cot_ref) | copy-start | bytes 7864324
  223.8 11.1 %copy-start.1 = (f32[256,1280]{1,0:T(8,128)}, f32[256,1280]{1,0:T(8,128)S(1)}, u32[]{:S(2)}) copy-start(f32[256,1280]{1,0:T(8,128)S(1)} %get-tuple-element.79.refs_1_.middle_ref) | copy-start | bytes 3932164
  223.8 11.1 %copy-start.26 = (bf16[4,256,1280]{2,1,0:T(8,128)(2,1)}, bf16[4,256,1280]{2,1,0:T(8,128)(2,1)S(1)}, u32[]{:S(2)}) copy-start(bf16[4,256,1280]{2,1,0:T(8,128)(2,1)S(1)} %get-tuple-element.72) | copy-start | bytes 7864324
  234.9 5.1 %copy-start.29 = (bf16[1024,1280]{1,0:T(8,128)(2,1)}, bf16[1024,1280]{1,0:T(8,128)(2,1)S(1)}, u32[]{:S(2)}) copy-start(bf16[1024,1280]{1,0:T(8,128)(2,1)S(1)} %get-tuple-element.76.activated_ref) | copy-start | bytes 7864324
  234.9 6.8 %copy-start = (bf16[1024,1280]{1,0:T(8,128)(2,1)}, bf16[1024,1280]{1,0:T(8,128)(2,1)S(1)}, u32[]{:S(2)}) copy-start(bf16[1024,1280]{1,0:T(8,128)(2,1)S(1)} %get-tuple-element.78.left_ref) | copy-start | bytes 7864324
  240.0 161.2 %reduce-scatter.5.cloned.1.call-start = ((), (), s32[]{:S(2)}) async-start(), calls=%async_computation.3 | async-start | bytes 2048000 | tf_op jit(solution)/shard_map/reduce_scatter | solution.py:1503
  241.8 7.0 %copy-start.2 = (f32[256,1280]{1,0:T(8,128)S(1)}, f32[256,1280]{1,0:T(8,128)}, u32[]{:S(2)}) copy-start(f32[256,1280]{1,0:T(8,128)} %copy-done.1) | copy-start | bytes 3932164
  248.8 46.3 %copy-start.28 = (bf16[4,80,1024]{2,1,0:T(8,128)(2,1)S(1)}, bf16[4,80,1024]{2,1,0:T(8,128)(2,1)}, u32[]{:S(2)}) copy-start(bf16[4,80,1024]{2,1,0:T(8,128)(2,1)} %copy-done.27) | copy-start | bytes 1966084
  401.2 86.4 %copy-start.35 = (bf16[320,1024]{1,0:T(8,128)(2,1)S(1)}, bf16[320,1024]{1,0:T(8,128)(2,1)}, u32[]{:S(2)}) copy-start(bf16[320,1024]{1,0:T(8,128)(2,1)} %get-tuple-element.89) | copy-start | bytes 1966084
  483.1 7.9 %copy-start.34 = (f32[3,320,320]{2,1,0:T(8,128)S(1)}, f32[3,320,320]{2,1,0:T(8,128)}, u32[]{:S(2)}) copy-start(f32[3,320,320]{2,1,0:T(8,128)} %get-tuple-element.100) | copy-start | bytes 3686404
  488.5 4.5 copy-start.42
  491.1 4.2 copy-start.38
  491.1 4.8 copy-start.33
  492.2 4.9 copy-start.32
  (14 other events, 35.9 us)
Sparse Core Ops, SparseCore 0:
  240.2 66.6 reduce-scatter.2
  309.1 56.5 reduce-scatter.4

commit v7 on v6

--- a/solution.py
+++ b/solution.py
@@ -397,7 +397,7 @@
 
 def attend_kernel(
     images, given_ref, height_ref, width_ref, cot_ref, weight_ref,
-    merged_ref, qkv_ref, exact_ref, stat_ref, cot_out, weight_all,
+    merged_ref, qkv_ref, exact_ref, stat_ref, cot_out, cot_own, weight_all,
     kaug, columns, acc, top, total, box, sems, cot_parts, cot_sems, local_sems, chain_sems, swap_sems,
     tab_t, tab_ref,
 ):
@@ -532,6 +532,8 @@
     for start in range(0, width, QUERIES):
         rows = slice(start, start + QUERIES)
         cot_out[rows] = upright([cot_parts[i, :, rows] for i in range(4)]).astype(BF16)
+    own = cot_own.shape[0]
+    cot_own[...] = cot_out[pl.ds(pl.multiple_of(row * own, own), own)]
     merged_ref[me] = box[me]
     for chain in chains:
         chain.end((1, 2))
@@ -1221,7 +1223,7 @@
     spare = jnp.zeros((LAST_ROWS - len(last), 128), F32)
     small[at : at + LAST_ROWS] = jnp.concatenate([*last, spare], 0)
 
-    go(sums, fc1, proj, qkv_sum, qkv, sums, patches, fc1, proj, sums, qkv, fc1, sums, qkv)
+    go(sums, fc1, proj, sums, fc1, proj, qkv_sum, qkv, sums, patches, qkv, fc1, proj, sums)
     firsts = [lines * i for i in (5, 6, 7, 4)] + [EARLY_ROWS + TABLE_ROWS + BIAS_ROWS + lines * i for i in range(2)]
     part = vector_outs[0].shape[0]
     for first, out in zip(firsts, vector_outs):
@@ -1235,6 +1237,7 @@
     for half in range(2):
         table = small[EARLY_ROWS + half * HEAD_DIM : EARLY_ROWS + (half + 1) * HEAD_DIM]
         tables_out[half] = sum(mm(term, flip) for term in split(table, 3))
+    go(qkv)
     for kind in range(3):
         rows = slice(kind * HEAD_DIM, (kind + 1) * HEAD_DIM)
         qkv_out[kind] = jnp.concatenate([values[rows] for values in head_grads], 0).T
@@ -1349,13 +1352,14 @@
     return pl.pallas_call(
         partial(attend_kernel, images),
         in_specs=[*[vmem] * 4, pl.BlockSpec(memory_space=pl.ANY)],
-        out_specs=[*[vmem] * 5, pl.BlockSpec(memory_space=pl.ANY)],
+        out_specs=[*[vmem] * 6, pl.BlockSpec(memory_space=pl.ANY)],
         out_shape=[
             jax.ShapeDtypeStruct((count, HEAD_DIM, width), BF16),
             jax.ShapeDtypeStruct(qkv.shape, BF16),
             jax.ShapeDtypeStruct((count, HEAD_DIM, width), F32),
             jax.ShapeDtypeStruct((count, 8, width), F32),
             jax.ShapeDtypeStruct((width, 4 * cotangent.shape[0]), BF16),
+            jax.ShapeDtypeStruct((width // 4, 4 * cotangent.shape[0]), BF16),
             jax.ShapeDtypeStruct((2, count, *weights.shape[1:]), BF16),
         ],
         scratch_shapes=[
@@ -1490,7 +1494,7 @@
 
     height, span = height_table.T, width_table.T
 
-    merged, qkv, exact, stat, cotangent, weights = attention(
+    merged, qkv, exact, stat, cotangent, cotangent_own, weights = attention(
         qkv, height, span, out_grad[0].T, local_rest.reshape(2, hidden, model)
     )
     weight_proj = weight_proj.reshape(cols * head, model)
@@ -1521,7 +1525,7 @@
     own_and_sums = [jax.ShapeDtypeStruct(own_shape, F32), jax.ShapeDtypeStruct((3, model), F32)]
     branch_grad, middle_grad, sums2, fc1_grad = row_mix(
         backward_finish, "middle_grad", 2, preact_grad, weights,
-        (vec2, middle, tokens_of_row(cotangent)), own_and_sums, False, fc1_grad,
+        (vec2, middle, cotangent_own), own_and_sums, False, fc1_grad,
     )
     branch_grad = branch_grad.reshape(width, model)
 

time: 515 us -> 514 us (level)
    unnamed x101 -> x103, local copies, waits for them, and re-layouts: 18.9 us -> 18.9 us
where the time goes in v7:
time: 514 us; the launch traced here: 506 us
  Pallas kernels  440 us (86%)
  local copies, waits for them, and re-layouts  26.2 us (5%)
  matrix products  17.7 us (3%)
  between operations  15 us (3%)
  waiting for transfers between devices  6.78 us (1%)
    pallas_call x1, Pallas kernels, attention(): pl.pallas_call(partial(attend_kernel, images), in_specs=[*[vmem] * 4, pl....  107 us
    pallas_call x1, Pallas kernels, attention_back(): pl.pallas_call(partial(attend_back_kernel, images), in_specs=[*[vmem] * 8...  94.3 us
    pallas_call x1, Pallas kernels, tail(): pl.pallas_call(partial(tail_kernel, axes), in_specs=[vmem] * 12, out_spec...  82.1 us
    pallas_call x2, Pallas kernels, row_mix(): pl.pallas_call(partial(row_mix_kernel, finish, len(extra), 1 + len(outs),...  79 us
    pallas_call x1, Pallas kernels, start(): pl.pallas_call(partial(start_kernel, lax.axis_size('batch')), in_specs=[v...  66.3 us
    unnamed x103, local copies, waits for them, and re-layouts  18.9 us
    dot_general x2, matrix products, contract_rows(): lax.dot_general(left, right, (((0,), (0,)), ((), ())), preferred_element_...  12 us
    pallas_call x1, Pallas kernels, feed_forward(): pl.pallas_call(hidden_kernel, grid=(hidden // step,), in_specs=[whole, fi...  11.1 us
  transfers between devices with their start and end apart: 2, of which 1 were waited for; matrix products, arithmetic and copies ran while one was open for 3% of the time, Pallas kernels for 27%

profile of v7, /device:TPU:8, one launch (start us, length us, event | category | flops | bytes accessed | tf_op | source)
XLA Modules:
  0.0 506.2 jit_solution(3749554692023481484)
XLA Ops:
  7.4 2.4 copy.36
  9.8 1.3 copy.37
  11.2 66.3 %start.1 = (bf16[4,240,1024]{2,1,0:T(8,128)(2,1)}, bf16[1024,1280]{1,0:T(8,128)(2,1)}, bf16[256,1280]{1,0:T(8,128)(2,1)S(1)}, bf16[4,240,1280]{2,1,0:T(8,128)(2,...) custom-call(bf16[320,1024]{1,0:T(8,128)(2,1)S(1)} %bitcast.64, ...), custom_call_target="tpu_custom_call" | custom-call | tf_op jit(solution)/shard_map/start/pallas_call | solution.py:361
  77.4 0.8 copy-done.9
  78.3 0.9 copy-done.21
  79.3 1.4 copy-done.20
  80.8 106.8 %attend.1 = (bf16[4,80,1024]{2,1,0:T(8,128)(2,1)S(1)}, bf16[4,240,1024]{2,1,0:T(8,128)(2,1)}, f32[4,80,1024]{2,1,0:T(8,128)S(1)}, f32[4,8,1024]{2,1,0:T(8,128)S(...) custom-call(bf16[4,240,1024]{2,1,0:T(8,128)(2,1)} %get-tuple-element.65.given_ref, ...), custom_call_target="tpu_custom_call" | custom-call | flops 17179869184 | bytes 3932160 | tf_op jit(solution)/shard_map/attend/pallas_call | solution.py:1352
  187.6 1.0 copy-done.31
  188.7 35.0 %middle_and_norm2.1 = (bf16[4,256,1280]{2,1,0:T(8,128)(2,1)S(1)}, f32[256,1280]{1,0:T(8,128)S(1)}, bf16[2,4,320,1280]{3,2,1,0:T(8,128)(2,1)}) custom-call(bf16[320,1024]{1,0:T(8,128)(2,1)S(1)} %bitcast.75, bf16[320,1280]{1,0:T(8,128)(2,1)S(1)} %bitcast.67, f32[3,1280]{1,0:T(4,128)S(1)} %slice.30.refs_0_, ...), custom_call_target="tpu_custom_call", output_to_operand_aliasing={{2}: (4, {})} | custom-call | flops 3355443200 | bytes 5242880 | tf_op jit(solution)/shard_map/middle_and_norm2/pallas_call | solution.py:990
  223.7 11.1 %feed_forward.1 = (bf16[1024,1280]{1,0:T(8,128)(2,1)S(1)}, bf16[1024,1280]{1,0:T(8,128)(2,1)S(1)}, f32[1,1280]{1,0:T(1,128)S(1)}) custom-call(bf16[1024,1280]{1,0:T(8,128)(2,1)S(1)} %bitcast.73, bf16[2,1280,1280]{2,1,0:T(8,128)(2,1)} %bitcast.78, f32[1,1280]{1,0:T(1,128)S(1)} %broadcast_in_dim_reshape_squeeze.3.bias_ref, bf16[1024,1280]{1,0:T(8,128)(2,1)S(1)} %copy-done.30, ...), custom_call_target="tpu_custom_call" | custom-call | flops 6710886400 | bytes 17039360 | tf_op jit(solution)/shard_map/feed_forward/pallas_call | solution.py:1323
  234.8 5.1 convolution_convert_fusion.1
  240.5 7.0 %convolution_convert_fusion = bf16[1280,1280]{1,0:T(8,128)(2,1)} fusion(bf16[1024,1280]{1,0:T(8,128)(2,1)S(1)} %get-tuple-element.79.left_ref, bf16[1024,1280]{1,0:T(8,128)(2,1)} %bitcast.74), kind=kOutput, calls=%fused_computation | convolution fusion | flops 3357081600 | bytes 8519680 | tf_op jit(solution)/shard_map/dot_general | solution.py:1504
  247.5 44.0 %middle_grad.1 = (bf16[4,256,1280]{2,1,0:T(8,128)(2,1)}, f32[256,1280]{1,0:T(8,128)S(1)}, f32[3,1280]{1,0:T(4,128)S(1)}, bf16[4,160,1280]{2,1,0:T(8,128)(2,1)}) custom-call(bf16[1024,1280]{1,0:T(8,128)(2,1)} %copy-done, bf16[2,1280,1280]{2,1,0:T(8,128)(2,1)} %bitcast.80, f32[3,1280]{1,0:T(4,128)S(1)} %slice.30.refs_0_, f32[256,1280]{1,0:T(8,128)S(1)} %copy-done.2, ...), custom_call_target="tpu_custom_call" | custom-call | flops 3355443200 | bytes 5242880 | tf_op jit(solution)/shard_map/middle_grad/pallas_call | solution.py:990
  291.5 1.0 copy-done.3
  293.1 0.6 maximum_bitcast_fusion.early_ref
  293.7 3.8 convolution_convert_fusion.2
  297.5 1.9 convolution_convert_fusion.3
  299.4 0.6 fusion
  300.0 6.7 %reduce-scatter.3.cloned.1.call-done = bf16[1,320,1280]{2,1,0:T(8,128)(2,1)} async-done(((bf16[4,320,1280]{2,1,0:T(8,128)(2,1)}), bf16[1,320,1280]{2,1,0:T(8,128)(2,1)}) %reduce-scatter.3.cloned.1.call-update) | async-done | bytes 819216 | tf_op jit(solution)/shard_map/reduce_scatter | solution.py:1507
  306.7 94.3 %attend_back.1 = (bf16[4,240,1024]{2,1,0:T(8,128)(2,1)}, f32[80,256]{1,0:T(8,128)}, f32[2,128]{1,0:T(2,128)}, f32[320,1280]{1,0:T(8,128)}, bf16[320,1024]{1,0:T(8,128)(2,1)}) custom-call(bf16[4,240,1024]{2,1,0:T(8,128)(2,1)} %get-tuple-element.67.qkv_ref, bf16[80,127]{1,0:T(8,128)(2,1)} %bitcast.69, bf16[80,127]{1,0:T(8,128)(2,1)} %bitcast.71, ...), custom_call_target="tpu_custom_call" | custom-call | flops 42949672960 | bytes 7864320 | tf_op jit(solution)/shard_map/attend_back/pallas_call | solution.py:1397
  401.1 82.1 %tail.1 = (f32[320,1024]{1,0:T(8,128)}, f32[3,320,320]{2,1,0:T(8,128)}, f32[320,1280]{1,0:T(8,128)}, f32[4,80,320]{2,1,0:T(8,128)}, f32[2,80,127]{2,1,0:T(8,128)...) custom-call(bf16[960,1024]{1,0:T(8,128)(2,1)} %bitcast.77, ...), custom_call_target="tpu_custom_call" | custom-call | tf_op jit(solution)/shard_map/tail/pallas_call | solution.py:1258
  483.2 0.8 slice.34
  484.1 0.7 slice.36
  484.8 0.7 reshape.121
  485.6 0.7 reshape.124
  486.3 1.4 slice_bitcast_fusion
  487.7 0.8 copy.54
  488.5 2.6 copy.55
  491.2 1.1 copy.56
  492.3 0.8 copy.57
  496.0 1.2 copy.63
  497.1 1.2 copy.64
  (111 shorter events, 5.0 us)
Async XLA Ops:
  7.2 3.8 copy-start.19
  7.2 3.8 copy-start.5
  7.2 3.8 copy-start.12
  7.2 3.8 copy-start.4
  7.2 3.8 copy-start.17
  7.2 3.8 copy-start.16
  7.2 3.8 copy-start.15
  7.3 3.8 copy-start.14
  7.3 3.8 copy-start.18
  7.3 299.4 %reduce-scatter.3.cloned.1.call-start = ((), (), s32[]{:S(2)}) async-start(), calls=%async_computation.2 | async-start | bytes 4096000 | tf_op jit(solution)/shard_map/reduce_scatter | solution.py:1507
  9.8 69.5 %copy-start.6 = (bf16[1,1024,320]{1,2,0:T(8,128)(2,1)S(1)}, bf16[1,1024,320]{1,2,0:T(8,128)(2,1)}, u32[]{:S(2)}) copy-start(bf16[1,1024,320]{1,2,0:T(8,128)(2,1)} %param.31) | copy-start | bytes 1966084
  9.8 69.5 %copy-start.24 = (bf16[127,80]{0,1:T(8,128)(2,1)S(1)}, bf16[127,80]{0,1:T(8,128)(2,1)}, u32[]{:S(2)}) copy-start(bf16[127,80]{0,1:T(8,128)(2,1)} %param.29) | copy-start | bytes 60964
  9.8 69.5 %copy-start.25 = (bf16[127,80]{0,1:T(8,128)(2,1)S(1)}, bf16[127,80]{0,1:T(8,128)(2,1)}, u32[]{:S(2)}) copy-start(bf16[127,80]{0,1:T(8,128)(2,1)} %param.30) | copy-start | bytes 60964
  80.7 107.9 %copy-start.10 = (bf16[256,1280]{1,0:T(8,128)(2,1)S(1)}, bf16[256,1280]{1,0:T(8,128)(2,1)}, u32[]{:S(2)}) copy-start(bf16[256,1280]{1,0:T(8,128)(2,1)} %copy-done.9) | copy-start | bytes 1966084
  80.8 107.9 %copy-start.22 = (bf16[4,80,1280]{2,1,0:T(8,128)(2,1)S(1)}, bf16[4,80,1280]{2,1,0:T(8,128)(2,1)}, u32[]{:S(2)}) copy-start(bf16[4,80,1280]{2,1,0:T(8,128)(2,1)} %copy-done.21) | copy-start | bytes 2457604
  188.7 35.0 %copy-start.27 = (bf16[4,80,1024]{2,1,0:T(8,128)(2,1)}, bf16[4,80,1024]{2,1,0:T(8,128)(2,1)S(1)}, u32[]{:S(2)}) copy-start(bf16[4,80,1024]{2,1,0:T(8,128)(2,1)S(1)} %get-tuple-element.69) | copy-start | bytes 1966084
  188.7 35.0 %copy-start.32 = (f32[4,8,1024]{2,1,0:T(8,128)}, f32[4,8,1024]{2,1,0:T(8,128)S(1)}, u32[]{:S(2)}) copy-start(f32[4,8,1024]{2,1,0:T(8,128)S(1)} %get-tuple-element.89.stat_ref) | copy-start | bytes 393220
  188.7 35.0 %copy-start.30 = (bf16[1024,1280]{1,0:T(8,128)(2,1)S(1)}, bf16[1024,1280]{1,0:T(8,128)(2,1)}, u32[]{:S(2)}) copy-start(bf16[1024,1280]{1,0:T(8,128)(2,1)} %get-tuple-element.76.cot_ref) | copy-start | bytes 7864324
  223.7 11.1 %copy-start.1 = (f32[256,1280]{1,0:T(8,128)}, f32[256,1280]{1,0:T(8,128)S(1)}, u32[]{:S(2)}) copy-start(f32[256,1280]{1,0:T(8,128)S(1)} %get-tuple-element.80.refs_1_.middle_ref) | copy-start | bytes 3932164
  223.7 11.1 %copy-start.26 = (bf16[4,256,1280]{2,1,0:T(8,128)(2,1)}, bf16[4,256,1280]{2,1,0:T(8,128)(2,1)S(1)}, u32[]{:S(2)}) copy-start(bf16[4,256,1280]{2,1,0:T(8,128)(2,1)S(1)} %get-tuple-element.73) | copy-start | bytes 7864324
  234.8 5.1 %copy-start.29 = (bf16[1024,1280]{1,0:T(8,128)(2,1)}, bf16[1024,1280]{1,0:T(8,128)(2,1)S(1)}, u32[]{:S(2)}) copy-start(bf16[1024,1280]{1,0:T(8,128)(2,1)S(1)} %get-tuple-element.77.activated_ref) | copy-start | bytes 7864324
  234.8 5.7 %copy-start = (bf16[1024,1280]{1,0:T(8,128)(2,1)}, bf16[1024,1280]{1,0:T(8,128)(2,1)S(1)}, u32[]{:S(2)}) copy-start(bf16[1024,1280]{1,0:T(8,128)(2,1)S(1)} %get-tuple-element.79.left_ref) | copy-start | bytes 7864324
  239.9 161.1 %reduce-scatter.5.cloned.1.call-start = ((), (), s32[]{:S(2)}) async-start(), calls=%async_computation.3 | async-start | bytes 2048000 | tf_op jit(solution)/shard_map/reduce_scatter | solution.py:1507
  240.5 7.0 %copy-start.2 = (f32[256,1280]{1,0:T(8,128)S(1)}, f32[256,1280]{1,0:T(8,128)}, u32[]{:S(2)}) copy-start(f32[256,1280]{1,0:T(8,128)} %copy-done.1) | copy-start | bytes 3932164
  247.5 45.1 %copy-start.7 = (bf16[1,1024,320]{1,2,0:T(8,128)(2,1)S(1)}, bf16[1,1024,320]{1,2,0:T(8,128)(2,1)}, u32[]{:S(2)}) copy-start(bf16[1,1024,320]{1,2,0:T(8,128)(2,1)} %param.31) | copy-start | bytes 1966084
  247.5 46.2 %copy-start.28 = (bf16[4,80,1024]{2,1,0:T(8,128)(2,1)S(1)}, bf16[4,80,1024]{2,1,0:T(8,128)(2,1)}, u32[]{:S(2)}) copy-start(bf16[4,80,1024]{2,1,0:T(8,128)(2,1)} %copy-done.27) | copy-start | bytes 1966084
  401.1 86.6 %copy-start.36 = (bf16[320,1024]{1,0:T(8,128)(2,1)S(1)}, bf16[320,1024]{1,0:T(8,128)(2,1)}, u32[]{:S(2)}) copy-start(bf16[320,1024]{1,0:T(8,128)(2,1)} %get-tuple-element.91) | copy-start | bytes 1966084
  483.2 7.9 %copy-start.35 = (f32[3,320,320]{2,1,0:T(8,128)S(1)}, f32[3,320,320]{2,1,0:T(8,128)}, u32[]{:S(2)}) copy-start(f32[3,320,320]{2,1,0:T(8,128)} %get-tuple-element.102) | copy-start | bytes 3686404
  488.5 4.5 copy-start.43
  491.1 4.2 copy-start.39
  491.1 4.8 copy-start.34
  492.3 4.9 copy-start.33
  (15 other events, 39.8 us)
Sparse Core Ops, SparseCore 0:
  240.0 66.6 reduce-scatter.2
  309.0 56.6 reduce-scatter.4
